TPU v7x, 32 devices: a whole 2x2x4 slice. The times are simulated.
32 devices in a mesh: dp: 4 (over y, core), fsdp: 8 (over z, x).
Axes of the slice: x: 2, y: 2, z: 4, core: 2. Of those that a mesh axis runs over, the one named last changes fastest.
Arguments:
- tokens: bfloat16 [65536, 512], P(('dp', 'fsdp')), may hold values from -6 to 6
- lengths: int32 [256], replicated, may hold values from 0 to 2048, as said below
- assignment: int32 [256], replicated, may hold values from 0 to 31, as said below
- weights: bfloat16 [2097152], P(('dp', 'fsdp')), may hold values from -1.5 to 1.5
- vectors: bfloat16 [5120], P(('dp', 'fsdp')), may hold values from -1.6 to 1.8
- cotangent: bfloat16 [65536, 512], P(('dp', 'fsdp')), may hold values from -6 to 6
Outputs:
- layer_output: bfloat16 [65536, 512], P(('dp', 'fsdp'))
- grad_tokens: float32 [65536, 512], P(('dp', 'fsdp'))
- grad_weights: float32 [2097152], P(('dp', 'fsdp'))
- grad_vectors: float32 [5120], P(('dp', 'fsdp'))
Inputs may be any that keep to these rules, and one draw needn't show every extreme that they name: The datasets that assignment gives one device have lengths adding up to exactly 2048; some dataset has 2048 samples. `assignment`: every device holds exactly 8 datasets.
All inputs are finite; a program needn't handle non-finite values.
Results may differ from a plain program's by a relative error of at most 0.012.
The roundings to bfloat16 on the way count: a program that leaves them out, or rounds other values in their place, can miss the bound.
Values may be sent and summed in bfloat16 or wider, within the bound.
No kernel may reach another device: no remote copies, remote signals or barrier semaphores. Data moves between devices by JAX's collectives and lax.ppermute only.
A program may use at most 256 MiB of HBM per device.

v0:
```python
import math

import jax
import jax.numpy as jnp
from jax import lax
from jax.sharding import PartitionSpec as P

HEADS = 4
HEAD_DIM = 128
FF = 1024


norm_eps = 1e-05


def dataset_labels(lengths, assignment, owner, row_count):
    owned = assignment == owner
    dataset_ends = jnp.cumsum(jnp.where(owned, lengths, 0), dtype=jnp.int32)
    places = jnp.arange(row_count, dtype=jnp.int32)
    passed = owned[None, :] & (dataset_ends[None, :] <= places[:, None])
    return jnp.sum(passed.astype(jnp.int32), axis=1, dtype=jnp.int32)


def piece_widths(model_width, hidden_width, device_count):
    square = model_width * model_width
    rect = model_width * hidden_width
    return [
        3 * square // device_count,
        square // device_count,
        rect // device_count,
        rect // device_count,
    ]


def unpack_params(flat_weights, flat_vectors, model_width, hidden_width, device_count):
    widths = piece_widths(model_width, hidden_width, device_count)
    blocks = flat_weights.reshape(device_count, -1)
    starts = [0, widths[0], widths[0] + widths[1], widths[0] + widths[1] + widths[2]]
    pieces = [blocks[:, starts[k] : starts[k] + widths[k]].reshape(-1) for k in range(4)]
    qkv_weight = pieces[0].reshape(3, model_width, model_width)
    attn_weight = pieces[1].reshape(model_width, model_width)
    in_weight = pieces[2].reshape(model_width, hidden_width)
    out_weight = pieces[3].reshape(hidden_width, model_width)
    float_vectors = flat_vectors.astype(jnp.float32)
    bias_rows = float_vectors[: 8 * model_width].reshape(8, model_width)
    hidden_bias = float_vectors[8 * model_width :]
    return (qkv_weight, attn_weight, in_weight, out_weight, bias_rows, hidden_bias)


def layer_norm(summed):
    row_mean = jnp.mean(summed, axis=-1, keepdims=True)
    centered = summed - row_mean
    variance = jnp.mean(centered * centered, axis=-1, keepdims=True)
    inverse = lax.rsqrt(variance + norm_eps)
    return (centered * inverse, inverse)


def norm_back(grad_normed, normed, inverse):
    first_mean = jnp.mean(grad_normed, axis=-1, keepdims=True)
    second_mean = jnp.mean(grad_normed * normed, axis=-1, keepdims=True)
    return inverse * (grad_normed - first_mean - normed * second_mean)


def gelu_slope(pre_act):
    normal_cdf = 0.5 * (1.0 + lax.erf(pre_act * 0.7071067811865476))
    density = jnp.exp(-0.5 * pre_act * pre_act) * 0.3989422804014327
    return normal_cdf + pre_act * density


def attention_forward(queries, key_heads, values, labels, block_rows):
    outputs = []
    totals = []
    for offset in range(0, queries.shape[0], block_rows):
        query_block = queries[offset : offset + block_rows]
        scores = jnp.einsum(
            "qhd,khd->hqk", query_block, key_heads, preferred_element_type=jnp.float32
        )
        allowed = labels[offset : offset + block_rows][:, None] == labels[None, :]
        scores = jnp.where(allowed[None], scores, -1e30)
        row_max = jnp.max(scores, axis=-1, keepdims=True)
        exp_scores = jnp.exp(scores - row_max)
        row_total = jnp.sum(exp_scores, axis=-1, keepdims=True)
        attn_probs = (exp_scores / row_total).astype(jnp.bfloat16)
        outputs.append(
            jnp.einsum("hqk,khd->qhd", attn_probs, values, preferred_element_type=jnp.float32)
        )
        totals.append(row_max + jnp.log(row_total))
    return (jnp.concatenate(outputs, axis=0), jnp.concatenate(totals, axis=1))


def attention_backward(queries, key_heads, values, labels, log_totals, grad_attended, block_rows):
    grad_query_parts = []
    grad_keys = jnp.zeros(key_heads.shape, jnp.float32)
    grad_values = jnp.zeros(values.shape, jnp.float32)
    for offset in range(0, queries.shape[0], block_rows):
        query_block = queries[offset : offset + block_rows]
        grad_block = grad_attended[offset : offset + block_rows]
        scores = jnp.einsum(
            "qhd,khd->hqk", query_block, key_heads, preferred_element_type=jnp.float32
        )
        allowed = labels[offset : offset + block_rows][:, None] == labels[None, :]
        scores = jnp.where(allowed[None], scores, -1e30)
        attn_probs = jnp.exp(scores - log_totals[:, offset : offset + block_rows])
        grad_probs = jnp.einsum(
            "qhd,khd->hqk", grad_block, values, preferred_element_type=jnp.float32
        )
        centre = jnp.sum(attn_probs * grad_probs, axis=-1, keepdims=True)
        grad_scores = (attn_probs * (grad_probs - centre)).astype(jnp.bfloat16)
        grad_query_parts.append(
            jnp.einsum("hqk,khd->qhd", grad_scores, key_heads, preferred_element_type=jnp.float32)
        )
        grad_keys = grad_keys + jnp.einsum(
            "hqk,qhd->khd", grad_scores, query_block, preferred_element_type=jnp.float32
        )
        grad_values = grad_values + jnp.einsum(
            "hqk,qhd->khd",
            attn_probs.astype(jnp.bfloat16),
            grad_block,
            preferred_element_type=jnp.float32,
        )
    return (jnp.concatenate(grad_query_parts, axis=0), grad_keys, grad_values)


def body(tokens, lengths, assignment, weights, vectors, cotangent):
    row_count, model_width = tokens.shape
    hidden_width = FF
    device_count = lax.axis_size(("dp", "fsdp"))
    score_scale = 1.0 / math.sqrt(HEAD_DIM)
    block_rows = min(512, row_count)
    owner_index = lax.axis_index(("dp", "fsdp"))
    labels = dataset_labels(lengths, assignment, owner_index, row_count)
    full_weights, full_vectors = (
        lax.all_gather(weights, ("dp", "fsdp"), axis=0, tiled=True),
        lax.all_gather(vectors, ("dp", "fsdp"), axis=0, tiled=True),
    )
    qkv_weight, attn_weight, in_weight, out_weight, bias_rows, hidden_bias = unpack_params(
        full_weights, full_vectors, model_width, hidden_width, device_count
    )
    inputs = tokens.astype(jnp.float32)
    projected = jnp.einsum("td,cde->cte", tokens, qkv_weight, preferred_element_type=jnp.float32)
    head_shape = (row_count, HEADS, HEAD_DIM)
    queries = ((projected[0] + bias_rows[0]) * score_scale).astype(jnp.bfloat16).reshape(head_shape)
    key_heads = projected[1].astype(jnp.bfloat16).reshape(head_shape)
    values = (projected[2] + bias_rows[1]).astype(jnp.bfloat16).reshape(head_shape)
    attended, log_totals = attention_forward(queries, key_heads, values, labels, block_rows)
    attended_low = attended.reshape(row_count, model_width).astype(jnp.bfloat16)
    branch = jnp.dot(attended_low, attn_weight, preferred_element_type=jnp.float32) + bias_rows[2]
    normed_one, inverse_one = layer_norm(inputs + branch)
    hidden = normed_one * bias_rows[4] + bias_rows[5]
    hidden_low = hidden.astype(jnp.bfloat16)
    pre_act = jnp.dot(hidden_low, in_weight, preferred_element_type=jnp.float32) + hidden_bias
    activated_low = jax.nn.gelu(pre_act, approximate=False).astype(jnp.bfloat16)
    ffn_result = (
        jnp.dot(activated_low, out_weight, preferred_element_type=jnp.float32) + bias_rows[3]
    )
    normed_two, inverse_two = layer_norm(hidden + ffn_result)
    result = normed_two * bias_rows[6] + bias_rows[7]
    again_weights, again_vectors = (
        lax.all_gather(weights, ("dp", "fsdp"), axis=0, tiled=True),
        lax.all_gather(vectors, ("dp", "fsdp"), axis=0, tiled=True),
    )
    qkv_weight, attn_weight, in_weight, out_weight, bias_rows, hidden_bias = unpack_params(
        again_weights, again_vectors, model_width, hidden_width, device_count
    )
    grad_result = cotangent.astype(jnp.float32)
    grad_gain_two = jnp.sum(grad_result * normed_two, axis=0)
    grad_shift_two = jnp.sum(grad_result, axis=0)
    grad_second = norm_back(grad_result * bias_rows[6], normed_two, inverse_two)
    grad_ffn = grad_second.astype(jnp.bfloat16)
    grad_ffn_bias = jnp.sum(grad_ffn.astype(jnp.float32), axis=0)
    grad_out_weight = jnp.einsum(
        "tf,td->fd", activated_low, grad_ffn, preferred_element_type=jnp.float32
    )
    grad_activated = jnp.einsum(
        "td,fd->tf", grad_ffn, out_weight, preferred_element_type=jnp.float32
    )
    grad_pre = (grad_activated * gelu_slope(pre_act)).astype(jnp.bfloat16)
    grad_hidden_bias = jnp.sum(grad_pre.astype(jnp.float32), axis=0)
    grad_in_weight = jnp.einsum(
        "td,tf->df", hidden_low, grad_pre, preferred_element_type=jnp.float32
    )
    grad_hidden = grad_second + jnp.einsum(
        "tf,df->td", grad_pre, in_weight, preferred_element_type=jnp.float32
    )
    grad_gain_one = jnp.sum(grad_hidden * normed_one, axis=0)
    grad_shift_one = jnp.sum(grad_hidden, axis=0)
    grad_first = norm_back(grad_hidden * bias_rows[4], normed_one, inverse_one)
    grad_branch = grad_first.astype(jnp.bfloat16)
    grad_attn_bias = jnp.sum(grad_branch.astype(jnp.float32), axis=0)
    grad_attn_weight = jnp.einsum(
        "td,te->de", attended_low, grad_branch, preferred_element_type=jnp.float32
    )
    grad_attended = jnp.einsum(
        "te,de->td", grad_branch, attn_weight, preferred_element_type=jnp.float32
    )
    grad_attended = grad_attended.astype(jnp.bfloat16).reshape(head_shape)
    grad_queries, grad_keys, grad_values = attention_backward(
        queries, key_heads, values, labels, log_totals, grad_attended, block_rows
    )
    grad_proj = (
        jnp.stack([grad_queries, grad_keys, grad_values])
        .reshape(3, row_count, model_width)
        .astype(jnp.bfloat16)
    )
    proj_factors = jnp.array([score_scale, 1.0, 1.0], jnp.float32)
    grad_qkv_weight = (
        jnp.einsum("td,cte->cde", tokens, grad_proj, preferred_element_type=jnp.float32)
        * proj_factors[:, None, None]
    )
    grad_query_bias = jnp.sum(grad_proj[0].astype(jnp.float32), axis=0) * score_scale
    grad_value_bias = jnp.sum(grad_proj[2].astype(jnp.float32), axis=0)
    grad_inputs = grad_first + score_scale * jnp.einsum(
        "te,de->td", grad_proj[0], qkv_weight[0], preferred_element_type=jnp.float32
    )
    grad_inputs = grad_inputs + jnp.einsum(
        "te,de->td", grad_proj[1], qkv_weight[1], preferred_element_type=jnp.float32
    )
    grad_inputs = grad_inputs + jnp.einsum(
        "te,de->td", grad_proj[2], qkv_weight[2], preferred_element_type=jnp.float32
    )
    grad_flat_vectors = jnp.concatenate(
        [
            grad_query_bias,
            grad_value_bias,
            grad_attn_bias,
            grad_ffn_bias,
            grad_gain_one,
            grad_shift_one,
            grad_gain_two,
            grad_shift_two,
            grad_hidden_bias,
        ]
    )
    grad_blocks = jnp.concatenate(
        [
            grad_qkv_weight.reshape(device_count, -1),
            grad_attn_weight.reshape(device_count, -1),
            grad_in_weight.reshape(device_count, -1),
            grad_out_weight.reshape(device_count, -1),
        ],
        axis=1,
    )
    own_weights, own_vectors = (
        lax.psum_scatter(grad_blocks.reshape(-1), ("dp", "fsdp"), scatter_dimension=0, tiled=True),
        lax.psum_scatter(grad_flat_vectors, ("dp", "fsdp"), scatter_dimension=0, tiled=True),
    )
    return (result.astype(jnp.bfloat16), grad_inputs, own_weights, own_vectors)


def solution(mesh):
    in_specs = (
        P(("dp", "fsdp"), None),
        P(),
        P(),
        P(("dp", "fsdp")),
        P(("dp", "fsdp")),
        P(("dp", "fsdp"), None),
    )
    out_specs = (
        P(("dp", "fsdp"), None),
        P(("dp", "fsdp"), None),
        P(("dp", "fsdp")),
        P(("dp", "fsdp")),
    )
    return jax.shard_map(body, mesh=mesh, in_specs=in_specs, out_specs=out_specs, check_vma=False)
```

profile of v0, /device:TPU:0, one launch (start us, length us, event | category | flops | bytes accessed | tf_op | source)
XLA Modules:
  0.0 679.6 jit_solution(17159015228087493320)
XLA Ops:
  8.8 42.2 %all-reduce = bf16[5120]{0:T(1024)(128)(2,1)S(1)} all-reduce(bf16[5120]{0:T(1024)(128)(2,1)S(1)} %dynamic-update-slice), channel_id=1, replica_groups=mesh['dp'=4,'fsdp'=8] {'dp','fsdp'}, use_global_device_ids=true, to_apply=%add | all-reduce | flops 5120 | bytes 20480
  52.8 3.9 copy.109
  63.7 12.3 %all-gather.2.cloned.1.call-done = bf16[2097152]{0:T(1024)(128)(2,1)} async-done(((bf16[65536]{0:T(1024)(128)(2,1)}), bf16[2097152]{0:T(1024)(128)(2,1)}) %all-gather.2.cloned.1.call-update) | async-done | bytes 4194320 | tf_op jit(solution)/shard_map/all_gather | solution.py:133
  76.0 5.5 reshape.308
  88.2 5.6 convolution_bitcast_fusion
  99.8 5.3 copy.95
  105.1 4.6 select_reduce_fusion.3
  109.7 4.4 fusion
  118.2 7.9 %fusion.84 = bf16[4,128,512]{2,1,0:T(8,128)(2,1)} fusion(bf16[2048,4,128]{2,0,1:T(8,128)(2,1)} %add_convert_fusion.3, f32[4,512,2048]{2,1,0:T(8,128)S(1)} %get-tuple-element.67, f32[4,512]{1,0:T(4,128)} %copy-done.45, f32[4,512]{1,0:T(4,128)S(1)} %get-tuple-element.66, pred[512,2048]{1,0:T(8,128)(4,1)S(1)} %get-tuple-element.52), kind=kOutput, calls=%fused_computation.151 | convolution fusion | flops 1090781184 | bytes 20463616 | tf_op jit(solution)/shard_map/hqk,khd->qhd/dot_general | solution.py:85
  126.1 4.9 select_reduce_fusion.2
  131.1 4.0 fusion.1
  137.0 8.2 %fusion.83 = bf16[4,128,512]{2,1,0:T(8,128)(2,1)} fusion(bf16[2048,4,128]{2,0,1:T(8,128)(2,1)} %add_convert_fusion.3, f32[4,512,2048]{2,1,0:T(8,128)S(1)} %get-tuple-element.65, f32[4,512]{1,0:T(4,128)} %copy-done.46, f32[4,512]{1,0:T(4,128)S(1)} %get-tuple-element.64, pred[512,2048]{1,0:T(8,128)(4,1)} %get-tuple-element.53), kind=kOutput, calls=%fused_computation.150 | convolution fusion | flops 1090781184 | bytes 20463616 | tf_op jit(solution)/shard_map/hqk,khd->qhd/dot_general | solution.py:85
  145.2 4.6 select_reduce_fusion.1
  149.8 4.0 fusion.2
  155.8 7.8 %fusion.82 = bf16[4,128,512]{2,1,0:T(8,128)(2,1)} fusion(bf16[2048,4,128]{2,0,1:T(8,128)(2,1)} %add_convert_fusion.3, f32[4,512,2048]{2,1,0:T(8,128)S(1)} %get-tuple-element.63, f32[4,512]{1,0:T(4,128)} %copy-done.47, f32[4,512]{1,0:T(4,128)S(1)} %get-tuple-element.62, pred[512,2048]{1,0:T(8,128)(4,1)S(1)} %copy-done.10), kind=kOutput, calls=%fused_computation.149 | convolution fusion | flops 1090781184 | bytes 20463616 | tf_op jit(solution)/shard_map/hqk,khd->qhd/dot_general | solution.py:85
  163.6 4.9 select_reduce_fusion
  168.5 4.0 fusion.3
  174.5 7.9 %fusion.81 = bf16[4,128,512]{2,1,0:T(8,128)(2,1)} fusion(bf16[2048,4,128]{2,0,1:T(8,128)(2,1)} %add_convert_fusion.3, f32[4,512,2048]{2,1,0:T(8,128)S(1)} %get-tuple-element.61, f32[4,512]{1,0:T(4,128)} %copy-done.48, f32[4,512]{1,0:T(4,128)S(1)} %get-tuple-element.60, pred[512,2048]{1,0:T(8,128)(4,1)S(1)} %copy-done.12), kind=kOutput, calls=%fused_computation.148 | convolution fusion | flops 1090781184 | bytes 20463616 | tf_op jit(solution)/shard_map/hqk,khd->qhd/dot_general | solution.py:85
  192.4 22.9 %fusion.18 = (bf16[2048,1024]{1,0:T(8,128)(2,1)S(1)}, f32[2048,1024]{1,0:T(8,128)}) fusion(f32[1024]{0:T(1024)S(1)} %copy-done.57, bf16[512,1024]{1,0:T(8,128)(2,1)S(1)} %reshape_reshape.18, f32[2048,512]{0,1:T(8,128)S(1)} %get-tuple-element.69, f32[512]{0:T(512)S(1)} %copy-done.58, f32[512]{0:T(512)S(1)} %copy-done.52, f32[2048]{0:T(1024)S(1)} %add_rsqrt_fusion.1, ...), kind=kOutput, calls=%fused_computation.40 | convolution fusion | flops 2291138560 | bytes 17850368 | tf_op jit(solution)/shard_map/dot_general | solution.py:151
  222.6 4.1 convert_reduce_fusion.2
  226.7 3.7 fusion.120
  230.4 8.4 %convert_reduce_fusion = (f32[1024]{0:T(1024)}, bf16[2048,1024]{1,0:T(8,128)(2,1)S(1)}) fusion(f32[2048,1024]{1,0:T(8,128)} %get-tuple-element.71, f32[1024]{0:T(1024)S(1)} %copy-done.57, bf16[2048,512]{0,1:T(8,128)(2,1)S(1)} %get-tuple-element.29, bf16[1024,512]{1,0:T(8,128)(2,1)S(1)} %copy-done.38), kind=kOutput, calls=%fused_computation.48 | convolution fusion | flops 2174745600 | bytes 15736832 | tf_op jit(solution)/shard_map/td,fd->tf/dot_general | solution.py:174
  238.9 5.1 multiply_reduce_fusion.4
  244.0 3.8 fusion.105
  254.2 8.5 %fusion.12 = f32[4,128,2048]{2,1,0:T(8,128)} fusion(bf16[512,4,128]{0,2,1:T(8,128)(2,1)} %bitcast.177, f32[4,512,2048]{2,1,0:T(8,128)S(1)} %bitcast.142, f32[4,512]{1,0:T(4,128)S(1)} %copy-done.43, pred[512,2048]{1,0:T(8,128)(4,1)} %get-tuple-element.53), kind=kOutput, calls=%fused_computation.36 | convolution fusion | flops 1086324736 | bytes 22552576 | tf_op jit(solution)/shard_map/hqk,qhd->khd/dot_general | solution.py:115
  262.6 12.5 %multiply_reduce_fusion.2 = (f32[4,512]{1,0:T(4,128)S(1)}, f32[4,512,2048]{2,1,0:T(8,128)}) fusion(f32[4,512,2048]{2,1,0:T(8,128)} %copy-done.3, f32[4,512]{1,0:T(4,128)S(1)} %copy-done.43, pred[512,2048]{1,0:T(8,128)(4,1)} %get-tuple-element.53, bf16[512,4,128]{0,2,1:T(8,128)(2,1)} %bitcast.178, bf16[2048,4,128]{2,0,1:T(8,128)(2,1)S(1)} %copy-done.5), kind=kOutput, calls=%fused_computation.7 | convolution fusion | flops 1090516992 | bytes 37240832 | tf_op jit(solution)/shard_map/qhd,khd->hqk/dot_general | solution.py:104
  275.2 12.7 %multiply_reduce_fusion.3 = (f32[4,512]{1,0:T(4,128)S(1)}, f32[4,512,2048]{2,1,0:T(8,128)}) fusion(f32[4,512,2048]{2,1,0:T(8,128)} %copy-done, f32[4,512]{1,0:T(4,128)S(1)} %copy-done.44, pred[512,2048]{1,0:T(8,128)(4,1)S(1)} %copy-done.8, bf16[512,4,128]{0,2,1:T(8,128)(2,1)S(1)} %bitcast.171, bf16[2048,4,128]{2,0,1:T(8,128)(2,1)S(1)} %copy-done.5), kind=kOutput, calls=%fused_computation.10 | convolution fusion | flops 1090516992 | bytes 37240832 | tf_op jit(solution)/shard_map/qhd,khd->hqk/dot_general | solution.py:104
  287.9 29.3 %multiply_convert_fusion.2 = (bf16[4,512,2048]{2,1,0:T(8,128)(2,1)}, bf16[4,512,2048]{2,1,0:T(8,128)(2,1)}) fusion(f32[4,512,2048]{2,1,0:T(8,128)} %get-tuple-element.80, f32[4,512,2048]{2,1,0:T(8,128)} %copy-done.3, f32[4,512]{1,0:T(4,128)S(1)} %get-tuple-element.79, f32[4,512]{1,0:T(4,128)S(1)} %copy-done.43, pred[512,2048]{1,0:T(8,128)(4,1)S(1)} %copy-done.15, ...), kind=kLoop, calls=%fused_computation.6 | loop fusion | flops 41943040 | bytes 86016000 | tf_op jit(solution)/shard_map/convert_element_type | solution.py:108
  317.2 7.2 %fusion.86 = bf16[512,4,128]{0,2,1:T(8,128)(2,1)} fusion(bf16[2048,4,128]{0,2,1:T(8,128)(2,1)S(1)} %bitcast.147, bf16[4,512,2048]{2,1,0:T(8,128)(2,1)} %get-tuple-element.87), kind=kOutput, calls=%fused_computation.153 | convolution fusion | flops 1074003968 | bytes 11010048 | tf_op jit(solution)/shard_map/hqk,khd->qhd/dot_general | solution.py:110
  327.9 7.8 %fusion.85 = bf16[512,4,128]{0,2,1:T(8,128)(2,1)} fusion(bf16[2048,4,128]{0,2,1:T(8,128)(2,1)S(1)} %bitcast.148, bf16[4,512,2048]{2,1,0:T(8,128)(2,1)} %get-tuple-element.88), kind=kOutput, calls=%fused_computation.152 | convolution fusion | flops 1074003968 | bytes 11010048 | tf_op jit(solution)/shard_map/hqk,khd->qhd/dot_general | solution.py:110
  335.7 6.7 fusion.117
  342.5 7.9 %fusion.8 = f32[4,128,2048]{2,1,0:T(8,128)} fusion(bf16[512,4,128]{0,2,1:T(8,128)(2,1)} %bitcast.175, f32[4,512,2048]{2,1,0:T(8,128)S(1)} %bitcast.140, f32[4,512]{1,0:T(4,128)S(1)} %copy-done.42, pred[512,2048]{1,0:T(8,128)(4,1)} %get-tuple-element.55), kind=kOutput, calls=%fused_computation.34 | convolution fusion | flops 1086324736 | bytes 22552576 | tf_op jit(solution)/shard_map/hqk,qhd->khd/dot_general | solution.py:115
  350.4 13.7 %multiply_reduce_fusion = (f32[4,512]{1,0:T(4,128)S(1)}, f32[4,512,2048]{2,1,0:T(8,128)}) fusion(f32[4,512,2048]{2,1,0:T(8,128)} %copy-done.2, f32[4,512]{1,0:T(4,128)S(1)} %copy-done.42, pred[512,2048]{1,0:T(8,128)(4,1)} %get-tuple-element.55, bf16[512,4,128]{0,2,1:T(8,128)(2,1)} %bitcast.176, bf16[2048,4,128]{2,0,1:T(8,128)(2,1)} %add_convert_fusion.3), kind=kOutput, calls=%fused_computation.1 | convolution fusion | flops 1090516992 | bytes 37240832 | tf_op jit(solution)/shard_map/qhd,khd->hqk/dot_general | solution.py:104
  364.0 10.4 %fusion.10 = f32[4,128,2048]{2,1,0:T(8,128)} fusion(bf16[512,4,128]{0,2,1:T(8,128)(2,1)S(1)} %bitcast.173, f32[4,512,2048]{2,1,0:T(8,128)} %copy-done.1, f32[4,512]{1,0:T(4,128)S(1)} %copy-done.41, pred[512,2048]{1,0:T(8,128)(4,1)S(1)} %copy-done.11), kind=kOutput, calls=%fused_computation.35 | convolution fusion | flops 1086324736 | bytes 22552576 | tf_op jit(solution)/shard_map/hqk,qhd->khd/dot_general | solution.py:115
  374.4 12.7 %multiply_reduce_fusion.1 = (f32[4,512]{1,0:T(4,128)S(1)}, f32[4,512,2048]{2,1,0:T(8,128)}) fusion(f32[4,512,2048]{2,1,0:T(8,128)} %copy-done.1, f32[4,512]{1,0:T(4,128)S(1)} %copy-done.41, pred[512,2048]{1,0:T(8,128)(4,1)S(1)} %copy-done.11, bf16[512,4,128]{0,2,1:T(8,128)(2,1)S(1)} %bitcast.174, bf16[2048,4,128]{2,0,1:T(8,128)(2,1)S(1)} %copy-done.6), kind=kOutput, calls=%fused_computation.4 | convolution fusion | flops 1090516992 | bytes 37240832 | tf_op jit(solution)/shard_map/qhd,khd->hqk/dot_general | solution.py:104
  387.1 29.4 %multiply_convert_fusion = (bf16[4,512,2048]{2,1,0:T(8,128)(2,1)}, bf16[4,512,2048]{2,1,0:T(8,128)(2,1)}) fusion(f32[4,512,2048]{2,1,0:T(8,128)} %get-tuple-element.82, f32[4,512,2048]{2,1,0:T(8,128)} %copy-done.2, f32[4,512]{1,0:T(4,128)S(1)} %get-tuple-element.81, f32[4,512]{1,0:T(4,128)S(1)} %copy-done.42, pred[512,2048]{1,0:T(8,128)(4,1)S(1)} %copy-done.13, ...), kind=kLoop, calls=%fused_computation | loop fusion | flops 41943040 | bytes 86016000 | tf_op jit(solution)/shard_map/convert_element_type | solution.py:108
  416.5 7.2 %fusion.87 = bf16[512,4,128]{0,2,1:T(8,128)(2,1)} fusion(bf16[2048,4,128]{0,2,1:T(8,128)(2,1)S(1)} %bitcast.149, bf16[4,512,2048]{2,1,0:T(8,128)(2,1)} %get-tuple-element.86), kind=kOutput, calls=%fused_computation.154 | convolution fusion | flops 1074003968 | bytes 11010048 | tf_op jit(solution)/shard_map/hqk,khd->qhd/dot_general | solution.py:110
  440.0 7.2 %fusion.88 = bf16[512,4,128]{0,2,1:T(8,128)(2,1)} fusion(bf16[2048,4,128]{0,2,1:T(8,128)(2,1)S(1)} %bitcast.150, bf16[4,512,2048]{2,1,0:T(8,128)(2,1)} %get-tuple-element.85), kind=kOutput, calls=%fused_computation.155 | convolution fusion | flops 1074003968 | bytes 11010048 | tf_op jit(solution)/shard_map/hqk,khd->qhd/dot_general | solution.py:110
  447.2 12.9 %add_convert_fusion = bf16[4,128,2048]{2,1,0:T(8,128)(2,1)S(1)} fusion(f32[4,128,2048]{2,1,0:T(8,128)} %fusion.8, f32[4,128,2048]{2,1,0:T(8,128)} %fusion.10, f32[4,128,2048]{2,1,0:T(8,128)} %fusion.12, bf16[512,4,128]{0,2,1:T(8,128)(2,1)S(1)} %bitcast.172, f32[4,512,2048]{2,1,0:T(8,128)} %copy-done, f32[4,512]{1,0:T(4,128)S(1)} %copy-done.44, ...), kind=kOutput, calls=%fused_computation.107 | convolution fusion | flops 1090519040 | bytes 33038336 | tf_op jit(solution)/shard_map/hqk,qhd->khd/dot_general | solution.py:115
  460.2 8.9 %add_convert_fusion.1 = bf16[4,128,2048]{2,1,0:T(8,128)(2,1)S(1)} fusion(f32[4,128,2048]{2,1,0:T(8,128)} %fusion.119, f32[4,128,2048]{2,1,0:T(8,128)} %fusion.117, f32[4,128,2048]{2,1,0:T(8,128)} %fusion.118, bf16[512,4,128]{0,2,1:T(8,128)(2,1)S(1)} %bitcast.164, bf16[4,512,2048]{2,1,0:T(8,128)(2,1)} %get-tuple-element.85), kind=kOutput, calls=%fused_computation.109 | convolution fusion | flops 1077936128 | bytes 23592960 | tf_op jit(solution)/shard_map/hqk,qhd->khd/dot_general | solution.py:112
  472.3 4.7 multiply_bitcast_fusion
  477.0 3.5 copy.118
  487.4 4.7 copy.143
  492.2 3.9 copy.119
  496.1 3.6 fusion.89
  505.4 5.4 copy.120
  513.4 40.8 %all-reduce.2 = f32[5120]{0:T(1024)S(1)} all-reduce(f32[5120]{0:T(1024)S(1)} %constant_dynamic-update-slice_fusion), channel_id=3, replica_groups=mesh['dp'=4,'fsdp'=8] {'dp','fsdp'}, use_global_device_ids=true, to_apply=%region_33.34.clone | all-reduce | flops 5120 | bytes 40960
  554.8 116.1 %all-reduce.5.cloned.1.call-done = f32[2097152]{0:T(1024)} async-done(((f32[2097152]{0:T(1024)}), f32[2097152]{0:T(1024)}) %all-reduce.5.cloned.1.call-update) | async-done | bytes 8388624
  (235 shorter events, 96.7 us)
Async XLA Ops:
  7.2 49.5 %copy-start.35 = (bf16[2048,512]{1,0:T(8,128)(2,1)S(1)}, bf16[2048,512]{1,0:T(8,128)(2,1)}, u32[]{:S(2)}) copy-start(bf16[2048,512]{1,0:T(8,128)(2,1)} %param.7) | copy-start | bytes 6291460
  7.2 68.8 %all-gather.2.cloned.1.call-start = ((), (), s32[]{:S(2)}) async-start(), calls=%async_computation | async-start | bytes 4325376 | tf_op jit(solution)/shard_map/all_gather | solution.py:133
  7.9 663.0 %all-reduce.5.cloned.1.call-start = ((), (), s32[]{:S(2)}) async-start(), calls=%async_computation.1 | async-start | bytes 16777216
  63.7 54.5 %copy-start.7 = (pred[512,2048]{1,0:T(8,128)(4,1)}, pred[512,2048]{1,0:T(8,128)(4,1)S(1)}, u32[]{:S(2)}) copy-start(pred[512,2048]{1,0:T(8,128)(4,1)S(1)} %get-tuple-element.52) | copy-start | bytes 3145732
  81.5 5.1 slice-start.12
  109.7 8.5 %copy-start = (f32[4,512,2048]{2,1,0:T(8,128)}, f32[4,512,2048]{2,1,0:T(8,128)S(1)}, u32[]{:S(2)}) copy-start(f32[4,512,2048]{2,1,0:T(8,128)S(1)} %get-tuple-element.67) | copy-start | bytes 50331652
  109.7 6.9 %copy-start.22 = (f32[2048,4,128]{2,0,1:T(8,128)S(1)}, f32[2048,4,128]{2,0,1:T(8,128)}, u32[]{:S(2)}) copy-start(f32[2048,4,128]{2,0,1:T(8,128)} %copy.95) | copy-start | bytes 12582916
  126.1 4.9 copy-start.14
  131.0 6.0 copy-start.3
  137.0 8.2 %copy-start.10 = (pred[512,2048]{1,0:T(8,128)(4,1)S(1)}, pred[512,2048]{1,0:T(8,128)(4,1)}, u32[]{:S(2)}) copy-start(pred[512,2048]{1,0:T(8,128)(4,1)} %get-tuple-element.54) | copy-start | bytes 3145732
  149.8 5.9 copy-start.1
  163.6 4.9 copy-start.12
  168.5 6.0 copy-start.2
  182.4 6.1 copy-start.37
  182.4 6.2 copy-start.60
  192.4 22.9 %copy-start.38 = (bf16[1024,512]{1,0:T(8,128)(2,1)S(1)}, bf16[1024,512]{1,0:T(8,128)(2,1)}, u32[]{:S(2)}) copy-start(bf16[1024,512]{1,0:T(8,128)(2,1)} %reshape_reshape.19) | copy-start | bytes 3145732
  192.4 22.9 %copy-start.59 = (f32[512]{0:T(512)S(1)}, f32[512]{0:T(512)}, u32[]{:S(2)}) copy-start(f32[512]{0:T(512)} %get-tuple-element.47) | copy-start | bytes 6148
  244.0 9.1 %slice-start.4 = ((s8[16777216]{0:T(1024)(128)(4,1)}), s8[4194304]{0:T(1024)(128)(4,1)S(1)}, s32[]{:S(2)}) async-start(s8[16777216]{0:T(1024)(128)(4,1)} %bitcast.141), calls=%async_computation.6 | async-start | bytes 8388608
  244.0 9.1 %slice-start.5 = ((s8[16777216]{0:T(1024)(128)(4,1)}), s8[4194304]{0:T(1024)(128)(4,1)S(1)}, s32[]{:S(2)}) async-start(s8[16777216]{0:T(1024)(128)(4,1)} %bitcast.141), calls=%async_computation.7 | async-start | bytes 8388608
  247.8 5.3 slice-start.6
  254.2 8.5 %copy-start.5 = (bf16[2048,4,128]{2,0,1:T(8,128)(2,1)S(1)}, bf16[2048,4,128]{2,0,1:T(8,128)(2,1)}, u32[]{:S(2)}) copy-start(bf16[2048,4,128]{2,0,1:T(8,128)(2,1)} %add_convert_fusion.3) | copy-start | bytes 6291460
  262.6 12.5 %copy-start.8 = (pred[512,2048]{1,0:T(8,128)(4,1)S(1)}, pred[512,2048]{1,0:T(8,128)(4,1)}, u32[]{:S(2)}) copy-start(pred[512,2048]{1,0:T(8,128)(4,1)} %copy-done.7) | copy-start | bytes 3145732
  262.6 12.5 %copy-start.44 = (f32[4,512]{1,0:T(4,128)S(1)}, f32[4,512]{1,0:T(4,128)}, u32[]{:S(2)}) copy-start(f32[4,512]{1,0:T(4,128)} %log_add_fusion.3) | copy-start | bytes 24580
  275.2 12.7 %copy-start.15 = (pred[512,2048]{1,0:T(8,128)(4,1)S(1)}, pred[512,2048]{1,0:T(8,128)(4,1)}, u32[]{:S(2)}) copy-start(pred[512,2048]{1,0:T(8,128)(4,1)} %get-tuple-element.53) | copy-start | bytes 3145732
  287.9 29.3 %copy-start.4 = (bf16[1,2048,512]{1,2,0:T(8,128)(2,1)S(1)}, bf16[1,2048,512]{1,2,0:T(8,128)(2,1)}, u32[]{:S(2)}) copy-start(bf16[1,2048,512]{1,2,0:T(8,128)(2,1)} %slice.259) | copy-start | bytes 6291460
  317.2 7.3 %slice-start.10 = ((s8[8388608]{0:T(1024)(128)(4,1)}), s8[4194304]{0:T(1024)(128)(4,1)S(1)}, s32[]{:S(2)}) async-start(s8[8388608]{0:T(1024)(128)(4,1)} %bitcast.153), calls=%async_computation.12 | async-start | bytes 8388608
  317.2 7.3 %slice-start.11 = ((s8[8388608]{0:T(1024)(128)(4,1)}), s8[4194304]{0:T(1024)(128)(4,1)S(1)}, s32[]{:S(2)}) async-start(s8[8388608]{0:T(1024)(128)(4,1)} %bitcast.153), calls=%async_computation.13 | async-start | bytes 8388608
  317.2 7.3 %copy-start.27 = (bf16[512,512]{0,1:T(8,128)(2,1)S(1)}, bf16[512,512]{0,1:T(8,128)(2,1)}, u32[]{:S(2)}) copy-start(bf16[512,512]{0,1:T(8,128)(2,1)} %get-tuple-element.44) | copy-start | bytes 1572868
  324.5 18.0 %slice-start = ((s8[16777216]{0:T(1024)(128)(4,1)}), s8[4194304]{0:T(1024)(128)(4,1)S(1)}, s32[]{:S(2)}) async-start(s8[16777216]{0:T(1024)(128)(4,1)} %bitcast.139), calls=%async_computation.2 | async-start | bytes 8388608
  324.5 18.0 %slice-start.1 = ((s8[16777216]{0:T(1024)(128)(4,1)}), s8[4194304]{0:T(1024)(128)(4,1)S(1)}, s32[]{:S(2)}) async-start(s8[16777216]{0:T(1024)(128)(4,1)} %bitcast.139), calls=%async_computation.3 | async-start | bytes 8388608
  327.9 7.8 %copy-start.26 = (bf16[512,512]{0,1:T(8,128)(2,1)S(1)}, bf16[512,512]{0,1:T(8,128)(2,1)}, u32[]{:S(2)}) copy-start(bf16[512,512]{0,1:T(8,128)(2,1)} %get-tuple-element.41) | copy-start | bytes 1572868
  327.9 14.5 %slice-start.2 = ((s8[16777216]{0:T(1024)(128)(4,1)}), s8[4194304]{0:T(1024)(128)(4,1)S(1)}, s32[]{:S(2)}) async-start(s8[16777216]{0:T(1024)(128)(4,1)} %bitcast.139), calls=%async_computation.4 | async-start | bytes 8388608
  335.7 6.7 slice-start.3
  335.7 6.8 copy-start.42
  350.3 13.7 %copy-start.11 = (pred[512,2048]{1,0:T(8,128)(4,1)S(1)}, pred[512,2048]{1,0:T(8,128)(4,1)}, u32[]{:S(2)}) copy-start(pred[512,2048]{1,0:T(8,128)(4,1)} %get-tuple-element.54) | copy-start | bytes 3145732
  350.3 13.7 %copy-start.29 = (bf16[512,512]{0,1:T(8,128)(2,1)S(1)}, bf16[512,512]{0,1:T(8,128)(2,1)}, u32[]{:S(2)}) copy-start(bf16[512,512]{0,1:T(8,128)(2,1)} %get-tuple-element.38) | copy-start | bytes 1572868
  350.3 13.7 %copy-start.41 = (f32[4,512]{1,0:T(4,128)S(1)}, f32[4,512]{1,0:T(4,128)}, u32[]{:S(2)}) copy-start(f32[4,512]{1,0:T(4,128)} %log_add_fusion.1) | copy-start | bytes 24580
  364.0 10.4 %copy-start.6 = (bf16[2048,4,128]{2,0,1:T(8,128)(2,1)S(1)}, bf16[2048,4,128]{2,0,1:T(8,128)(2,1)}, u32[]{:S(2)}) copy-start(bf16[2048,4,128]{2,0,1:T(8,128)(2,1)} %add_convert_fusion.3) | copy-start | bytes 6291460
  374.4 12.7 %copy-start.13 = (pred[512,2048]{1,0:T(8,128)(4,1)S(1)}, pred[512,2048]{1,0:T(8,128)(4,1)}, u32[]{:S(2)}) copy-start(pred[512,2048]{1,0:T(8,128)(4,1)} %get-tuple-element.55) | copy-start | bytes 3145732
  416.5 7.3 %slice-start.8 = ((s8[8388608]{0:T(1024)(128)(4,1)}), s8[4194304]{0:T(1024)(128)(4,1)S(1)}, s32[]{:S(2)}) async-start(s8[8388608]{0:T(1024)(128)(4,1)} %bitcast.151), calls=%async_computation.10 | async-start | bytes 8388608
  416.5 7.3 %slice-start.9 = ((s8[8388608]{0:T(1024)(128)(4,1)}), s8[4194304]{0:T(1024)(128)(4,1)S(1)}, s32[]{:S(2)}) async-start(s8[8388608]{0:T(1024)(128)(4,1)} %bitcast.151), calls=%async_computation.11 | async-start | bytes 8388608
  416.5 7.3 %copy-start.25 = (bf16[512,512]{0,1:T(8,128)(2,1)S(1)}, bf16[512,512]{0,1:T(8,128)(2,1)}, u32[]{:S(2)}) copy-start(bf16[512,512]{0,1:T(8,128)(2,1)} %get-tuple-element.43) | copy-start | bytes 1572868
  440.0 7.2 %copy-start.9 = (pred[512,2048]{1,0:T(8,128)(4,1)S(1)}, pred[512,2048]{1,0:T(8,128)(4,1)}, u32[]{:S(2)}) copy-start(pred[512,2048]{1,0:T(8,128)(4,1)} %copy-done.7) | copy-start | bytes 3145732
  447.2 13.0 %copy-start.24 = (bf16[512,512]{0,1:T(8,128)(2,1)S(1)}, bf16[512,512]{0,1:T(8,128)(2,1)}, u32[]{:S(2)}) copy-start(bf16[512,512]{0,1:T(8,128)(2,1)} %get-tuple-element.42) | copy-start | bytes 1572868
  460.2 9.0 %copy-start.31 = (bf16[512,4,128]{0,2,1:T(8,128)(2,1)S(1)}, bf16[512,4,128]{0,2,1:T(8,128)(2,1)}, u32[]{:S(2)}) copy-start(bf16[512,4,128]{0,2,1:T(8,128)(2,1)} %fusion.86) | copy-start | bytes 1572868
  460.2 9.0 %copy-start.32 = (bf16[512,4,128]{0,2,1:T(8,128)(2,1)S(1)}, bf16[512,4,128]{0,2,1:T(8,128)(2,1)}, u32[]{:S(2)}) copy-start(bf16[512,4,128]{0,2,1:T(8,128)(2,1)} %fusion.85) | copy-start | bytes 1572868
  460.2 9.0 %copy-start.33 = (bf16[512,4,128]{0,2,1:T(8,128)(2,1)S(1)}, bf16[512,4,128]{0,2,1:T(8,128)(2,1)}, u32[]{:S(2)}) copy-start(bf16[512,4,128]{0,2,1:T(8,128)(2,1)} %fusion.87) | copy-start | bytes 1572868
  460.2 9.0 %copy-start.34 = (bf16[512,4,128]{0,2,1:T(8,128)(2,1)S(1)}, bf16[512,4,128]{0,2,1:T(8,128)(2,1)}, u32[]{:S(2)}) copy-start(bf16[512,4,128]{0,2,1:T(8,128)(2,1)} %fusion.88) | copy-start | bytes 1572868
  (31 other events, 70.6 us)
Sparse Core Ops, SparseCore 0:
  11.0 64.9 all-gather.1
  492.3 178.5 all-reduce.4
where the time goes:
time: 690 us; the launch traced here: 680 us
  matrix products  267 us (39%)
  waiting for transfers between devices  129 us (19%)
  other arithmetic  102 us (15%)
  local copies, waits for them, and re-layouts  84.1 us (12%)
  blocking collectives  83 us (12%)
  between operations  15.1 us (2%)
    unnamed x3, waiting for transfers between devices  117 us
    unnamed x2, blocking collectives  83 us
    convert_element_type x2, other arithmetic, attention_backward(): grad_scores = (attn_probs * (grad_probs - centre)).astype(jnp.bfloat16)  58.7 us
    dot_general x4, matrix products, attention_backward(): jnp.einsum('qhd,khd->hqk', grad_block, values, preferred_element_type=jnp...  51.6 us
    dot_general x4, matrix products, attention_backward(): jnp.einsum('hqk,qhd->khd', attn_probs.astype(jnp.bfloat16), grad_block, p...  39.6 us
    unnamed x168, local copies, waits for them, and re-layouts  37.3 us
    dot_general x4, matrix products, attention_forward(): jnp.einsum('hqk,khd->qhd', attn_probs, values, preferred_element_type=jnp...  31.8 us
    dot_general x4, matrix products, attention_backward(): jnp.einsum('hqk,khd->qhd', grad_scores, key_heads, preferred_element_type...  29.5 us
  transfers between devices with their start and end apart: 2, of which 2 were waited for; matrix products, arithmetic and copies ran while one was open for 5% of the time, Pallas kernels for 0%

commit v1 on v0

v1 whole, which is shorter than its diff:
```python
import functools
import math

import jax
import jax.numpy as jnp
from jax import lax
from jax.experimental import pallas as pl
from jax.experimental.pallas import tpu as pltpu
from jax.sharding import PartitionSpec as P

HEADS = 4
HEAD_DIM = 128
FF = 1024
AXES = ("dp", "fsdp")
NORM_EPS = 1e-05
BLOCKS = 32
QKV_ROWS = 48
Q_ROWS = 4 * QKV_ROWS + 16
R_ROWS = 320
FAR = -1e30
f32 = jnp.float32
bf16 = jnp.bfloat16
NT = (((1,), (1,)), ((), ()))
NN = (((1,), (0,)), ((), ()))
TN = (((0,), (0,)), ((), ()))
TT = (((0,), (1,)), ((), ()))
VMEM_BYTES = 60 << 20


def dot(a, b, dims):
    return lax.dot_general(a, b, dims, preferred_element_type=f32)


def params():
    return pltpu.CompilerParams(vmem_limit_bytes=VMEM_BYTES)


def whole(shape):
    return pl.BlockSpec(shape, lambda *_: (0,) * len(shape))


def scalar_spec():
    return pl.BlockSpec(memory_space=pltpu.SMEM)


def owner_of(place, me, order):
    mask = 0
    for bit, step in enumerate(order):
        mask = mask + ((place >> bit) & 1) * step
    return jnp.bitwise_xor(me, mask)


def split3(value):
    high = value.astype(bf16)
    rest = value - high.astype(f32)
    middle = rest.astype(bf16)
    low = (rest - middle.astype(f32)).astype(bf16)
    return high, middle, low


PANELS = ((0, 48, 4), (192, 16, 4), (256, 16, 8), (384, 32, 4))


def pack_kernel(flat, vec, q_out, r_out, wide):
    wide[...] = flat[...].astype(f32)
    parts = []
    for start, rows, count in PANELS:
        for j in range(count):
            parts.append(wide[pl.ds(start + j, rows, stride=count), :].astype(bf16))
    q_out[0:192, :] = jnp.concatenate(parts[:4], axis=0)
    q_out[192:208, :] = vec[...]
    r_out[...] = jnp.concatenate(parts[4:], axis=0)


def pack(flat, vec):
    return pl.pallas_call(
        pack_kernel,
        out_shape=[
            jax.ShapeDtypeStruct((Q_ROWS, 128), bf16),
            jax.ShapeDtypeStruct((R_ROWS, 128), bf16),
        ],
        scratch_shapes=[pltpu.VMEM((512, 128), f32)],
        name="pack",
    )(flat, vec)


def project_kernel(
    order, vec_width, vec_count, me_ref, ends, tokens, first, second, qkv, keys_extra, query_extra, vec_out, weight, vec
):
    step = pl.program_id(0)
    rows = tokens.shape[0]
    me = me_ref[0]

    @pl.when(step == 0)
    def _():
        half = BLOCKS // 2
        for base, ref in ((0, first), (half, second)):

            def place(i, _, base=base, ref=ref):
                d = owner_of(base + i, me, order)
                for j in range(4):
                    weight[pl.ds(pl.multiple_of(d * QKV_ROWS, 16), QKV_ROWS), 128 * j : 128 * (j + 1)] = ref[
                        pl.ds(pl.multiple_of(i * Q_ROWS + QKV_ROWS * j, 16), QKV_ROWS), :
                    ]
                return 0

            lax.fori_loop(0, half, place, 0)
        vec[...] = jnp.zeros_like(vec)
        for base, ref in ((0, first), (half, second)):

            def add(i, _, base=base, ref=ref):
                d = owner_of(base + i, me, order)
                row = (d * vec_width) // 128
                piece = ref[pl.ds(pl.multiple_of(i * Q_ROWS + 4 * QKV_ROWS, 16), 16), :].astype(f32)
                vec[pl.ds(row, 2), :] = vec[pl.ds(row, 2), :] + piece[0:2, :]
                return 0

            lax.fori_loop(0, half, add, 0)
        vec_out[...] = vec[...]

    x = tokens[...]
    scale = 1.0 / math.sqrt(HEAD_DIM)
    query_bias = jnp.concatenate([vec[j : j + 1, :] for j in range(4)], axis=1)
    value_bias = jnp.concatenate([vec[4 + j : 5 + j, :] for j in range(4)], axis=1)
    queries = ((dot(x, weight[0:512, :], NN) + query_bias) * scale).astype(bf16)
    key_heads = dot(x, weight[512:1024, :], NN).astype(bf16)
    values = (dot(x, weight[1024:1536, :], NN) + value_bias).astype(bf16)
    qkv[:, 0:512] = queries
    qkv[:, 512:1024] = key_heads
    qkv[:, 1024:1536] = values
    places = step * rows + lax.broadcasted_iota(jnp.int32, (rows, ends.shape[1]), 0)
    label = jnp.sum((ends[...] <= places).astype(f32), axis=1, keepdims=True)
    lane = lax.broadcasted_iota(jnp.int32, (rows, 128), 1)
    same = lane.astype(f32) == label
    keys_extra[...] = jnp.where(lane < 8, jnp.where(same, 1.0, 0.0), jnp.where(lane < 12, 1.0, 0.0)).astype(bf16)
    apart = jnp.where((lane < 8) & jnp.logical_not(same), FAR, 0.0)
    product = queries.astype(f32) * key_heads.astype(f32)
    for h in range(HEADS):
        own = jnp.sum(product[:, 128 * h : 128 * (h + 1)], axis=1, keepdims=True)
        query_extra[h] = jnp.where(lane == 8, -own, apart).astype(bf16)


def project(me, ends, tokens, first, second, order, vec_width, vec_count, rows=512):
    count = tokens.shape[0]
    sets = ends.shape[1]
    return pl.pallas_call(
        functools.partial(project_kernel, order, vec_width, vec_count),
        grid=(count // rows,),
        in_specs=[
            scalar_spec(),
            whole((1, sets)),
            pl.BlockSpec((rows, 512), lambda i: (i, 0)),
            whole(first.shape),
            whole(second.shape),
        ],
        out_specs=[
            pl.BlockSpec((rows, 1536), lambda i: (i, 0)),
            pl.BlockSpec((rows, 128), lambda i: (i, 0)),
            pl.BlockSpec((HEADS, rows, 128), lambda i: (0, i, 0)),
            whole((48, 128)),
        ],
        out_shape=[
            jax.ShapeDtypeStruct((count, 1536), bf16),
            jax.ShapeDtypeStruct((count, 128), bf16),
            jax.ShapeDtypeStruct((HEADS, count, 128), bf16),
            jax.ShapeDtypeStruct((48, 128), f32),
        ],
        scratch_shapes=[pltpu.VMEM((1536, 512), bf16), pltpu.VMEM((48, 128), f32)],
        compiler_params=params(),
        name="project",
    )(me, ends, tokens, first, second)


def attend_kernel(q, k, v, query_extra, keys_extra, attended, query_extra_out, total, mixed, peak):
    rows = q.shape[0]
    left = jnp.concatenate([k[...], keys_extra[...]], axis=1)
    right = jnp.concatenate([q[...], query_extra[0]], axis=1)
    scores = dot(left, right, NT)
    weights = jnp.exp(scores)
    total[...] = jnp.sum(weights, axis=0, keepdims=True)
    mixed[...] = dot(v[...], weights.astype(bf16), TN)
    peak[...] = jnp.zeros_like(peak)
    good = jnp.where((total[...] > 1e-20) & (total[...] < 1e30), 0.0, 1.0)

    @pl.when(jnp.sum(good) > 0.0)
    def _():
        again = dot(left, right, NT)
        top = jnp.max(again, axis=0, keepdims=True)
        safe = jnp.exp(again - top)
        total[...] = jnp.sum(safe, axis=0, keepdims=True)
        mixed[...] = dot(v[...], safe.astype(bf16), TN)
        peak[...] = top

    attended[...] = (mixed[...] * (1.0 / total[...])).T.astype(bf16)
    offset = jnp.broadcast_to(peak[...] + jnp.log(total[...]), (128, rows)).T
    high, middle, low = split3(-offset)
    lane = lax.broadcasted_iota(jnp.int32, (rows, 128), 1)
    extra = query_extra[0].astype(f32)
    extra = jnp.where(lane == 9, high.astype(f32), extra)
    extra = jnp.where(lane == 10, middle.astype(f32), extra)
    extra = jnp.where(lane == 11, low.astype(f32), extra)
    query_extra_out[0] = extra.astype(bf16)


def attend(qkv, query_extra, keys_extra, rows=1024):
    count = qkv.shape[0]
    return pl.pallas_call(
        attend_kernel,
        grid=(HEADS, count // rows),
        in_specs=[
            pl.BlockSpec((rows, 128), lambda h, i: (i, h)),
            pl.BlockSpec((count, 128), lambda h, i: (0, HEADS + h)),
            pl.BlockSpec((count, 128), lambda h, i: (0, 2 * HEADS + h)),
            pl.BlockSpec((1, rows, 128), lambda h, i: (h, i, 0)),
            pl.BlockSpec((count, 128), lambda h, i: (0, 0)),
        ],
        out_specs=[
            pl.BlockSpec((rows, 128), lambda h, i: (i, h)),
            pl.BlockSpec((1, rows, 128), lambda h, i: (h, i, 0)),
        ],
        out_shape=[
            jax.ShapeDtypeStruct((count, 512), bf16),
            jax.ShapeDtypeStruct((HEADS, count, 128), bf16),
        ],
        scratch_shapes=[pltpu.VMEM((1, rows), f32), pltpu.VMEM((128, rows), f32), pltpu.VMEM((1, rows), f32)],
        compiler_params=params(),
        name="attend",
    )(qkv, qkv, qkv, query_extra, keys_extra)


def mean_row(value):
    return jnp.sum(value, axis=1, keepdims=True) * (1.0 / value.shape[1])


def norm_rows(summed):
    centered = summed - mean_row(summed)
    inverse = lax.rsqrt(mean_row(centered * centered) + NORM_EPS)
    return centered * inverse, inverse


def norm_back(grad, normed, inverse):
    return inverse * (grad - mean_row(grad) - normed * mean_row(grad * normed))


def fold8(value):
    return jnp.sum(value.reshape(value.shape[0] // 8, 8, value.shape[1]), axis=0)


def middle_kernel(
    order_in,
    order_out,
    sub,
    me_ref,
    tokens,
    attended,
    cotangent,
    vec,
    first,
    second,
    layer_output,
    grad_first_out,
    grad_attended_out,
    grad_extra,
    keep,
    send,
    vec_out,
    attn_weight,
    in_weight,
    out_weight,
    grad_attn,
    grad_in,
    grad_out,
    sums,
    hidden_sum,
):
    step = pl.program_id(0)
    me = me_ref[0]
    half = BLOCKS // 2

    @pl.when(step == 0)
    def _():
        for base, ref in ((0, first), (half, second)):

            def place(i, _, base=base, ref=ref):
                d = owner_of(base + i, me, order_in)
                start = i * R_ROWS
                a_row = pl.multiple_of(d * 16, 16)
                o_row = pl.multiple_of(d * 32, 16)
                for j in range(4):
                    attn_weight[pl.ds(a_row, 16), 128 * j : 128 * (j + 1)] = ref[
                        pl.ds(pl.multiple_of(start + 16 * j, 16), 16), :
                    ]
                for j in range(8):
                    in_weight[pl.ds(a_row, 16), 128 * j : 128 * (j + 1)] = ref[
                        pl.ds(pl.multiple_of(start + 64 + 16 * j, 16), 16), :
                    ]
                for j in range(4):
                    out_weight[pl.ds(o_row, 32), 128 * j : 128 * (j + 1)] = ref[
                        pl.ds(pl.multiple_of(start + 192 + 32 * j, 16), 32), :
                    ]
                return 0

            lax.fori_loop(0, half, place, 0)
        grad_attn[...] = jnp.zeros_like(grad_attn)
        grad_in[...] = jnp.zeros_like(grad_in)
        grad_out[...] = jnp.zeros_like(grad_out)
        sums[...] = jnp.zeros_like(sums)
        hidden_sum[...] = jnp.zeros_like(hidden_sum)

    def row_of(index):
        return jnp.concatenate([vec[4 * index + j : 4 * index + j + 1, :] for j in range(4)], axis=1)

    attn_bias, ffn_bias, gain_one, shift_one, gain_two, shift_two = [row_of(i) for i in range(2, 8)]
    hidden_bias = jnp.concatenate([vec[32 + j : 33 + j, :] for j in range(8)], axis=1)

    def chain(s):
        sl = slice(s * sub, (s + 1) * sub)
        att = attended[sl, :]
        branch = dot(att, attn_weight[...], NN) + attn_bias
        yield
        normed_one, inverse_one = norm_rows(tokens[sl, :].astype(f32) + branch)
        hidden = normed_one * gain_one + shift_one
        hidden_low = hidden.astype(bf16)
        yield
        pre_act = dot(hidden_low, in_weight[...], NN) + hidden_bias
        yield
        cdf = 0.5 * (1.0 + lax.erf(pre_act * 0.7071067811865476))
        density = jnp.exp(-0.5 * pre_act * pre_act) * 0.3989422804014327
        activated = (pre_act * cdf).astype(bf16)
        slope = cdf + pre_act * density
        yield
        ffn_result = dot(activated, out_weight[...], NN) + ffn_bias
        yield
        normed_two, inverse_two = norm_rows(hidden + ffn_result)
        layer_output[sl, :] = (normed_two * gain_two + shift_two).astype(bf16)
        grad_result = cotangent[sl, :].astype(f32)
        sums[4] += fold8(grad_result * normed_two)
        sums[5] += fold8(grad_result)
        grad_second = norm_back(grad_result * gain_two, normed_two, inverse_two)
        grad_ffn = grad_second.astype(bf16)
        sums[1] += fold8(grad_ffn.astype(f32))
        yield
        grad_activated = dot(grad_ffn, out_weight[...], NT)
        grad_out[...] += dot(activated, grad_ffn, TN)
        yield
        grad_pre = (grad_activated * slope).astype(bf16)
        hidden_sum[...] += fold8(grad_pre.astype(f32))
        yield
        grad_hidden = grad_second + dot(grad_pre, in_weight[...], NT)
        grad_in[...] += dot(hidden_low, grad_pre, TN)
        yield
        sums[2] += fold8(grad_hidden * normed_one)
        sums[3] += fold8(grad_hidden)
        grad_first = norm_back(grad_hidden * gain_one, normed_one, inverse_one)
        grad_first_out[sl, :] = grad_first
        grad_branch = grad_first.astype(bf16)
        sums[0] += fold8(grad_branch.astype(f32))
        yield
        grad_attended = dot(grad_branch, attn_weight[...], NT).astype(bf16)
        grad_attn[...] += dot(att, grad_branch, TN)
        yield
        grad_attended_out[sl, :] = grad_attended
        product = grad_attended.astype(f32) * att.astype(f32)
        lane = lax.broadcasted_iota(jnp.int32, (sub, 128), 1)
        for h in range(HEADS):
            centre = jnp.sum(product[:, 128 * h : 128 * (h + 1)], axis=1, keepdims=True)
            high, middle, low = split3(-centre)
            extra = jnp.where(lane == 0, high.astype(f32), 0.0)
            extra = jnp.where(lane == 1, middle.astype(f32), extra)
            extra = jnp.where(lane == 2, low.astype(f32), extra)
            grad_extra[h, sl, :] = extra.astype(bf16)
        yield

    chains = [chain(s) for s in range(tokens.shape[0] // sub)]
    started = 0
    live = []
    while started < len(chains) or live:
        if started < len(chains):
            live.append(chains[started])
            started += 1
        remaining = []
        for c in live:
            try:
                next(c)
                remaining.append(c)
            except StopIteration:
                pass
        live = remaining

    @pl.when(step == pl.num_programs(0) - 1)
    def _():
        for base, ref in ((0, keep), (half, send)):

            def place(i, _, base=base, ref=ref):
                d = owner_of(base + i, me, order_out)
                start = i * R_ROWS
                a_row = pl.multiple_of(d * 16, 16)
                o_row = pl.multiple_of(d * 32, 16)
                for j in range(4):
                    ref[pl.ds(pl.multiple_of(start + 16 * j, 16), 16), :] = grad_attn[
                        pl.ds(a_row, 16), 128 * j : 128 * (j + 1)
                    ].astype(bf16)
                for j in range(8):
                    ref[pl.ds(pl.multiple_of(start + 64 + 16 * j, 16), 16), :] = grad_in[
                        pl.ds(a_row, 16), 128 * j : 128 * (j + 1)
                    ].astype(bf16)
                for j in range(4):
                    ref[pl.ds(pl.multiple_of(start + 192 + 32 * j, 16), 32), :] = grad_out[
                        pl.ds(o_row, 32), 128 * j : 128 * (j + 1)
                    ].astype(bf16)
                return 0

            lax.fori_loop(0, half, place, 0)
        vec_out[...] = jnp.zeros_like(vec_out)
        for i in range(6):
            row = jnp.sum(sums[i], axis=0, keepdims=True)
            for j in range(4):
                vec_out[8 + 4 * i + j : 9 + 4 * i + j, :] = row[:, 128 * j : 128 * (j + 1)]
        row = jnp.sum(hidden_sum[...], axis=0, keepdims=True)
        for j in range(8):
            vec_out[32 + j : 33 + j, :] = row[:, 128 * j : 128 * (j + 1)]


def middle(me, tokens, attended, cotangent, vec, first, second, order_in, order_out, rows=512, sub=256):
    count = tokens.shape[0]
    by_row = pl.BlockSpec((rows, 512), lambda i: (i, 0))
    half_rows = BLOCKS // 2 * R_ROWS
    return pl.pallas_call(
        functools.partial(middle_kernel, order_in, order_out, sub),
        grid=(count // rows,),
        in_specs=[
            scalar_spec(),
            by_row,
            by_row,
            by_row,
            whole((48, 128)),
            whole(first.shape),
            whole(second.shape),
        ],
        out_specs=[
            by_row,
            by_row,
            by_row,
            pl.BlockSpec((HEADS, rows, 128), lambda i: (0, i, 0)),
            whole((half_rows, 128)),
            whole((half_rows, 128)),
            whole((48, 128)),
        ],
        out_shape=[
            jax.ShapeDtypeStruct((count, 512), bf16),
            jax.ShapeDtypeStruct((count, 512), f32),
            jax.ShapeDtypeStruct((count, 512), bf16),
            jax.ShapeDtypeStruct((HEADS, count, 128), bf16),
            jax.ShapeDtypeStruct((half_rows, 128), bf16),
            jax.ShapeDtypeStruct((half_rows, 128), bf16),
            jax.ShapeDtypeStruct((48, 128), f32),
        ],
        scratch_shapes=[
            pltpu.VMEM((512, 512), bf16),
            pltpu.VMEM((512, FF), bf16),
            pltpu.VMEM((FF, 512), bf16),
            pltpu.VMEM((512, 512), f32),
            pltpu.VMEM((512, FF), f32),
            pltpu.VMEM((FF, 512), f32),
            pltpu.VMEM((6, 8, 512), f32),
            pltpu.VMEM((8, FF), f32),
        ],
        compiler_params=params(),
        name="middle",
    )(me, tokens, attended, cotangent, vec, first, second)


def attend_back_kernel(
    q, k, v, grad, query_extra, keys_extra, grad_extra, grad_query, grad_keys, grad_values, acc
):
    step = pl.program_id(1)
    width = k.shape[0]
    lane = lax.broadcasted_iota(jnp.int32, (width, 128), 1)
    ones = jnp.where(lane < 3, 1.0, 0.0).astype(bf16)
    scores = dot(
        jnp.concatenate([q[...], query_extra[0]], axis=1),
        jnp.concatenate([k[...], keys_extra[...]], axis=1),
        NT,
    )
    centred = dot(
        jnp.concatenate([grad[...], grad_extra[0]], axis=1), jnp.concatenate([v[...], ones], axis=1), NT
    )
    probs = jnp.exp(scores)
    probs_low = probs.astype(bf16)
    grad_scores = (probs * centred).astype(bf16)
    grad_values[...] = dot(grad[...], probs_low, TN).astype(bf16)
    grad_keys[...] = dot(q[...], grad_scores, TN).astype(bf16)
    part = dot(grad_scores, k[...], NN)

    @pl.when(step == 0)
    def _():
        acc[...] = part

    @pl.when(step > 0)
    def _():
        acc[...] += part

    @pl.when(step == pl.num_programs(1) - 1)
    def _():
        grad_query[...] = acc[...].astype(bf16)


def attend_back(qkv, grad_attended, query_extra, keys_extra, grad_extra, width=512):
    count = qkv.shape[0]
    return pl.pallas_call(
        attend_back_kernel,
        grid=(HEADS, count // width),
        in_specs=[
            pl.BlockSpec((count, 128), lambda h, i: (0, h)),
            pl.BlockSpec((width, 128), lambda h, i: (i, HEADS + h)),
            pl.BlockSpec((width, 128), lambda h, i: (i, 2 * HEADS + h)),
            pl.BlockSpec((count, 128), lambda h, i: (0, h)),
            pl.BlockSpec((1, count, 128), lambda h, i: (h, 0, 0)),
            pl.BlockSpec((width, 128), lambda h, i: (i, 0)),
            pl.BlockSpec((1, count, 128), lambda h, i: (h, 0, 0)),
        ],
        out_specs=[
            pl.BlockSpec((count, 128), lambda h, i: (0, h)),
            pl.BlockSpec((128, width), lambda h, i: (h, i)),
            pl.BlockSpec((128, width), lambda h, i: (h, i)),
        ],
        out_shape=[
            jax.ShapeDtypeStruct((count, 512), bf16),
            jax.ShapeDtypeStruct((512, count), bf16),
            jax.ShapeDtypeStruct((512, count), bf16),
        ],
        scratch_shapes=[pltpu.VMEM((count, 128), f32)],
        compiler_params=params(),
        name="attend_back",
    )(qkv, qkv, qkv, grad_attended, query_extra, keys_extra, grad_extra)


def weight_grad_kernel(
    order, vec_width, me_ref, tokens, grad_query, grad_keys, grad_values, vec_in, keep, send, vec, grad_weight
):
    me = me_ref[0]
    half = BLOCKS // 2
    scale = 1.0 / math.sqrt(HEAD_DIM)
    x = tokens[...]
    ones = jnp.ones((8, x.shape[0]), bf16)
    vec[...] = vec_in[...]
    for h in range(HEADS):
        cols = slice(128 * h, 128 * (h + 1))
        gq = grad_query[:, cols]
        gk = grad_keys[cols, :]
        gv = grad_values[cols, :]
        grad_weight[0:512, cols] = dot(gq, x, TN).T * scale
        grad_weight[512:1024, cols] = dot(gk, x, NN).T
        grad_weight[1024:1536, cols] = dot(gv, x, NN).T
        vec[h : h + 1, :] = dot(ones, gq, NN)[0:1] * scale
        vec[4 + h : 5 + h, :] = dot(ones, gv, NT)[0:1]
    for base, ref in ((0, keep), (half, send)):

        def place(i, _, base=base, ref=ref):
            d = owner_of(base + i, me, order)
            start = i * Q_ROWS
            row = pl.multiple_of(d * QKV_ROWS, 16)
            for j in range(4):
                ref[pl.ds(pl.multiple_of(start + QKV_ROWS * j, 16), QKV_ROWS), :] = grad_weight[
                    pl.ds(row, QKV_ROWS), 128 * j : 128 * (j + 1)
                ].astype(bf16)
            pair = vec[pl.ds((d * vec_width) // 128, 2), :]
            pair = jnp.concatenate([pair, jnp.zeros((14, 128), f32)], axis=0)
            ref[pl.ds(pl.multiple_of(start + 4 * QKV_ROWS, 16), 16), :] = pair.astype(bf16)
            return 0

        lax.fori_loop(0, half, place, 0)


def weight_grad(me, tokens, grad_query, grad_keys, grad_values, vec, order, vec_width):
    half_rows = BLOCKS // 2 * Q_ROWS
    vmem = pl.BlockSpec(memory_space=pltpu.VMEM)
    return pl.pallas_call(
        functools.partial(weight_grad_kernel, order, vec_width),
        in_specs=[scalar_spec()] + [vmem] * 5,
        out_specs=[vmem, vmem],
        out_shape=[jax.ShapeDtypeStruct((half_rows, 128), bf16)] * 2,
        scratch_shapes=[pltpu.VMEM((48, 128), f32), pltpu.VMEM((1536, 512), f32)],
        compiler_params=params(),
        name="weight_grad",
    )(me, tokens, grad_query, grad_keys, grad_values, vec)


def input_grad_kernel(order, me_ref, grad_first, grad_query, grad_keys, grad_values, first, second, out, weight):
    step = pl.program_id(0)
    me = me_ref[0]

    @pl.when(step == 0)
    def _():
        half = BLOCKS // 2
        for base, ref in ((0, first), (half, second)):

            def place(i, _, base=base, ref=ref):
                d = owner_of(base + i, me, order)
                for j in range(4):
                    weight[pl.ds(pl.multiple_of(d * QKV_ROWS, 16), QKV_ROWS), 128 * j : 128 * (j + 1)] = ref[
                        pl.ds(pl.multiple_of(i * Q_ROWS + QKV_ROWS * j, 16), QKV_ROWS), :
                    ]
                return 0

            lax.fori_loop(0, half, place, 0)

    scale = 1.0 / math.sqrt(HEAD_DIM)
    total = grad_first[...] + scale * dot(grad_query[...], weight[0:512, :], NT)
    total = total + dot(grad_keys[...], weight[512:1024, :], TT)
    out[...] = total + dot(grad_values[...], weight[1024:1536, :], TT)


def input_grad(me, grad_first, grad_query, grad_keys, grad_values, first, second, order, rows=512):
    count = grad_first.shape[0]
    by_row = pl.BlockSpec((rows, 512), lambda i: (i, 0))
    by_column = pl.BlockSpec((512, rows), lambda i: (0, i))
    return pl.pallas_call(
        functools.partial(input_grad_kernel, order),
        grid=(count // rows,),
        in_specs=[scalar_spec(), by_row, by_row, by_column, by_column, whole(first.shape), whole(second.shape)],
        out_specs=by_row,
        out_shape=jax.ShapeDtypeStruct((count, 512), f32),
        scratch_shapes=[pltpu.VMEM((1536, 512), bf16)],
        compiler_params=params(),
        name="input_grad",
    )(me, grad_first, grad_query, grad_keys, grad_values, first, second)


def unpack_kernel(q_keep, q_got, r_keep, r_got, out, vec_out):
    q_sum = q_keep[...].astype(f32) + q_got[...].astype(f32)
    r_sum = r_keep[...].astype(f32) + r_got[...].astype(f32)
    at = 0
    source = q_sum
    for index, (start, rows, count) in enumerate(PANELS):
        if index == 1:
            source, at = r_sum, 0
        for j in range(count):
            out[pl.ds(start + j, rows, stride=count), :] = source[at : at + rows, :]
            at += rows
    vec_out[...] = q_sum[192:200, :]


def unpack(q_keep, q_got, r_keep, r_got):
    return pl.pallas_call(
        unpack_kernel,
        out_shape=[jax.ShapeDtypeStruct((512, 128), f32), jax.ShapeDtypeStruct((8, 128), f32)],
        name="unpack",
    )(q_keep, q_got, r_keep, r_got)


def swap(array, step, count):
    return lax.ppermute(array, AXES, [(i, i ^ step) for i in range(count)])


def gather_blocks(block, order, count):
    for step in order[:-1]:
        block = jnp.concatenate([block, swap(block, step, count)], axis=0)
    return block, swap(block, order[-1], count)


def scatter_blocks(keep, send, steps, count):
    for step in steps[:-1]:
        got = swap(send, step, count)
        half = keep.shape[0] // 2
        total = keep.astype(f32) + got.astype(f32)
        send = total[half:].astype(bf16)
        keep = total[:half].astype(bf16)
    return keep, swap(send, steps[-1], count)


def fast_layout(dp, fsdp):
    return dp == 4 and fsdp == 8


def body(dp, fsdp, tokens, lengths, assignment, weights, vectors, cotangent):
    count = dp * fsdp
    owner = lax.axis_index(AXES).astype(jnp.int32)
    owned = assignment == owner
    ends = jnp.cumsum(jnp.where(owned, lengths, 0), dtype=jnp.int32)
    ends = jnp.where(owned, ends, 1 << 30)[None, :]
    if fast_layout(dp, fsdp):
        vec_width = vectors.shape[0]
        core, x_step, y_step, z_near, z_far = fsdp, 1, 2 * fsdp, 2, 4
        gather_order = [z_far, z_near, y_step, x_step, core]
        scatter_steps = [core, x_step, y_step, z_near, z_far]
        scatter_order = scatter_steps[::-1]
        me = owner[None]
        placed = lax.dynamic_update_slice(jnp.zeros((16 * 128,), bf16), vectors, ((owner * vec_width) % 128,))
        q_block, r_block = pack(weights.reshape(512, 128), placed.reshape(16, 128))
        q_first, q_second = gather_blocks(q_block, gather_order, count)
        r_first, r_second = gather_blocks(r_block, gather_order, count)
    else:
        vec_width = 160
        gather_order = scatter_order = [1, 2, 4, 8, 16]
        me = jnp.zeros((1,), jnp.int32)
        blocks = lax.all_gather(weights, AXES, axis=0, tiled=True).reshape(count, -1)
        flat = lax.all_gather(vectors, AXES, axis=0, tiled=True).reshape(40, 128)
        square = 512 * 512 // count
        cuts = [0, 3 * square, 4 * square, 6 * square, 8 * square]
        panels = []
        for index, (start, rows, width) in enumerate(PANELS):
            piece = blocks[:, cuts[index] : cuts[index + 1]].reshape(BLOCKS, rows, width, 128)
            panels.append(piece.transpose(0, 2, 1, 3).reshape(BLOCKS, rows * width, 128))
        spots = [(d * vec_width) // 128 for d in range(BLOCKS)]
        lanes = jnp.arange(256)
        vec_blocks = []
        for d in range(BLOCKS):
            pair = jnp.concatenate([flat, jnp.zeros((8, 128), bf16)], axis=0)[spots[d] : spots[d] + 2].reshape(256)
            offset = d * vec_width - 128 * spots[d]
            pair = jnp.where((lanes >= offset) & (lanes < offset + vec_width), pair, 0)
            vec_blocks.append(jnp.concatenate([pair.reshape(2, 128), jnp.zeros((14, 128), bf16)], axis=0))
        q_all = jnp.concatenate([panels[0], jnp.stack(vec_blocks)], axis=1)
        r_all = jnp.concatenate(panels[1:], axis=1)
        half = BLOCKS // 2
        q_first, q_second = q_all[:half].reshape(-1, 128), q_all[half:].reshape(-1, 128)
        r_first, r_second = r_all[:half].reshape(-1, 128), r_all[half:].reshape(-1, 128)
    qkv, keys_extra, query_extra, vec = project(
        me, ends, tokens, q_first, q_second, gather_order, vec_width, vectors.shape[0] * count
    )
    attended, query_extra = attend(qkv, query_extra, keys_extra)
    layer_output, grad_first, grad_attended, grad_extra, r_keep, r_send, vec_grad = middle(
        me, tokens, attended, cotangent, vec, r_first, r_second, gather_order, scatter_order
    )
    grad_query, grad_keys, grad_values = attend_back(qkv, grad_attended, query_extra, keys_extra, grad_extra)
    q_keep, q_send = weight_grad(me, tokens, grad_query, grad_keys, grad_values, vec_grad, scatter_order, vec_width)
    grad_tokens = input_grad(
        me, grad_first, grad_query, grad_keys, grad_values, q_first, q_second, gather_order
    )
    if fast_layout(dp, fsdp):
        r_keep, r_got = scatter_blocks(r_keep, r_send, scatter_steps, count)
        q_keep, q_got = scatter_blocks(q_keep, q_send, scatter_steps, count)
        own_weights, own_vec = unpack(q_keep, q_got, r_keep, r_got)
        own_weights = own_weights.reshape(-1)
        own_vectors = lax.dynamic_slice(own_vec.reshape(-1), ((owner * vec_width) % 128,), (vec_width,))
    else:
        q_all = jnp.concatenate([q_keep, q_send], axis=0).astype(f32).reshape(BLOCKS, Q_ROWS, 128)
        r_all = jnp.concatenate([r_keep, r_send], axis=0).astype(f32).reshape(BLOCKS, R_ROWS, 128)
        sources = (q_all[:, : 4 * QKV_ROWS], r_all[:, :64], r_all[:, 64:192], r_all[:, 192:])
        pieces = []
        for source, (start, rows, width) in zip(sources, PANELS):
            piece = source.reshape(BLOCKS, width, rows, 128).transpose(0, 2, 1, 3)
            pieces.append(piece.reshape(count, -1))
        own_weights = lax.psum_scatter(
            jnp.concatenate(pieces, axis=1).reshape(-1), AXES, scatter_dimension=0, tiled=True
        )
        pairs = q_all[:, 4 * QKV_ROWS : 4 * QKV_ROWS + 2].reshape(BLOCKS, 256)
        rows = [
            pairs[d, (d * vec_width) % 128 : (d * vec_width) % 128 + vec_width] for d in range(BLOCKS)
        ]
        own_vectors = lax.psum_scatter(jnp.concatenate(rows), AXES, scatter_dimension=0, tiled=True)
    return (layer_output, grad_tokens, own_weights, own_vectors)


def solution(mesh):
    dp, fsdp = mesh.shape["dp"], mesh.shape["fsdp"]
    in_specs = (
        P(AXES, None),
        P(),
        P(),
        P(AXES),
        P(AXES),
        P(AXES, None),
    )
    out_specs = (
        P(AXES, None),
        P(AXES, None),
        P(AXES),
        P(AXES),
    )
    return jax.shard_map(
        functools.partial(body, dp, fsdp), mesh=mesh, in_specs=in_specs, out_specs=out_specs, check_vma=False
    )
```

time: 690 us -> 234 us (0.34); the launches traced: 680 us -> 233 us
  matrix products: 267 us -> 0 us
  Pallas kernels: 0 us -> 126 us
  other arithmetic: 102 us -> 6.03 us
  blocking collectives: 83 us -> 0 us
  local copies, waits for them, and re-layouts: 84.1 us -> 7.94 us
  waiting for transfers between devices: 129 us -> 63.2 us
  starting transfers between devices: 0.08 us -> 29 us
  between operations: 15.1 us -> 0.94 us
    dot_general x38 -> x0, matrix products: 267 us -> none  [the longest x4 51.6 us: attention_backward(): jnp.einsum('qhd,khd->hqk', grad_block, values, preferred_element_type=jnp...]
    pallas_call x0 -> x8, Pallas kernels: none -> 126 us  [the longest x1 44 us: attend_back(): pl.pallas_call(attend_back_kernel, grid=(HEADS, count // width), in_specs...]
    unnamed x3 -> x0, waiting for transfers between devices: 117 us -> none
    unnamed x2 -> x0, blocking collectives: 83 us -> none
    ppermute x0 -> x20, waiting for transfers between devices: none -> 63.2 us  [swap(): return lax.ppermute(array, AXES, [(i, i ^ step) for i in range(count)])]
    convert_element_type x5 -> x0, other arithmetic: 60.7 us -> none  [the longest x2 58.7 us: attention_backward(): grad_scores = (attn_probs * (grad_probs - centre)).astype(jnp.bfloat16)]
    unnamed x168 -> x32, local copies, waits for them, and re-layouts: 37.3 us -> 4.02 us
    ppermute x0 -> x20, starting transfers between devices: none -> 29 us  [swap(): return lax.ppermute(array, AXES, [(i, i ^ step) for i in range(count)])]
  transfers between devices with their start and end apart: 2 -> 20, of which waited for: 2 -> 13; matrix products, arithmetic and copies ran while one was open for 5% -> 4% of each run, Pallas kernels for 0% -> 17%
where the time goes in v1:
time: 234 us; the launch traced here: 233 us
  Pallas kernels  126 us (54%)
  waiting for transfers between devices  63.2 us (27%)
  starting transfers between devices  29 us (12%)
  local copies, waits for them, and re-layouts  7.94 us (3%)
  other arithmetic  6.03 us (3%)
    ppermute x20, waiting for transfers between devices, swap(): return lax.ppermute(array, AXES, [(i, i ^ step) for i in range(count)])  63.2 us
    pallas_call x1, Pallas kernels, attend_back(): pl.pallas_call(attend_back_kernel, grid=(HEADS, count // width), in_specs...  44 us
    pallas_call x1, Pallas kernels, middle(): pl.pallas_call(functools.partial(middle_kernel, order_in, order_out, sub)...  30.2 us
    ppermute x20, starting transfers between devices, swap(): return lax.ppermute(array, AXES, [(i, i ^ step) for i in range(count)])  29 us
    pallas_call x1, Pallas kernels, attend(): pl.pallas_call(attend_kernel, grid=(HEADS, count // rows), in_specs=[pl.B...  20.3 us
    pallas_call x1, Pallas kernels, weight_grad(): pl.pallas_call(functools.partial(weight_grad_kernel, order, vec_width), i...  9.8 us
    pallas_call x1, Pallas kernels, input_grad(): pl.pallas_call(functools.partial(input_grad_kernel, order), grid=(count /...  9.44 us
    pallas_call x1, Pallas kernels, project(): pl.pallas_call(functools.partial(project_kernel, order, vec_width, vec_co...  9 us
  transfers between devices with their start and end apart: 20, of which 13 were waited for; matrix products, arithmetic and copies ran while one was open for 4% of the time, Pallas kernels for 17%

profile of v1, /device:TPU:0, one launch (start us, length us, event | category | flops | bytes accessed | tf_op | source)
XLA Modules:
  0.0 233.2 jit_solution(9071451372320174781)
XLA Ops:
  0.7 0.9 dynamic_update_slice.3
  1.5 0.6 copy-done.8
  2.1 1.6 pack.1
  3.7 4.0 %collective-permute-start.5 = (bf16[320,128]{1,0:T(8,128)(2,1)}, bf16[320,128]{1,0:T(8,128)(2,1)S(1)}, u32[]{:S(2)}, u32[]{:S(2)}) collective-permute-start(bf16[320,128]{1,0:T(8,128)(2,1)} %get-tuple-element.32), channel_id=1, source_target_pairs={{0,4},{1,5},{2,6},{3,7},{4,0},{5,1},{6,2},{7,3},{8,12},{9,13},{10,... | collective-permute-start | bytes 245768 | tf_op jit(solution)/shard_map/ppermute | solution.py:653
  7.8 5.3 %collective-permute-done.5 = bf16[320,128]{1,0:T(8,128)(2,1)S(1)} collective-permute-done((bf16[320,128]{1,0:T(8,128)(2,1)}, bf16[320,128]{1,0:T(8,128)(2,1)S(1)}, u32[]{:S(2)}, u32[]{:S(2)}) %collective-permute-start.5) | collective-permute-done | bytes 81952 | tf_op jit(solution)/shard_map/ppermute | solution.py:653
  13.2 0.9 pad_maximum_fusion.4
  14.1 1.1 collective-permute-start.6
  15.2 0.8 constant_dynamic-update-slice_fusion.4
  16.0 0.9 constant_dynamic-update-slice_fusion.9
  16.9 2.6 %collective-permute-done.6 = bf16[640,128]{1,0:T(8,128)(2,1)S(1)} collective-permute-done((bf16[640,128]{1,0:T(8,128)(2,1)S(1)}, bf16[640,128]{1,0:T(8,128)(2,1)S(1)}, u32[]{:S(2)}, u32[]{:S(2)}) %collective-permute-start.6) | collective-permute-done | bytes 163872 | tf_op jit(solution)/shard_map/ppermute | solution.py:653
  19.5 0.9 pad_maximum_fusion.2
  20.4 1.9 collective-permute-start.7
  22.3 0.8 pad_maximum_fusion.5
  23.1 1.4 collective-permute-start.1
  24.5 3.3 %collective-permute-done.1 = bf16[416,128]{1,0:T(8,128)(2,1)S(1)} collective-permute-done((bf16[416,128]{1,0:T(8,128)(2,1)S(1)}, bf16[416,128]{1,0:T(8,128)(2,1)S(1)}, u32[]{:S(2)}, u32[]{:S(2)}) %collective-permute-start.1) | collective-permute-done | bytes 106528 | tf_op jit(solution)/shard_map/ppermute | solution.py:653
  28.1 0.8 collective-permute-done.7
  28.9 1.6 collective-permute-start.8
  30.5 3.2 %collective-permute-done.2 = bf16[832,128]{1,0:T(8,128)(2,1)S(1)} collective-permute-done((bf16[832,128]{1,0:T(8,128)(2,1)S(1)}, bf16[832,128]{1,0:T(8,128)(2,1)S(1)}, u32[]{:S(2)}, u32[]{:S(2)}) %collective-permute-start.2) | collective-permute-done | bytes 213024 | tf_op jit(solution)/shard_map/ppermute | solution.py:653
  33.8 1.6 collective-permute-start.3
  35.4 11.3 %collective-permute-done.8 = bf16[2560,128]{1,0:T(8,128)(2,1)S(1)} collective-permute-done((bf16[2560,128]{1,0:T(8,128)(2,1)S(1)}, bf16[2560,128]{1,0:T(8,128)(2,1)S(1)}, u32[]{:S(2)}, u32[]{:S(2)}) %collective-permute-start.8) | collective-permute-done | bytes 655392 | tf_op jit(solution)/shard_map/ppermute | solution.py:653
  46.9 4.8 %collective-permute-done.3 = bf16[1664,128]{1,0:T(8,128)(2,1)S(1)} collective-permute-done((bf16[1664,128]{1,0:T(8,128)(2,1)S(1)}, bf16[1664,128]{1,0:T(8,128)(2,1)S(1)}, u32[]{:S(2)}, u32[]{:S(2)}) %collective-permute-start.3) | collective-permute-done | bytes 426016 | tf_op jit(solution)/shard_map/ppermute | solution.py:653
  52.4 0.6 bitcast_select_fusion
  53.0 1.2 collective-permute-done.4.second
  54.2 0.9 copy-done.1
  55.1 9.0 %project.1 = (bf16[2048,1536]{1,0:T(8,128)(2,1)}, bf16[2048,128]{1,0:T(8,128)(2,1)}, bf16[4,2048,128]{2,1,0:T(8,128)(2,1)}, f32[48,128]{1,0:T(8,128)}) custom-call(s32[1]{0:T(128)} %bitcast.me_ref, s32[1,256]{1,0:T(1,128)} %bitcast.12, bf16[2048,512]{1,0:T(8,128)(2,1)} %tokens.5, bf16[3328,128]{1,0:T(8,128)(2,1)} %copy-done, bf16[3328,128]{1,0:T(8,128)(2,1)} %copy-done.1), custom_call_target="tpu_custom_call" | custom-call | tf_op jit(solution)/shard_map/project/pallas_call | solution.py:146
  64.1 20.3 %attend.1 = (bf16[2048,512]{1,0:T(8,128)(2,1)}, bf16[4,2048,128]{2,1,0:T(8,128)(2,1)}) custom-call(bf16[2048,1536]{1,0:T(8,128)(2,1)} %get-tuple-element.27.q.k.v, bf16[2048,1536]{1,0:T(8,128)(2,1)} %get-tuple-element.27.q.k.v, bf16[2048,1536]{1,0:T(8,128)(2,1)} %get-tuple-element.27.q.k.v, bf16[4,2048,128]{2,1,0:T(8,128)(2,1)} %get-tuple-element.28.query_extra, ...), custom_call_target="tpu_custom_call" | custom-call | tf_op jit(solution)/shard_map/attend/pallas_call | solution.py:207
  84.4 30.2 %middle.1 = (bf16[2048,512]{1,0:T(8,128)(2,1)}, f32[2048,512]{1,0:T(8,128)}, bf16[2048,512]{1,0:T(8,128)(2,1)}, bf16[4,2048,128]{2,1,0:T(8,128)(2,1)}, bf16[5120...) custom-call(s32[1]{0:T(128)} %bitcast.me_ref, bf16[2048,512]{1,0:T(8,128)(2,1)} %tokens.5, ...), custom_call_target="tpu_custom_call" | custom-call | tf_op jit(solution)/shard_map/middle/pallas_call | solution.py:428
  114.7 44.0 %attend_back.1 = (bf16[2048,512]{1,0:T(8,128)(2,1)}, bf16[512,2048]{1,0:T(8,128)(2,1)}, bf16[512,2048]{1,0:T(8,128)(2,1)}) custom-call(bf16[2048,1536]{1,0:T(8,128)(2,1)} %get-tuple-element.27.q.k.v, bf16[2048,1536]{1,0:T(8,128)(2,1)} %get-tuple-element.27.q.k.v, bf16[2048,1536]{1,0:T(8,128)(2,1)} %get-tuple-element.27.q.k.v, ...), custom_call_target="tpu_custom_call" | custom-call | tf_op jit(solution)/shard_map/attend_back/pallas_call | solution.py:510
  158.7 9.8 %weight_grad.1 = (bf16[3328,128]{1,0:T(8,128)(2,1)}, bf16[3328,128]{1,0:T(8,128)(2,1)}) custom-call(s32[1]{0:T(128)} %bitcast.me_ref, bf16[2048,512]{1,0:T(8,128)(2,1)} %tokens.5, bf16[2048,512]{1,0:T(8,128)(2,1)} %get-tuple-element.38.grad_query, bf16[512,2048]{1,0:T(8,128)(2,1)} %get-tuple-element.39.grad_keys, ...), custom_call_target="tpu_custom_call" | custom-call | tf_op jit(solution)/shard_map/weight_grad/pallas_call | solution.py:578
  169.0 2.1 collective-permute-done.10
  171.1 1.5 add_convert_fusion.1
  172.6 1.3 collective-permute-start.11
  174.3 0.8 collective-permute-start.16
  175.1 10.2 %collective-permute-done.11 = bf16[1664,128]{1,0:T(8,128)(2,1)S(1)} collective-permute-done((bf16[1664,128]{1,0:T(8,128)(2,1)S(1)}, bf16[1664,128]{1,0:T(8,128)(2,1)S(1)}, u32[]{:S(2)}, u32[]{:S(2)}) %collective-permute-start.11) | collective-permute-done | bytes 426016 | tf_op jit(solution)/shard_map/ppermute | solution.py:653
  185.4 1.9 collective-permute-start.12
  187.3 11.2 %collective-permute-done.16 = bf16[2560,128]{1,0:T(8,128)(2,1)S(1)} collective-permute-done((bf16[2560,128]{1,0:T(8,128)(2,1)S(1)}, bf16[2560,128]{1,0:T(8,128)(2,1)S(1)}, u32[]{:S(2)}, u32[]{:S(2)}) %collective-permute-start.16) | collective-permute-done | bytes 655392 | tf_op jit(solution)/shard_map/ppermute | solution.py:653
  198.8 1.9 collective-permute-start.17
  200.7 3.0 %collective-permute-start.13 = (bf16[416,128]{1,0:T(8,128)(2,1)S(1)}, bf16[416,128]{1,0:T(8,128)(2,1)S(1)}, u32[]{:S(2)}, u32[]{:S(2)}) collective-permute-start(bf16[416,128]{1,0:T(8,128)(2,1)S(1)} %slice.94), channel_id=1, source_target_pairs={{0,2},{1,3},{2,0},{3,1},{4,6},{5,7},{6,4},{7,5},{8,10},{9,11},{10,... | collective-permute-start | bytes 319496 | tf_op jit(solution)/shard_map/ppermute | solution.py:653
  203.7 4.1 %collective-permute-done.17 = bf16[1280,128]{1,0:T(8,128)(2,1)S(1)} collective-permute-done((bf16[1280,128]{1,0:T(8,128)(2,1)S(1)}, bf16[1280,128]{1,0:T(8,128)(2,1)S(1)}, u32[]{:S(2)}, u32[]{:S(2)}) %collective-permute-start.17) | collective-permute-done | bytes 327712 | tf_op jit(solution)/shard_map/ppermute | solution.py:653
  207.9 3.6 %collective-permute-start.18 = (bf16[640,128]{1,0:T(8,128)(2,1)S(1)}, bf16[640,128]{1,0:T(8,128)(2,1)S(1)}, u32[]{:S(2)}, u32[]{:S(2)}) collective-permute-start(bf16[640,128]{1,0:T(8,128)(2,1)S(1)} %slice.102), channel_id=1, source_target_pairs={{0,2},{1,3},{2,0},{3,1},{4,6},{5,7},{6,4},{7,5},{8,10},{9,11},{10,... | collective-permute-start | bytes 491528 | tf_op jit(solution)/shard_map/ppermute | solution.py:653
  211.5 3.3 %collective-permute-done.18 = bf16[640,128]{1,0:T(8,128)(2,1)S(1)} collective-permute-done((bf16[640,128]{1,0:T(8,128)(2,1)S(1)}, bf16[640,128]{1,0:T(8,128)(2,1)S(1)}, u32[]{:S(2)}, u32[]{:S(2)}) %collective-permute-start.18) | collective-permute-done | bytes 163872 | tf_op jit(solution)/shard_map/ppermute | solution.py:653
  214.8 0.7 fusion
  215.5 3.9 %collective-permute-start.19 = (bf16[320,128]{1,0:T(8,128)(2,1)S(1)}, bf16[320,128]{1,0:T(8,128)(2,1)S(1)}, u32[]{:S(2)}, u32[]{:S(2)}) collective-permute-start(bf16[320,128]{1,0:T(8,128)(2,1)S(1)} %get-tuple-element.48), channel_id=1, source_target_pairs={{0,4},{1,5},{2,6},{3,7},{4,0},{5,1},{6,2},{7,3},{8,12},{9,13},{10,... | collective-permute-start | bytes 245768 | tf_op jit(solution)/shard_map/ppermute | solution.py:653
  219.4 0.6 fusion.1
  220.0 9.4 %input_grad.1 = f32[2048,512]{1,0:T(8,128)} custom-call(s32[1]{0:T(128)} %bitcast.me_ref, f32[2048,512]{1,0:T(8,128)} %get-tuple-element.34.grad_first, bf16[2048,512]{1,0:T(8,128)(2,1)} %get-tuple-element.38.grad_query, bf16[512,2048]{1,0:T(8,128)(2,1)} %get-tuple-element.39.grad_keys, bf16[512,2048]{1,0:T(8,128)(2,1)} %get-tuple-element.40.grad_values, ...), custom_call_target="tpu_custom_call" | custom-call | tf_op jit(solution)/shard_map/input_grad/pallas_call | solution.py:618
  229.5 0.6 copy-done.7
  230.1 1.7 unpack.1
  231.9 1.3 dynamic_slice.3
  (65 shorter events, 3.0 us)
Async XLA Ops:
  1.5 0.6 copy-start.8
  3.7 24.1 %copy-start.5 = (bf16[208,128]{1,0:T(8,128)(2,1)S(1)}, bf16[208,128]{1,0:T(8,128)(2,1)}, u32[]{:S(2)}) copy-start(bf16[208,128]{1,0:T(8,128)(2,1)} %get-tuple-element.26) | copy-start | bytes 159748
  3.7 25.2 %copy-start.3 = (bf16[320,128]{1,0:T(8,128)(2,1)S(1)}, bf16[320,128]{1,0:T(8,128)(2,1)}, u32[]{:S(2)}) copy-start(bf16[320,128]{1,0:T(8,128)(2,1)} %get-tuple-element.32) | copy-start | bytes 245764
  3.7 9.4 %collective-permute-start.5 = (bf16[320,128]{1,0:T(8,128)(2,1)}, bf16[320,128]{1,0:T(8,128)(2,1)S(1)}, u32[]{:S(2)}, u32[]{:S(2)}) collective-permute-start(bf16[320,128]{1,0:T(8,128)(2,1)} %get-tuple-element.32), channel_id=1, source_target_pairs={{0,4},{1,5},{2,6},{3,7},{4,0},{5,1},{6,2},{7,3},{8,12},{9,13},{10,... | collective-permute-start | bytes 245768 | tf_op jit(solution)/shard_map/ppermute | solution.py:653
  7.8 14.6 %collective-permute-start = (bf16[208,128]{1,0:T(8,128)(2,1)}, bf16[208,128]{1,0:T(8,128)(2,1)S(1)}, u32[]{:S(2)}, u32[]{:S(2)}) collective-permute-start(bf16[208,128]{1,0:T(8,128)(2,1)} %get-tuple-element.26), channel_id=1, source_target_pairs={{0,4},{1,5},{2,6},{3,7},{4,0},{5,1},{6,2},{7,3},{8,12},{9,13},{10,... | collective-permute-start | bytes 159752 | tf_op jit(solution)/shard_map/ppermute | solution.py:653
  14.1 5.4 %collective-permute-start.6 = (bf16[640,128]{1,0:T(8,128)(2,1)S(1)}, bf16[640,128]{1,0:T(8,128)(2,1)S(1)}, u32[]{:S(2)}, u32[]{:S(2)}) collective-permute-start(bf16[640,128]{1,0:T(8,128)(2,1)S(1)} %pad_maximum_fusion.4), channel_id=1, source_target_pairs={{0,2},{1,3},{2,0},{3,1},{4,6},{5,7},{6,4},{7,5},{8,10},{9,11},{10,... | collective-permute-start | bytes 491528 | tf_op jit(solution)/shard_map/ppermute | solution.py:653
  20.4 8.5 %collective-permute-start.7 = (bf16[1280,128]{1,0:T(8,128)(2,1)S(1)}, bf16[1280,128]{1,0:T(8,128)(2,1)S(1)}, u32[]{:S(2)}, u32[]{:S(2)}) collective-permute-start(bf16[1280,128]{1,0:T(8,128)(2,1)S(1)} %pad_maximum_fusion.2), channel_id=1, source_target_pairs={{0,16},{1,17},{2,18},{3,19},{4,20},{5,21},{6,22},{7,23},{8,24},{9,... | collective-permute-start | bytes 983048 | tf_op jit(solution)/shard_map/ppermute | solution.py:653
  23.1 4.7 %collective-permute-start.1 = (bf16[416,128]{1,0:T(8,128)(2,1)S(1)}, bf16[416,128]{1,0:T(8,128)(2,1)S(1)}, u32[]{:S(2)}, u32[]{:S(2)}) collective-permute-start(bf16[416,128]{1,0:T(8,128)(2,1)S(1)} %pad_maximum_fusion.5), channel_id=1, source_target_pairs={{0,2},{1,3},{2,0},{3,1},{4,6},{5,7},{6,4},{7,5},{8,10},{9,11},{10,... | collective-permute-start | bytes 319496 | tf_op jit(solution)/shard_map/ppermute | solution.py:653
  27.8 5.9 %collective-permute-start.2 = (bf16[832,128]{1,0:T(8,128)(2,1)S(1)}, bf16[832,128]{1,0:T(8,128)(2,1)S(1)}, u32[]{:S(2)}, u32[]{:S(2)}) collective-permute-start(bf16[832,128]{1,0:T(8,128)(2,1)S(1)} %pad_maximum_fusion.3), channel_id=1, source_target_pairs={{0,16},{1,17},{2,18},{3,19},{4,20},{5,21},{6,22},{7,23},{8,24},{9,... | collective-permute-start | bytes 638984 | tf_op jit(solution)/shard_map/ppermute | solution.py:653
  28.9 17.7 %collective-permute-start.8 = (bf16[2560,128]{1,0:T(8,128)(2,1)S(1)}, bf16[2560,128]{1,0:T(8,128)(2,1)S(1)}, u32[]{:S(2)}, u32[]{:S(2)}) collective-permute-start(bf16[2560,128]{1,0:T(8,128)(2,1)S(1)} %pad_maximum_fusion), channel_id=1, source_target_pairs={{0,1},{1,0},{2,3},{3,2},{4,5},{5,4},{6,7},{7,6},{8,9},{9,8},{10,11... | collective-permute-start | bytes 1966088 | tf_op jit(solution)/shard_map/ppermute | solution.py:653
  33.8 17.9 %collective-permute-start.3 = (bf16[1664,128]{1,0:T(8,128)(2,1)S(1)}, bf16[1664,128]{1,0:T(8,128)(2,1)S(1)}, u32[]{:S(2)}, u32[]{:S(2)}) collective-permute-start(bf16[1664,128]{1,0:T(8,128)(2,1)S(1)} %pad_maximum_fusion.1), channel_id=1, source_target_pairs={{0,1},{1,0},{2,3},{3,2},{4,5},{5,4},{6,7},{7,6},{8,9},{9,8},{10,11... | collective-permute-start | bytes 1277960 | tf_op jit(solution)/shard_map/ppermute | solution.py:653
  35.4 16.4 %copy-start.9 = (s32[256]{0:T(256)S(1)}, s32[256]{0:T(256)}, u32[]{:S(2)}) copy-start(s32[256]{0:T(256)} %param.8) | copy-start | bytes 3076
  35.4 16.4 %copy-start.10 = (s32[256]{0:T(256)S(1)}, s32[256]{0:T(256)}, u32[]{:S(2)}) copy-start(s32[256]{0:T(256)} %param.7) | copy-start | bytes 3076
  46.8 17.4 %copy-start.2 = (bf16[5120,128]{1,0:T(8,128)(2,1)}, bf16[5120,128]{1,0:T(8,128)(2,1)S(1)}, u32[]{:S(2)}) copy-start(bf16[5120,128]{1,0:T(8,128)(2,1)S(1)} %constant_dynamic-update-slice_fusion.5.first) | copy-start | bytes 3932164
  46.8 37.7 %collective-permute-start.9 = (bf16[5120,128]{1,0:T(8,128)(2,1)S(1)}, bf16[5120,128]{1,0:T(8,128)(2,1)}, u32[]{:S(2)}, u32[]{:S(2)}) collective-permute-start(bf16[5120,128]{1,0:T(8,128)(2,1)S(1)} %constant_dynamic-update-slice_fusion.5.first), channel_id=1, source_target_pairs={{0,8},{1,9},{2,10},{3,11},{4,12},{5,13},{6,14},{7,15},{8,0},{9,1},... | collective-permute-start | bytes 3932168 | tf_op jit(solution)/shard_map/ppermute | solution.py:653
  51.7 2.5 %copy-start = (bf16[3328,128]{1,0:T(8,128)(2,1)}, bf16[3328,128]{1,0:T(8,128)(2,1)S(1)}, u32[]{:S(2)}) copy-start(bf16[3328,128]{1,0:T(8,128)(2,1)S(1)} %constant_dynamic-update-slice_fusion.first) | copy-start | bytes 2555908
  51.7 2.4 %collective-permute-start.4 = (bf16[3328,128]{1,0:T(8,128)(2,1)S(1)}, bf16[3328,128]{1,0:T(8,128)(2,1)S(1)}, u32[]{:S(2)}, u32[]{:S(2)}) collective-permute-start(bf16[3328,128]{1,0:T(8,128)(2,1)S(1)} %constant_dynamic-update-slice_fusion.first), channel_id=1, source_target_pairs={{0,8},{1,9},{2,10},{3,11},{4,12},{5,13},{6,14},{7,15},{8,0},{9,1},... | collective-permute-start | bytes 2555912 | tf_op jit(solution)/shard_map/ppermute | solution.py:653
  54.2 0.9 copy-start.1
  158.7 9.9 %copy-start.11 = (bf16[5120,128]{1,0:T(8,128)(2,1)S(1)}, bf16[5120,128]{1,0:T(8,128)(2,1)}, u32[]{:S(2)}) copy-start(bf16[5120,128]{1,0:T(8,128)(2,1)} %get-tuple-element.45) | copy-start | bytes 3932164
  168.5 2.6 %collective-permute-start.10 = (bf16[3328,128]{1,0:T(8,128)(2,1)}, bf16[3328,128]{1,0:T(8,128)(2,1)S(1)}, u32[]{:S(2)}, u32[]{:S(2)}) collective-permute-start(bf16[3328,128]{1,0:T(8,128)(2,1)} %get-tuple-element.43), channel_id=1, source_target_pairs={{0,8},{1,9},{2,10},{3,11},{4,12},{5,13},{6,14},{7,15},{8,0},{9,1},... | collective-permute-start | bytes 2555912 | tf_op jit(solution)/shard_map/ppermute | solution.py:653
  168.6 5.3 %collective-permute-start.15 = (bf16[5120,128]{1,0:T(8,128)(2,1)S(1)}, bf16[5120,128]{1,0:T(8,128)(2,1)S(1)}, u32[]{:S(2)}, u32[]{:S(2)}) collective-permute-start(bf16[5120,128]{1,0:T(8,128)(2,1)S(1)} %copy-done.11), channel_id=1, source_target_pairs={{0,8},{1,9},{2,10},{3,11},{4,12},{5,13},{6,14},{7,15},{8,0},{9,1},... | collective-permute-start | bytes 3932168 | tf_op jit(solution)/shard_map/ppermute | solution.py:653
  171.1 2.8 %copy-start.4 = (bf16[5120,128]{1,0:T(8,128)(2,1)S(1)}, bf16[5120,128]{1,0:T(8,128)(2,1)}, u32[]{:S(2)}) copy-start(bf16[5120,128]{1,0:T(8,128)(2,1)} %get-tuple-element.44) | copy-start | bytes 3932164
  172.6 12.7 %collective-permute-start.11 = (bf16[1664,128]{1,0:T(8,128)(2,1)S(1)}, bf16[1664,128]{1,0:T(8,128)(2,1)S(1)}, u32[]{:S(2)}, u32[]{:S(2)}) collective-permute-start(bf16[1664,128]{1,0:T(8,128)(2,1)S(1)} %slice.90), channel_id=1, source_target_pairs={{0,1},{1,0},{2,3},{3,2},{4,5},{5,4},{6,7},{7,6},{8,9},{9,8},{10,11... | collective-permute-start | bytes 1277960 | tf_op jit(solution)/shard_map/ppermute | solution.py:653
  174.3 24.2 %collective-permute-start.16 = (bf16[2560,128]{1,0:T(8,128)(2,1)S(1)}, bf16[2560,128]{1,0:T(8,128)(2,1)S(1)}, u32[]{:S(2)}, u32[]{:S(2)}) collective-permute-start(bf16[2560,128]{1,0:T(8,128)(2,1)S(1)} %slice.98), channel_id=1, source_target_pairs={{0,1},{1,0},{2,3},{3,2},{4,5},{5,4},{6,7},{7,6},{8,9},{9,8},{10,11... | collective-permute-start | bytes 1966088 | tf_op jit(solution)/shard_map/ppermute | solution.py:653
  185.4 15.2 %collective-permute-start.12 = (bf16[832,128]{1,0:T(8,128)(2,1)S(1)}, bf16[832,128]{1,0:T(8,128)(2,1)S(1)}, u32[]{:S(2)}, u32[]{:S(2)}) collective-permute-start(bf16[832,128]{1,0:T(8,128)(2,1)S(1)} %slice.92), channel_id=1, source_target_pairs={{0,16},{1,17},{2,18},{3,19},{4,20},{5,21},{6,22},{7,23},{8,24},{9,... | collective-permute-start | bytes 638984 | tf_op jit(solution)/shard_map/ppermute | solution.py:653
  198.8 9.1 %collective-permute-start.17 = (bf16[1280,128]{1,0:T(8,128)(2,1)S(1)}, bf16[1280,128]{1,0:T(8,128)(2,1)S(1)}, u32[]{:S(2)}, u32[]{:S(2)}) collective-permute-start(bf16[1280,128]{1,0:T(8,128)(2,1)S(1)} %slice.100), channel_id=1, source_target_pairs={{0,16},{1,17},{2,18},{3,19},{4,20},{5,21},{6,22},{7,23},{8,24},{9,... | collective-permute-start | bytes 983048 | tf_op jit(solution)/shard_map/ppermute | solution.py:653
  200.7 10.8 %collective-permute-start.13 = (bf16[416,128]{1,0:T(8,128)(2,1)S(1)}, bf16[416,128]{1,0:T(8,128)(2,1)S(1)}, u32[]{:S(2)}, u32[]{:S(2)}) collective-permute-start(bf16[416,128]{1,0:T(8,128)(2,1)S(1)} %slice.94), channel_id=1, source_target_pairs={{0,2},{1,3},{2,0},{3,1},{4,6},{5,7},{6,4},{7,5},{8,10},{9,11},{10,... | collective-permute-start | bytes 319496 | tf_op jit(solution)/shard_map/ppermute | solution.py:653
  207.9 6.9 %collective-permute-start.18 = (bf16[640,128]{1,0:T(8,128)(2,1)S(1)}, bf16[640,128]{1,0:T(8,128)(2,1)S(1)}, u32[]{:S(2)}, u32[]{:S(2)}) collective-permute-start(bf16[640,128]{1,0:T(8,128)(2,1)S(1)} %slice.102), channel_id=1, source_target_pairs={{0,2},{1,3},{2,0},{3,1},{4,6},{5,7},{6,4},{7,5},{8,10},{9,11},{10,... | collective-permute-start | bytes 491528 | tf_op jit(solution)/shard_map/ppermute | solution.py:653
  215.5 14.0 %collective-permute-start.19 = (bf16[320,128]{1,0:T(8,128)(2,1)S(1)}, bf16[320,128]{1,0:T(8,128)(2,1)S(1)}, u32[]{:S(2)}, u32[]{:S(2)}) collective-permute-start(bf16[320,128]{1,0:T(8,128)(2,1)S(1)} %get-tuple-element.48), channel_id=1, source_target_pairs={{0,4},{1,5},{2,6},{3,7},{4,0},{5,1},{6,2},{7,3},{8,12},{9,13},{10,... | collective-permute-start | bytes 245768 | tf_op jit(solution)/shard_map/ppermute | solution.py:653
  220.0 9.4 %collective-permute-start.14 = (bf16[208,128]{1,0:T(8,128)(2,1)S(1)}, bf16[208,128]{1,0:T(8,128)(2,1)S(1)}, u32[]{:S(2)}, u32[]{:S(2)}) collective-permute-start(bf16[208,128]{1,0:T(8,128)(2,1)S(1)} %get-tuple-element.50), channel_id=1, source_target_pairs={{0,4},{1,5},{2,6},{3,7},{4,0},{5,1},{6,2},{7,3},{8,12},{9,13},{10,... | collective-permute-start | bytes 159752 | tf_op jit(solution)/shard_map/ppermute | solution.py:653
  229.5 0.6 copy-start.7
  229.5 0.6 copy-start.6

commit v2 on v1

--- a/solution.py
+++ b/solution.py
@@ -35,6 +35,10 @@
     return pltpu.CompilerParams(vmem_limit_bytes=VMEM_BYTES)
 
 
+def cost(flops, moved, special=0):
+    return pl.CostEstimate(flops=int(flops), bytes_accessed=int(moved), transcendentals=int(special))
+
+
 def whole(shape):
     return pl.BlockSpec(shape, lambda *_: (0,) * len(shape))
 
@@ -61,61 +65,53 @@
 PANELS = ((0, 48, 4), (192, 16, 4), (256, 16, 8), (384, 32, 4))
 
 
-def pack_kernel(flat, vec, q_out, r_out, wide):
+def pack_kernel(vec_width, me_ref, flat, vec, q_out, r_out, wide):
     wide[...] = flat[...].astype(f32)
+    shifted = pltpu.roll(vec[...].astype(f32), (me_ref[0] * vec_width) % 128, 1)
     parts = []
     for start, rows, count in PANELS:
         for j in range(count):
             parts.append(wide[pl.ds(start + j, rows, stride=count), :].astype(bf16))
     q_out[0:192, :] = jnp.concatenate(parts[:4], axis=0)
-    q_out[192:208, :] = vec[...]
+    placed = jnp.concatenate([shifted[0:1, 0:128], shifted[0:1, 128:256], jnp.zeros((14, 128), f32)], axis=0)
+    q_out[192:208, :] = placed.astype(bf16)
     r_out[...] = jnp.concatenate(parts[4:], axis=0)
 
 
-def pack(flat, vec):
+def pack(me, flat, vec, vec_width):
+    vmem = pl.BlockSpec(memory_space=pltpu.VMEM)
     return pl.pallas_call(
-        pack_kernel,
+        functools.partial(pack_kernel, vec_width),
+        in_specs=[scalar_spec(), vmem, vmem],
         out_shape=[
             jax.ShapeDtypeStruct((Q_ROWS, 128), bf16),
             jax.ShapeDtypeStruct((R_ROWS, 128), bf16),
         ],
         scratch_shapes=[pltpu.VMEM((512, 128), f32)],
         name="pack",
-    )(flat, vec)
-
-
-def project_kernel(
-    order, vec_width, vec_count, me_ref, ends, tokens, first, second, qkv, keys_extra, query_extra, vec_out, weight, vec
-):
+    )(me, flat, vec)
+
+
+def project_kernel(masks, order, vec_width, me_ref, ends, tokens, *refs):
+    pieces = refs[: len(masks)]
+    qkv, keys_extra, query_extra, vec_out, weight, vec = refs[len(masks) :]
     step = pl.program_id(0)
     rows = tokens.shape[0]
     me = me_ref[0]
 
     @pl.when(step == 0)
     def _():
-        half = BLOCKS // 2
-        for base, ref in ((0, first), (half, second)):
-
-            def place(i, _, base=base, ref=ref):
-                d = owner_of(base + i, me, order)
+        vec[...] = jnp.zeros_like(vec)
+        for mask, ref in zip(masks, pieces):
+            for i in range(1 << len(order)):
+                d = owner_of(i, jnp.bitwise_xor(me, mask), order)
+                row = pl.multiple_of(d * QKV_ROWS, 16)
                 for j in range(4):
-                    weight[pl.ds(pl.multiple_of(d * QKV_ROWS, 16), QKV_ROWS), 128 * j : 128 * (j + 1)] = ref[
-                        pl.ds(pl.multiple_of(i * Q_ROWS + QKV_ROWS * j, 16), QKV_ROWS), :
-                    ]
-                return 0
-
-            lax.fori_loop(0, half, place, 0)
-        vec[...] = jnp.zeros_like(vec)
-        for base, ref in ((0, first), (half, second)):
-
-            def add(i, _, base=base, ref=ref):
-                d = owner_of(base + i, me, order)
+                    at = i * Q_ROWS + QKV_ROWS * j
+                    weight[pl.ds(row, QKV_ROWS), 128 * j : 128 * (j + 1)] = ref[at : at + QKV_ROWS, :]
                 row = (d * vec_width) // 128
-                piece = ref[pl.ds(pl.multiple_of(i * Q_ROWS + 4 * QKV_ROWS, 16), 16), :].astype(f32)
-                vec[pl.ds(row, 2), :] = vec[pl.ds(row, 2), :] + piece[0:2, :]
-                return 0
-
-            lax.fori_loop(0, half, add, 0)
+                at = i * Q_ROWS + 4 * QKV_ROWS
+                vec[pl.ds(row, 2), :] = vec[pl.ds(row, 2), :] + ref[at : at + 16, :].astype(f32)[0:2, :]
         vec_out[...] = vec[...]
 
     x = tokens[...]
@@ -140,38 +136,41 @@
         query_extra[h] = jnp.where(lane == 8, -own, apart).astype(bf16)
 
 
-def project(me, ends, tokens, first, second, order, vec_width, vec_count, rows=512):
+def project(me, ends, tokens, pieces, masks, order, vec_width, rows=512):
     count = tokens.shape[0]
     sets = ends.shape[1]
     return pl.pallas_call(
-        functools.partial(project_kernel, order, vec_width, vec_count),
+        functools.partial(project_kernel, masks, order, vec_width),
         grid=(count // rows,),
         in_specs=[
             scalar_spec(),
             whole((1, sets)),
             pl.BlockSpec((rows, 512), lambda i: (i, 0)),
-            whole(first.shape),
-            whole(second.shape),
-        ],
+        ]
+        + [whole(piece.shape) for piece in pieces],
         out_specs=[
             pl.BlockSpec((rows, 1536), lambda i: (i, 0)),
             pl.BlockSpec((rows, 128), lambda i: (i, 0)),
             pl.BlockSpec((HEADS, rows, 128), lambda i: (0, i, 0)),
             whole((48, 128)),
+            whole((1536, 512)),
         ],
         out_shape=[
             jax.ShapeDtypeStruct((count, 1536), bf16),
             jax.ShapeDtypeStruct((count, 128), bf16),
             jax.ShapeDtypeStruct((HEADS, count, 128), bf16),
             jax.ShapeDtypeStruct((48, 128), f32),
-        ],
-        scratch_shapes=[pltpu.VMEM((1536, 512), bf16), pltpu.VMEM((48, 128), f32)],
+            jax.ShapeDtypeStruct((1536, 512), bf16),
+        ],
+        scratch_shapes=[pltpu.VMEM((48, 128), f32)],
         compiler_params=params(),
+        cost_estimate=cost(2 * count * 512 * 1536, 12e6),
         name="project",
-    )(me, ends, tokens, first, second)
-
-
-def attend_kernel(q, k, v, query_extra, keys_extra, attended, query_extra_out, total, mixed, peak):
+    )(me, ends, tokens, *pieces)
+
+
+def attend_kernel(q, k, v, query_extra, keys_extra, *refs):
+    attended, query_extra_out, total, mixed, peak = refs[-5:]
     rows = q.shape[0]
     left = jnp.concatenate([k[...], keys_extra[...]], axis=1)
     right = jnp.concatenate([q[...], query_extra[0]], axis=1)
@@ -202,30 +201,33 @@
     query_extra_out[0] = extra.astype(bf16)
 
 
-def attend(qkv, query_extra, keys_extra, rows=1024):
+def attend(qkv, query_extra, keys_extra, base, heads, prior, rows=1024):
     count = qkv.shape[0]
     return pl.pallas_call(
         attend_kernel,
-        grid=(HEADS, count // rows),
+        grid=(heads, count // rows),
         in_specs=[
-            pl.BlockSpec((rows, 128), lambda h, i: (i, h)),
-            pl.BlockSpec((count, 128), lambda h, i: (0, HEADS + h)),
-            pl.BlockSpec((count, 128), lambda h, i: (0, 2 * HEADS + h)),
-            pl.BlockSpec((1, rows, 128), lambda h, i: (h, i, 0)),
+            pl.BlockSpec((rows, 128), lambda h, i: (i, base + h)),
+            pl.BlockSpec((count, 128), lambda h, i: (0, HEADS + base + h)),
+            pl.BlockSpec((count, 128), lambda h, i: (0, 2 * HEADS + base + h)),
+            pl.BlockSpec((1, rows, 128), lambda h, i: (base + h, i, 0)),
             pl.BlockSpec((count, 128), lambda h, i: (0, 0)),
-        ],
+        ]
+        + [pl.BlockSpec(memory_space=pl.ANY) for _ in prior],
         out_specs=[
-            pl.BlockSpec((rows, 128), lambda h, i: (i, h)),
-            pl.BlockSpec((1, rows, 128), lambda h, i: (h, i, 0)),
+            pl.BlockSpec((rows, 128), lambda h, i: (i, base + h)),
+            pl.BlockSpec((1, rows, 128), lambda h, i: (base + h, i, 0)),
         ],
         out_shape=[
-            jax.ShapeDtypeStruct((count, 512), bf16),
+            jax.ShapeDtypeStruct((count, 128 * HEADS), bf16),
             jax.ShapeDtypeStruct((HEADS, count, 128), bf16),
         ],
         scratch_shapes=[pltpu.VMEM((1, rows), f32), pltpu.VMEM((128, rows), f32), pltpu.VMEM((1, rows), f32)],
+        input_output_aliases={5: 0, 6: 1} if prior else {},
         compiler_params=params(),
+        cost_estimate=cost(heads * 8 * count * count * 128, 6e6, heads * count * count),
         name="attend",
-    )(qkv, qkv, qkv, query_extra, keys_extra)
+    )(qkv, qkv, qkv, query_extra, keys_extra, *prior)
 
 
 def mean_row(value):
@@ -246,43 +248,20 @@
     return jnp.sum(value.reshape(value.shape[0] // 8, 8, value.shape[1]), axis=0)
 
 
-def middle_kernel(
-    order_in,
-    order_out,
-    sub,
-    me_ref,
-    tokens,
-    attended,
-    cotangent,
-    vec,
-    first,
-    second,
-    layer_output,
-    grad_first_out,
-    grad_attended_out,
-    grad_extra,
-    keep,
-    send,
-    vec_out,
-    attn_weight,
-    in_weight,
-    out_weight,
-    grad_attn,
-    grad_in,
-    grad_out,
-    sums,
-    hidden_sum,
-):
+def middle_kernel(masks, order_in, order_out, sub, me_ref, tokens, attended, cotangent, vec, *refs):
+    pieces = refs[: len(masks)]
+    layer_output, grad_first_out, grad_attended_out, grad_extra, keep, send, vec_out = refs[len(masks) : -8]
+    attn_weight, in_weight, out_weight, grad_attn, grad_in, grad_out, sums, hidden_sum = refs[-8:]
     step = pl.program_id(0)
     me = me_ref[0]
     half = BLOCKS // 2
 
     @pl.when(step == 0)
     def _():
-        for base, ref in ((0, first), (half, second)):
-
-            def place(i, _, base=base, ref=ref):
-                d = owner_of(base + i, me, order_in)
+        for mask, ref in zip(masks, pieces):
+
+            def place(i, _, mask=mask, ref=ref):
+                d = owner_of(i, jnp.bitwise_xor(me, mask), order_in)
                 start = i * R_ROWS
                 a_row = pl.multiple_of(d * 16, 16)
                 o_row = pl.multiple_of(d * 32, 16)
@@ -300,7 +279,7 @@
                     ]
                 return 0
 
-            lax.fori_loop(0, half, place, 0)
+            lax.fori_loop(0, 1 << len(order_in), place, 0)
         grad_attn[...] = jnp.zeros_like(grad_attn)
         grad_in[...] = jnp.zeros_like(grad_in)
         grad_out[...] = jnp.zeros_like(grad_out)
@@ -421,12 +400,14 @@
             vec_out[32 + j : 33 + j, :] = row[:, 128 * j : 128 * (j + 1)]
 
 
-def middle(me, tokens, attended, cotangent, vec, first, second, order_in, order_out, rows=512, sub=256):
+def middle(
+    me, tokens, attended, cotangent, vec, pieces, masks, order_in, order_out, rows=512, sub=256
+):
     count = tokens.shape[0]
     by_row = pl.BlockSpec((rows, 512), lambda i: (i, 0))
     half_rows = BLOCKS // 2 * R_ROWS
     return pl.pallas_call(
-        functools.partial(middle_kernel, order_in, order_out, sub),
+        functools.partial(middle_kernel, masks, order_in, order_out, sub),
         grid=(count // rows,),
         in_specs=[
             scalar_spec(),
@@ -434,9 +415,8 @@
             by_row,
             by_row,
             whole((48, 128)),
-            whole(first.shape),
-            whole(second.shape),
-        ],
+        ]
+        + [whole(piece.shape) for piece in pieces],
         out_specs=[
             by_row,
             by_row,
@@ -466,15 +446,51 @@
             pltpu.VMEM((8, FF), f32),
         ],
         compiler_params=params(),
+        cost_estimate=cost(6 * count * 1310720, 22e6, 3 * count * FF),
         name="middle",
-    )(me, tokens, attended, cotangent, vec, first, second)
+    )(me, tokens, attended, cotangent, vec, *pieces)
 
 
 def attend_back_kernel(
-    q, k, v, grad, query_extra, keys_extra, grad_extra, grad_query, grad_keys, grad_values, acc
+    base,
+    heads,
+    order,
+    vec_width,
+    me_ref,
+    tokens,
+    q,
+    k,
+    v,
+    grad,
+    query_extra,
+    keys_extra,
+    grad_extra,
+    vec_in,
+    grad_query,
+    grad_keys,
+    grad_values,
+    keep,
+    send,
+    vec,
+    acc,
+    keys_t,
+    values_t,
+    grad_weight,
+    held,
+    sem,
 ):
+    local = pl.program_id(0)
     step = pl.program_id(1)
+    steps = pl.num_programs(1)
     width = k.shape[0]
+    last = base + heads == HEADS
+    copy = pltpu.make_async_copy(tokens, held, sem)
+
+    @pl.when((local == 0) & (step == 0))
+    def _():
+        copy.start()
+        vec[...] = vec_in[...]
+
     lane = lax.broadcasted_iota(jnp.int32, (width, 128), 1)
     ones = jnp.where(lane < 3, 1.0, 0.0).astype(bf16)
     scores = dot(
@@ -488,8 +504,10 @@
     probs = jnp.exp(scores)
     probs_low = probs.astype(bf16)
     grad_scores = (probs * centred).astype(bf16)
-    grad_values[...] = dot(grad[...], probs_low, TN).astype(bf16)
-    grad_keys[...] = dot(q[...], grad_scores, TN).astype(bf16)
+    keys_t[step] = dot(q[...], grad_scores, TN).astype(bf16)
+    values_t[step] = dot(grad[...], probs_low, TN).astype(bf16)
+    grad_keys[...] = keys_t[step]
+    grad_values[...] = values_t[step]
     part = dot(grad_scores, k[...], NN)
 
     @pl.when(step == 0)
@@ -500,136 +518,127 @@
     def _():
         acc[...] += part
 
-    @pl.when(step == pl.num_programs(1) - 1)
+    @pl.when((local == 0) & (step == steps - 1))
     def _():
-        grad_query[...] = acc[...].astype(bf16)
-
-
-def attend_back(qkv, grad_attended, query_extra, keys_extra, grad_extra, width=512):
+        copy.wait()
+
+    @pl.when(step == steps - 1)
+    def _():
+        me = me_ref[0]
+        scale = 1.0 / math.sqrt(HEAD_DIM)
+        x = held[...]
+        gq = acc[...].astype(bf16)
+        grad_query[...] = gq
+        gk = jnp.concatenate([keys_t[i] for i in range(keys_t.shape[0])], axis=1)
+        gv = jnp.concatenate([values_t[i] for i in range(values_t.shape[0])], axis=1)
+        grad_weight[0:512, :] = dot(gq, x, TN).T * scale
+        grad_weight[512:1024, :] = dot(gk, x, NN).T
+        grad_weight[1024:1536, :] = dot(gv, x, NN).T
+        row_ones = jnp.ones((8, x.shape[0]), bf16)
+        vec[pl.ds(base + local, 1), :] = dot(row_ones, gq, NN)[0:1] * scale
+        vec[pl.ds(4 + base + local, 1), :] = dot(row_ones, gv, NT)[0:1]
+        half = BLOCKS // 2
+        block = heads * QKV_ROWS + (16 if last else 0)
+        for start, ref in ((0, keep), (half, send)):
+
+            def place(i, _, start=start, ref=ref):
+                d = owner_of(start + i, me, order)
+                ref[pl.ds(pl.multiple_of(i * block + local * QKV_ROWS, 16), QKV_ROWS), :] = grad_weight[
+                    pl.ds(pl.multiple_of(d * QKV_ROWS, 16), QKV_ROWS), :
+                ].astype(bf16)
+                if last:
+                    pair = vec[pl.ds((d * vec_width) // 128, 2), :]
+                    pair = jnp.concatenate([pair, jnp.zeros((14, 128), f32)], axis=0)
+                    ref[pl.ds(pl.multiple_of(i * block + heads * QKV_ROWS, 16), 16), :] = pair.astype(bf16)
+                return 0
+
+            lax.fori_loop(0, half, place, 0)
+
+
+def attend_back(
+    me, tokens, qkv, grad_attended, query_extra, keys_extra, grad_extra, vec, order, vec_width, base, heads, width=512
+):
     count = qkv.shape[0]
+    half_rows = BLOCKS // 2 * (heads * QKV_ROWS + (16 if base + heads == HEADS else 0))
     return pl.pallas_call(
-        attend_back_kernel,
-        grid=(HEADS, count // width),
+        functools.partial(attend_back_kernel, base, heads, order, vec_width),
+        grid=(heads, count // width),
         in_specs=[
-            pl.BlockSpec((count, 128), lambda h, i: (0, h)),
-            pl.BlockSpec((width, 128), lambda h, i: (i, HEADS + h)),
-            pl.BlockSpec((width, 128), lambda h, i: (i, 2 * HEADS + h)),
-            pl.BlockSpec((count, 128), lambda h, i: (0, h)),
-            pl.BlockSpec((1, count, 128), lambda h, i: (h, 0, 0)),
+            scalar_spec(),
+            pl.BlockSpec(memory_space=pl.ANY),
+            pl.BlockSpec((count, 128), lambda h, i: (0, base + h)),
+            pl.BlockSpec((width, 128), lambda h, i: (i, HEADS + base + h)),
+            pl.BlockSpec((width, 128), lambda h, i: (i, 2 * HEADS + base + h)),
+            pl.BlockSpec((count, 128), lambda h, i: (0, base + h)),
+            pl.BlockSpec((1, count, 128), lambda h, i: (base + h, 0, 0)),
             pl.BlockSpec((width, 128), lambda h, i: (i, 0)),
-            pl.BlockSpec((1, count, 128), lambda h, i: (h, 0, 0)),
+            pl.BlockSpec((1, count, 128), lambda h, i: (base + h, 0, 0)),
+            whole((48, 128)),
         ],
         out_specs=[
             pl.BlockSpec((count, 128), lambda h, i: (0, h)),
             pl.BlockSpec((128, width), lambda h, i: (h, i)),
             pl.BlockSpec((128, width), lambda h, i: (h, i)),
+            whole((half_rows, 128)),
+            whole((half_rows, 128)),
+            whole((48, 128)),
         ],
         out_shape=[
-            jax.ShapeDtypeStruct((count, 512), bf16),
-            jax.ShapeDtypeStruct((512, count), bf16),
-            jax.ShapeDtypeStruct((512, count), bf16),
-        ],
-        scratch_shapes=[pltpu.VMEM((count, 128), f32)],
+            jax.ShapeDtypeStruct((count, 128 * heads), bf16),
+            jax.ShapeDtypeStruct((128 * heads, count), bf16),
+            jax.ShapeDtypeStruct((128 * heads, count), bf16),
+            jax.ShapeDtypeStruct((half_rows, 128), bf16),
+            jax.ShapeDtypeStruct((half_rows, 128), bf16),
+            jax.ShapeDtypeStruct((48, 128), f32),
+        ],
+        scratch_shapes=[
+            pltpu.VMEM((count, 128), f32),
+            pltpu.VMEM((count // width, 128, width), bf16),
+            pltpu.VMEM((count // width, 128, width), bf16),
+            pltpu.VMEM((1536, 128), f32),
+            pltpu.VMEM((count, 512), bf16),
+            pltpu.SemaphoreType.DMA,
+        ],
         compiler_params=params(),
+        cost_estimate=cost(heads * 20 * count * count * 128, heads * 6e6, heads * count * count),
         name="attend_back",
-    )(qkv, qkv, qkv, grad_attended, query_extra, keys_extra, grad_extra)
-
-
-def weight_grad_kernel(
-    order, vec_width, me_ref, tokens, grad_query, grad_keys, grad_values, vec_in, keep, send, vec, grad_weight
-):
-    me = me_ref[0]
-    half = BLOCKS // 2
+    )(me, tokens, qkv, qkv, qkv, grad_attended, query_extra, keys_extra, grad_extra, vec)
+
+
+def input_grad_kernel(groups, *refs):
+    grad_first = refs[0]
+    queries, keys, values = [refs[1 + i * groups : 1 + (i + 1) * groups] for i in range(3)]
+    weight, out = refs[-2], refs[-1]
     scale = 1.0 / math.sqrt(HEAD_DIM)
-    x = tokens[...]
-    ones = jnp.ones((8, x.shape[0]), bf16)
-    vec[...] = vec_in[...]
-    for h in range(HEADS):
-        cols = slice(128 * h, 128 * (h + 1))
-        gq = grad_query[:, cols]
-        gk = grad_keys[cols, :]
-        gv = grad_values[cols, :]
-        grad_weight[0:512, cols] = dot(gq, x, TN).T * scale
-        grad_weight[512:1024, cols] = dot(gk, x, NN).T
-        grad_weight[1024:1536, cols] = dot(gv, x, NN).T
-        vec[h : h + 1, :] = dot(ones, gq, NN)[0:1] * scale
-        vec[4 + h : 5 + h, :] = dot(ones, gv, NT)[0:1]
-    for base, ref in ((0, keep), (half, send)):
-
-        def place(i, _, base=base, ref=ref):
-            d = owner_of(base + i, me, order)
-            start = i * Q_ROWS
-            row = pl.multiple_of(d * QKV_ROWS, 16)
-            for j in range(4):
-                ref[pl.ds(pl.multiple_of(start + QKV_ROWS * j, 16), QKV_ROWS), :] = grad_weight[
-                    pl.ds(row, QKV_ROWS), 128 * j : 128 * (j + 1)
-                ].astype(bf16)
-            pair = vec[pl.ds((d * vec_width) // 128, 2), :]
-            pair = jnp.concatenate([pair, jnp.zeros((14, 128), f32)], axis=0)
-            ref[pl.ds(pl.multiple_of(start + 4 * QKV_ROWS, 16), 16), :] = pair.astype(bf16)
-            return 0
-
-        lax.fori_loop(0, half, place, 0)
-
-
-def weight_grad(me, tokens, grad_query, grad_keys, grad_values, vec, order, vec_width):
-    half_rows = BLOCKS // 2 * Q_ROWS
-    vmem = pl.BlockSpec(memory_space=pltpu.VMEM)
-    return pl.pallas_call(
-        functools.partial(weight_grad_kernel, order, vec_width),
-        in_specs=[scalar_spec()] + [vmem] * 5,
-        out_specs=[vmem, vmem],
-        out_shape=[jax.ShapeDtypeStruct((half_rows, 128), bf16)] * 2,
-        scratch_shapes=[pltpu.VMEM((48, 128), f32), pltpu.VMEM((1536, 512), f32)],
-        compiler_params=params(),
-        name="weight_grad",
-    )(me, tokens, grad_query, grad_keys, grad_values, vec)
-
-
-def input_grad_kernel(order, me_ref, grad_first, grad_query, grad_keys, grad_values, first, second, out, weight):
-    step = pl.program_id(0)
-    me = me_ref[0]
-
-    @pl.when(step == 0)
-    def _():
-        half = BLOCKS // 2
-        for base, ref in ((0, first), (half, second)):
-
-            def place(i, _, base=base, ref=ref):
-                d = owner_of(base + i, me, order)
-                for j in range(4):
-                    weight[pl.ds(pl.multiple_of(d * QKV_ROWS, 16), QKV_ROWS), 128 * j : 128 * (j + 1)] = ref[
-                        pl.ds(pl.multiple_of(i * Q_ROWS + QKV_ROWS * j, 16), QKV_ROWS), :
-                    ]
-                return 0
-
-            lax.fori_loop(0, half, place, 0)
-
-    scale = 1.0 / math.sqrt(HEAD_DIM)
-    total = grad_first[...] + scale * dot(grad_query[...], weight[0:512, :], NT)
-    total = total + dot(grad_keys[...], weight[512:1024, :], TT)
-    out[...] = total + dot(grad_values[...], weight[1024:1536, :], TT)
-
-
-def input_grad(me, grad_first, grad_query, grad_keys, grad_values, first, second, order, rows=512):
+    gq = jnp.concatenate([r[...] for r in queries], axis=1)
+    gk = jnp.concatenate([r[...] for r in keys], axis=0)
+    gv = jnp.concatenate([r[...] for r in values], axis=0)
+    total = grad_first[...] + scale * dot(gq, weight[0:512, :], NT)
+    total = total + dot(gk, weight[512:1024, :], TT)
+    out[...] = total + dot(gv, weight[1024:1536, :], TT)
+
+
+def input_grad(grad_first, queries, keys, values, weight, rows=512):
     count = grad_first.shape[0]
     by_row = pl.BlockSpec((rows, 512), lambda i: (i, 0))
-    by_column = pl.BlockSpec((512, rows), lambda i: (0, i))
     return pl.pallas_call(
-        functools.partial(input_grad_kernel, order),
+        functools.partial(input_grad_kernel, len(queries)),
         grid=(count // rows,),
-        in_specs=[scalar_spec(), by_row, by_row, by_column, by_column, whole(first.shape), whole(second.shape)],
+        in_specs=[by_row]
+        + [pl.BlockSpec((rows, a.shape[1]), lambda i: (i, 0)) for a in queries]
+        + [pl.BlockSpec((a.shape[0], rows), lambda i: (0, i)) for a in keys + values]
+        + [whole((1536, 512))],
         out_specs=by_row,
         out_shape=jax.ShapeDtypeStruct((count, 512), f32),
-        scratch_shapes=[pltpu.VMEM((1536, 512), bf16)],
         compiler_params=params(),
+        cost_estimate=cost(2 * count * 512 * 1536, 16e6),
         name="input_grad",
-    )(me, grad_first, grad_query, grad_keys, grad_values, first, second)
-
-
-def unpack_kernel(q_keep, q_got, r_keep, r_got, out, vec_out):
-    q_sum = q_keep[...].astype(f32) + q_got[...].astype(f32)
-    r_sum = r_keep[...].astype(f32) + r_got[...].astype(f32)
+    )(grad_first, *queries, *keys, *values, weight)
+
+
+def unpack_kernel(vec_width, me_ref, q_keep, q_got, r_keep, r_got, out, vec_out):
+    q_sum = q_keep[...] + q_got[...].astype(f32)
+    r_sum = r_keep[...] + r_got[...].astype(f32)
     at = 0
     source = q_sum
     for index, (start, rows, count) in enumerate(PANELS):
@@ -638,61 +647,81 @@
         for j in range(count):
             out[pl.ds(start + j, rows, stride=count), :] = source[at : at + rows, :]
             at += rows
-    vec_out[...] = q_sum[192:200, :]
-
-
-def unpack(q_keep, q_got, r_keep, r_got):
+    pair = jnp.concatenate([q_sum[192:200, :], q_sum[193:201, :]], axis=1)
+    vec_out[...] = pltpu.roll(pair, 256 - (me_ref[0] * vec_width) % 128, 1)
+
+
+def unpack(me, q_keep, q_got, r_keep, r_got, vec_width):
+    vmem = pl.BlockSpec(memory_space=pltpu.VMEM)
     return pl.pallas_call(
-        unpack_kernel,
-        out_shape=[jax.ShapeDtypeStruct((512, 128), f32), jax.ShapeDtypeStruct((8, 128), f32)],
+        functools.partial(unpack_kernel, vec_width),
+        in_specs=[scalar_spec()] + [vmem] * 4,
+        out_shape=[jax.ShapeDtypeStruct((512, 128), f32), jax.ShapeDtypeStruct((8, 256), f32)],
         name="unpack",
-    )(q_keep, q_got, r_keep, r_got)
+    )(me, q_keep, q_got, r_keep, r_got)
 
 
 def swap(array, step, count):
     return lax.ppermute(array, AXES, [(i, i ^ step) for i in range(count)])
 
 
-def gather_blocks(block, order, count):
-    for step in order[:-1]:
-        block = jnp.concatenate([block, swap(block, step, count)], axis=0)
-    return block, swap(block, order[-1], count)
-
-
-def scatter_blocks(keep, send, steps, count):
-    for step in steps[:-1]:
-        got = swap(send, step, count)
-        half = keep.shape[0] // 2
+def after(value, *others):
+    return lax.optimization_barrier((value, *others))[0]
+
+
+def quarters(groups):
+    totals = []
+    for keep, got in groups:
         total = keep.astype(f32) + got.astype(f32)
-        send = total[half:].astype(bf16)
-        keep = total[:half].astype(bf16)
-    return keep, swap(send, steps[-1], count)
+        totals.append(total.reshape(4, 4, -1, 128))
+    total = jnp.concatenate(totals, axis=2) if len(totals) > 1 else totals[0]
+    return total[0], [total[i].astype(bf16).reshape(-1, 128) for i in range(1, 4)]
+
+
+def halves(keep, gots, blocks):
+    total = keep
+    for got in gots:
+        total = total + got.astype(f32).reshape(keep.shape)
+    rows = blocks // 2
+    return total[:rows], total[rows:].astype(bf16).reshape(-1, 128)
 
 
 def fast_layout(dp, fsdp):
     return dp == 4 and fsdp == 8
 
 
+def gather_far(block, z_far, z_near, count):
+    block = jnp.concatenate([block, swap(block, z_far, count)], axis=0)
+    return jnp.concatenate([block, swap(block, z_near, count)], axis=0)
+
+
 def body(dp, fsdp, tokens, lengths, assignment, weights, vectors, cotangent):
     count = dp * fsdp
+    fast = fast_layout(dp, fsdp)
     owner = lax.axis_index(AXES).astype(jnp.int32)
     owned = assignment == owner
     ends = jnp.cumsum(jnp.where(owned, lengths, 0), dtype=jnp.int32)
     ends = jnp.where(owned, ends, 1 << 30)[None, :]
-    if fast_layout(dp, fsdp):
+    if fast:
         vec_width = vectors.shape[0]
         core, x_step, y_step, z_near, z_far = fsdp, 1, 2 * fsdp, 2, 4
-        gather_order = [z_far, z_near, y_step, x_step, core]
-        scatter_steps = [core, x_step, y_step, z_near, z_far]
-        scatter_order = scatter_steps[::-1]
+        planes = [x_step, y_step, x_step + y_step]
+        order_in = [z_far, z_near]
+        order_out = [z_far, z_near, x_step, y_step, core]
+        masks = [0] + planes
+        masks = masks + [m + core for m in masks]
         me = owner[None]
-        placed = lax.dynamic_update_slice(jnp.zeros((16 * 128,), bf16), vectors, ((owner * vec_width) % 128,))
-        q_block, r_block = pack(weights.reshape(512, 128), placed.reshape(16, 128))
-        q_first, q_second = gather_blocks(q_block, gather_order, count)
-        r_first, r_second = gather_blocks(r_block, gather_order, count)
+        padded = jnp.pad(vectors, (0, 256 - vec_width)).reshape(1, 256)
+        q_block, r_block = pack(me, weights.reshape(512, 128), jnp.broadcast_to(padded, (16, 256)), vec_width)
+        q_far = gather_far(q_block, z_far, z_near, count)
+        q_pieces = [q_far] + [swap(q_far, step, count) for step in planes]
+        q_pieces = q_pieces + [swap(piece, core, count) for piece in q_pieces]
+        r_far = gather_far(after(r_block, q_far), z_far, z_near, count)
+        r_pieces = [swap(after(r_far, *q_pieces), step, count) for step in planes]
     else:
         vec_width = 160
-        gather_order = scatter_order = [1, 2, 4, 8, 16]
+        order_in, order_out = [1, 2], [1, 2, 4, 8, 16]
+        masks = [4 * i for i in range(8)]
         me = jnp.zeros((1,), jnp.int32)
         blocks = lax.all_gather(weights, AXES, axis=0, tiled=True).reshape(count, -1)
         flat = lax.all_gather(vectors, AXES, axis=0, tiled=True).reshape(40, 128)
@@ -712,29 +741,76 @@
             vec_blocks.append(jnp.concatenate([pair.reshape(2, 128), jnp.zeros((14, 128), bf16)], axis=0))
         q_all = jnp.concatenate([panels[0], jnp.stack(vec_blocks)], axis=1)
         r_all = jnp.concatenate(panels[1:], axis=1)
-        half = BLOCKS // 2
-        q_first, q_second = q_all[:half].reshape(-1, 128), q_all[half:].reshape(-1, 128)
-        r_first, r_second = r_all[:half].reshape(-1, 128), r_all[half:].reshape(-1, 128)
-    qkv, keys_extra, query_extra, vec = project(
-        me, ends, tokens, q_first, q_second, gather_order, vec_width, vectors.shape[0] * count
+        q_pieces = [q_all[4 * i : 4 * i + 4].reshape(-1, 128) for i in range(8)]
+        r_pieces = [r_all[4 * i : 4 * i + 4].reshape(-1, 128) for i in range(8)]
+    qkv, keys_extra, query_extra, vec, weight = project(
+        me, ends, tokens, q_pieces, masks, order_in, vec_width
     )
-    attended, query_extra = attend(qkv, query_extra, keys_extra)
+    prior = attend(qkv, query_extra, keys_extra, 0, 2, [])
+    if fast:
+        r_pieces = [r_far] + [after(piece, prior[0]) for piece in r_pieces]
+        keys_extra = after(keys_extra, *r_pieces)
+        r_pieces = r_pieces + [swap(piece, core, count) for piece in r_pieces]
+    attended, query_extra = attend(qkv, query_extra, keys_extra, 2, 2, prior)
     layer_output, grad_first, grad_attended, grad_extra, r_keep, r_send, vec_grad = middle(
-        me, tokens, attended, cotangent, vec, r_first, r_second, gather_order, scatter_order
+        me, tokens, attended, cotangent, vec, r_pieces, masks, order_in, order_out
     )
-    grad_query, grad_keys, grad_values = attend_back(qkv, grad_attended, query_extra, keys_extra, grad_extra)
-    q_keep, q_send = weight_grad(me, tokens, grad_query, grad_keys, grad_values, vec_grad, scatter_order, vec_width)
-    grad_tokens = input_grad(
-        me, grad_first, grad_query, grad_keys, grad_values, q_first, q_second, gather_order
-    )
-    if fast_layout(dp, fsdp):
-        r_keep, r_got = scatter_blocks(r_keep, r_send, scatter_steps, count)
-        q_keep, q_got = scatter_blocks(q_keep, q_send, scatter_steps, count)
-        own_weights, own_vec = unpack(q_keep, q_got, r_keep, r_got)
+    queries, keys, values, keeps, sends, gots = [], [], [], [], [], []
+    if fast:
+        r_got = swap(r_send, core, count)
+    for base, heads in ((0, 1), (1, 2), (3, 1)):
+        gq, gk, gv, keep, send, vec_grad = attend_back(
+            me,
+            tokens,
+            qkv,
+            grad_attended,
+            query_extra,
+            keys_extra,
+            grad_extra,
+            vec_grad,
+            order_out,
+            vec_width,
+            base,
+            heads,
+        )
+        queries.append(gq)
+        keys.append(gk)
+        values.append(gv)
+        keeps.append(keep)
+        sends.append(send)
+        if not fast:
+            continue
+        gots.append(swap(send, core, count))
+        if base == 0:
+            r_keep, r_sends = quarters([(r_keep, after(r_got, gq))])
+            vec_grad = after(vec_grad, *r_sends)
+            r_gots = [swap(part, step, count) for part, step in zip(r_sends, planes)]
+        elif base == 1:
+            r_gots = [after(part, gq) for part in r_gots]
+            r_keep, r_send = halves(r_keep, r_gots, 4)
+            vec_grad = after(vec_grad, r_send)
+            r_got = swap(r_send, z_near, count)
+    if fast:
+        r_keep, r_send = halves(r_keep, [after(r_got, gq)], 2)
+        r_got = swap(r_send, z_far, count)
+        q_keep, q_sends = quarters(list(zip(keeps, gots)))
+        grad_first = after(grad_first, *q_sends)
+        q_gots = [swap(part, step, count) for part, step in zip(q_sends, planes)]
+    grad_tokens = input_grad(grad_first, queries, keys, values, weight)
+    if fast:
+        q_gots = [after(part, grad_tokens) for part in q_gots]
+        q_keep, q_send = halves(q_keep, q_gots, 4)
+        q_got = swap(q_send, z_near, count)
+        q_keep, q_send = halves(q_keep, [q_got], 2)
+        q_got = swap(q_send, z_far, count)
+        own_weights, own_vec = unpack(
+            me, q_keep.reshape(-1, 128), q_got, r_keep.reshape(-1, 128), r_got, vec_width
+        )
         own_weights = own_weights.reshape(-1)
-        own_vectors = lax.dynamic_slice(own_vec.reshape(-1), ((owner * vec_width) % 128,), (vec_width,))
+        own_vectors = own_vec[0, :vec_width]
     else:
-        q_all = jnp.concatenate([q_keep, q_send], axis=0).astype(f32).reshape(BLOCKS, Q_ROWS, 128)
+        heads = [jnp.concatenate([k, g], axis=0).astype(f32).reshape(BLOCKS, -1, 128) for k, g in zip(keeps, sends)]
+        q_all = jnp.concatenate(heads, axis=1)
         r_all = jnp.concatenate([r_keep, r_send], axis=0).astype(f32).reshape(BLOCKS, R_ROWS, 128)
         sources = (q_all[:, : 4 * QKV_ROWS], r_all[:, :64], r_all[:, 64:192], r_all[:, 192:])
         pieces = []

time: 234 us -> 204 us (0.87)
  waiting for transfers between devices: 63.2 us -> 22.7 us
  Pallas kernels: 126 us -> 130 us
  other arithmetic: 6.03 us -> 8.9 us
  local copies, waits for them, and re-layouts: 7.94 us -> 10.8 us
    ppermute x20 -> x32, waiting for transfers between devices: 63.2 us -> 22.7 us  [swap(): return lax.ppermute(array, AXES, [(i, i ^ step) for i in range(count)])]
    add x0 -> x8, other arithmetic: none -> 4.61 us  [the longest x4 3.16 us: quarters(): total = keep.astype(f32) + got.astype(f32)]
    pallas_call x8 -> x10, Pallas kernels: 126 us -> 130 us  [the longest x3 56.5 us: attend_back(): pl.pallas_call(functools.partial(attend_back_kernel, base, heads, order,...]
    unnamed x32 -> x54, local copies, waits for them, and re-layouts: 4.02 us -> 5.6 us
    ppermute x20 -> x32, starting transfers between devices: 29 us -> 28.8 us  [swap(): return lax.ppermute(array, AXES, [(i, i ^ step) for i in range(count)])]
  transfers between devices with their start and end apart: 20 -> 32, of which waited for: 13 -> 13; matrix products, arithmetic and copies ran while one was open for 4% -> 4% of each run, Pallas kernels for 17% -> 48%
where the time goes in v2:
time: 204 us; the launch traced here: 203 us
  Pallas kernels  130 us (64%)
  starting transfers between devices  28.8 us (14%)
  waiting for transfers between devices  22.7 us (11%)
  local copies, waits for them, and re-layouts  10.8 us (5%)
  other arithmetic  8.9 us (4%)
    pallas_call x3, Pallas kernels, attend_back(): pl.pallas_call(functools.partial(attend_back_kernel, base, heads, order,...  56.5 us
    pallas_call x1, Pallas kernels, middle(): pl.pallas_call(functools.partial(middle_kernel, masks, order_in, order_ou...  30.1 us
    ppermute x32, starting transfers between devices, swap(): return lax.ppermute(array, AXES, [(i, i ^ step) for i in range(count)])  28.8 us
    ppermute x32, waiting for transfers between devices, swap(): return lax.ppermute(array, AXES, [(i, i ^ step) for i in range(count)])  22.7 us
    pallas_call x2, Pallas kernels, attend(): pl.pallas_call(attend_kernel, grid=(heads, count // rows), in_specs=[pl.B...  22.5 us
    pallas_call x1, Pallas kernels, input_grad(): pl.pallas_call(functools.partial(input_grad_kernel, len(queries)), grid=(...  9.36 us
    pallas_call x1, Pallas kernels, project(): pl.pallas_call(functools.partial(project_kernel, masks, order, vec_width)...  8.67 us
    unnamed x54, local copies, waits for them, and re-layouts  5.6 us
  transfers between devices with their start and end apart: 32, of which 13 were waited for; matrix products, arithmetic and copies ran while one was open for 4% of the time, Pallas kernels for 48%

profile of v2, /device:TPU:0, one launch (start us, length us, event | category | flops | bytes accessed | tf_op | source)
XLA Modules:
  0.0 202.9 jit_solution(18359551456360737045)
XLA Ops:
  0.6 0.7 pad.4
  1.9 1.6 pack.1
  3.5 4.0 %collective-permute-start = (bf16[208,128]{1,0:T(8,128)(2,1)}, bf16[208,128]{1,0:T(8,128)(2,1)S(1)}, u32[]{:S(2)}, u32[]{:S(2)}) collective-permute-start(bf16[208,128]{1,0:T(8,128)(2,1)} %get-tuple-element.58), channel_id=1, source_target_pairs={{0,4},{1,5},{2,6},{3,7},{4,0},{5,1},{6,2},{7,3},{8,12},{9,13},{10,... | collective-permute-start | bytes 159752 | tf_op jit(solution)/shard_map/ppermute | solution.py:665
  7.5 0.8 constant_dynamic-update-slice_fusion.2
  8.4 0.7 select_bitcast_fusion
  9.6 0.8 collective-permute-done
  10.4 0.8 pad_maximum_fusion.2
  11.3 1.3 collective-permute-start.1
  12.6 3.4 %collective-permute-done.1 = bf16[416,128]{1,0:T(8,128)(2,1)S(1)} collective-permute-done((bf16[416,128]{1,0:T(8,128)(2,1)S(1)}, bf16[416,128]{1,0:T(8,128)(2,1)S(1)}, u32[]{:S(2)}, u32[]{:S(2)}) %collective-permute-start.1) | collective-permute-done | bytes 106528 | tf_op jit(solution)/shard_map/ppermute | solution.py:665
  16.0 2.5 %collective-permute-start.9 = (bf16[320,128]{1,0:T(8,128)(2,1)}, bf16[320,128]{1,0:T(8,128)(2,1)S(1)}, u32[]{:S(2)}, u32[]{:S(2)}) collective-permute-start(bf16[320,128]{1,0:T(8,128)(2,1)} %get-tuple-element.63), channel_id=1, source_target_pairs={{0,4},{1,5},{2,6},{3,7},{4,0},{5,1},{6,2},{7,3},{8,12},{9,13},{10,... | collective-permute-start | bytes 245768 | tf_op jit(solution)/shard_map/ppermute | solution.py:665
  18.5 1.3 bitcast_select_fusion
  19.8 2.4 %collective-permute-start.4 = (bf16[832,128]{1,0:T(8,128)(2,1)S(1)}, bf16[832,128]{1,0:T(8,128)(2,1)S(1)}, u32[]{:S(2)}, u32[]{:S(2)}) collective-permute-start(bf16[832,128]{1,0:T(8,128)(2,1)S(1)} %constant_dynamic-update-slice_fusion.refs_0_), channel_id=1, source_target_pairs={{0,17},{1,16},{2,19},{3,18},{4,21},{5,20},{6,23},{7,22},{8,25},{9,... | collective-permute-start | bytes 638984 | tf_op jit(solution)/shard_map/ppermute | solution.py:665
  23.3 0.9 pad_maximum_fusion.1
  24.2 2.0 %collective-permute-start.10 = (bf16[640,128]{1,0:T(8,128)(2,1)S(1)}, bf16[640,128]{1,0:T(8,128)(2,1)S(1)}, u32[]{:S(2)}, u32[]{:S(2)}) collective-permute-start(bf16[640,128]{1,0:T(8,128)(2,1)S(1)} %pad_maximum_fusion.1), channel_id=1, source_target_pairs={{0,2},{1,3},{2,0},{3,1},{4,6},{5,7},{6,4},{7,5},{8,10},{9,11},{10,... | collective-permute-start | bytes 491528 | tf_op jit(solution)/shard_map/ppermute | solution.py:665
  26.2 0.9 constant_dynamic-update-slice_fusion.5
  27.1 1.7 collective-permute-done.4.refs_3_
  28.8 4.1 %collective-permute-done.3.refs_2_ = bf16[832,128]{1,0:T(8,128)(2,1)S(1)} collective-permute-done((bf16[832,128]{1,0:T(8,128)(2,1)S(1)}, bf16[832,128]{1,0:T(8,128)(2,1)S(1)}, u32[]{:S(2)}, u32[]{:S(2)}) %collective-permute-start.3) | collective-permute-done | bytes 213024 | tf_op jit(solution)/shard_map/ppermute | solution.py:665
  33.7 0.7 collective-permute-done.7.refs_6_
  34.7 1.7 collective-permute-start.13
  36.4 1.2 collective-permute-start.12
  38.2 8.7 %project.1 = (bf16[2048,1536]{1,0:T(8,128)(2,1)}, bf16[2048,128]{1,0:T(8,128)(2,1)}, bf16[4,2048,128]{2,1,0:T(8,128)(2,1)}, f32[48,128]{1,0:T(8,128)}, bf16[1536,512]{1,0:T(8,128)(2,1)}) custom-call(s32[1]{0:T(128)} %bitcast.me_ref, s32[1,256]{1,0:T(1,128)} %bitcast.52, bf16[2048,512]{1,0:T(8,128)(2,1)} %tokens.9, bf16[832,128]{1,0:T(8,128)(2,1)} %copy-done.10, ...), custom_call_target="tpu_custom_call" | custom-call | flops 3221225472 | bytes 12000000 | tf_op jit(solution)/shard_map/project/pallas_call | solution.py:142
  46.9 11.3 %attend.2 = (bf16[2048,512]{1,0:T(8,128)(2,1)}, bf16[4,2048,128]{2,1,0:T(8,128)(2,1)}) custom-call(bf16[2048,1536]{1,0:T(8,128)(2,1)} %get-tuple-element.59.q.k.v, bf16[2048,1536]{1,0:T(8,128)(2,1)} %get-tuple-element.59.q.k.v, bf16[2048,1536]{1,0:T(8,128)(2,1)} %get-tuple-element.59.q.k.v, bf16[4,2048,128]{2,1,0:T(8,128)(2,1)} %get-tuple-element.60.query_extra, ...), custom_call_target="tpu_custom_call" | custom-call | flops 8589934592 | bytes 6000000 | tf_op jit(solution)/shard_map/attend/pallas_call | solution.py:206
  58.9 11.3 %attend.3 = (bf16[2048,512]{1,0:T(8,128)(2,1)}, bf16[4,2048,128]{2,1,0:T(8,128)(2,1)}) custom-call(bf16[2048,1536]{1,0:T(8,128)(2,1)} %get-tuple-element.59.q.k.v, bf16[2048,1536]{1,0:T(8,128)(2,1)} %get-tuple-element.59.q.k.v, bf16[2048,1536]{1,0:T(8,128)(2,1)} %get-tuple-element.59.q.k.v, ...), custom_call_target="tpu_custom_call", output_to_operand_aliasing={{0}: (5, {}), {1}: (6, {})} | custom-call | flops 8589934592 | bytes 6000000 | tf_op jit(solution)/shard_map/attend/pallas_call | solution.py:206
  70.3 0.7 copy-done.11
  71.3 30.1 %middle.1 = (bf16[2048,512]{1,0:T(8,128)(2,1)}, f32[2048,512]{1,0:T(8,128)}, bf16[2048,512]{1,0:T(8,128)(2,1)}, bf16[4,2048,128]{2,1,0:T(8,128)(2,1)}, bf16[5120...) custom-call(s32[1]{0:T(128)} %bitcast.me_ref, bf16[2048,512]{1,0:T(8,128)(2,1)} %tokens.9, ...), custom_call_target="tpu_custom_call" | custom-call | flops 16106127360 | bytes 22000000 | tf_op jit(solution)/shard_map/middle/pallas_call | solution.py:409
  101.8 14.5 %attend_back.3 = (bf16[2048,128]{1,0:T(8,128)(2,1)}, bf16[128,2048]{1,0:T(8,128)(2,1)}, bf16[128,2048]{1,0:T(8,128)(2,1)}, bf16[768,128]{1,0:T(8,128)(2,1)}, bf1...) custom-call(s32[1]{0:T(128)} %bitcast.me_ref, bf16[2048,512]{1,0:T(8,128)(2,1)} %tokens.9, ...), custom_call_target="tpu_custom_call" | custom-call | flops 10737418240 | bytes 6000000 | tf_op jit(solution)/shard_map/attend_back/pallas_call | solution.py:563
  116.5 1.6 collective-permute-done.18
  118.1 1.0 convert_add_fusion.3
  119.1 1.0 copy-done
  120.2 2.1 %convert_add_fusion = (f32[5120,128]{1,0:T(8,128)S(1)}, bf16[5120,128]{1,0:T(8,128)(2,1)S(1)}) fusion(bf16[5120,128]{1,0:T(8,128)(2,1)} %copy-done, bf16[5120,128]{1,0:T(8,128)(2,1)} %get-tuple-element.82), kind=kLoop, calls=%fused_computation | loop fusion | flops 2621440 | bytes 6553600 | tf_op jit(solution)/shard_map/add | solution.py:675
  122.2 1.1 fusion.8
  123.3 1.7 collective-permute-start.23
  125.0 1.2 collective-permute-start.22
  126.8 27.1 %attend_back.4 = (bf16[2048,256]{1,0:T(8,128)(2,1)}, bf16[256,2048]{1,0:T(8,128)(2,1)}, bf16[256,2048]{1,0:T(8,128)(2,1)}, bf16[1536,128]{1,0:T(8,128)(2,1)}, bf...) custom-call(s32[1]{0:T(128)} %bitcast.me_ref, bf16[2048,512]{1,0:T(8,128)(2,1)} %tokens.9, ...), custom_call_target="tpu_custom_call" | custom-call | flops 21474836480 | bytes 12000000 | tf_op jit(solution)/shard_map/attend_back/pallas_call | solution.py:563
  154.0 0.7 copy-done.2
  154.8 1.3 fusion.1
  156.2 2.0 %collective-permute-start.30 = (bf16[640,128]{1,0:T(8,128)(2,1)S(1)}, bf16[640,128]{1,0:T(8,128)(2,1)S(1)}, u32[]{:S(2)}, u32[]{:S(2)}) collective-permute-start(bf16[640,128]{1,0:T(8,128)(2,1)S(1)} %slice.133), channel_id=1, source_target_pairs={{0,2},{1,3},{2,0},{3,1},{4,6},{5,7},{6,4},{7,5},{8,10},{9,11},{10,... | collective-permute-start | bytes 491528 | tf_op jit(solution)/shard_map/ppermute | solution.py:665
  158.2 14.8 %attend_back.5 = (bf16[2048,128]{1,0:T(8,128)(2,1)}, bf16[128,2048]{1,0:T(8,128)(2,1)}, bf16[128,2048]{1,0:T(8,128)(2,1)}, bf16[1024,128]{1,0:T(8,128)(2,1)}, bf...) custom-call(s32[1]{0:T(128)} %bitcast.me_ref, bf16[2048,512]{1,0:T(8,128)(2,1)} %tokens.9, ...), custom_call_target="tpu_custom_call" | custom-call | flops 10737418240 | bytes 6000000 | tf_op jit(solution)/shard_map/attend_back/pallas_call | solution.py:563
  173.4 1.4 collective-permute-done.24
  175.1 1.6 collective-permute-start.26
  176.7 1.4 collective-permute-start.27
  178.7 9.4 %input_grad.1 = f32[2048,512]{1,0:T(8,128)} custom-call(f32[2048,512]{1,0:T(8,128)} %get-tuple-element.97.refs_0_, bf16[2048,128]{1,0:T(8,128)(2,1)} %get-tuple-element.84.refs_1_, bf16[2048,256]{1,0:T(8,128)(2,1)} %get-tuple-element.90.refs_2_, bf16[2048,128]{1,0:T(8,128)(2,1)} %get-tuple-element.98.refs_3_, bf16[128,2048]{1,0:T(8,128)(2,1)} %get-tuple-element.99.refs_4_, ...), custom_call_target="tpu_custom_call" | custom-call | flops 3221225472 | bytes 16000000 | tf_op jit(solution)/shard_map/input_grad/pallas_call | solution.py:624
  189.1 0.7 slice.109.r_keep
  189.9 3.9 %collective-permute-done.28 = bf16[416,128]{1,0:T(8,128)(2,1)S(1)} collective-permute-done((bf16[416,128]{1,0:T(8,128)(2,1)S(1)}, bf16[416,128]{1,0:T(8,128)(2,1)S(1)}, u32[]{:S(2)}, u32[]{:S(2)}) %collective-permute-start.28) | collective-permute-done | bytes 106528 | tf_op jit(solution)/shard_map/ppermute | solution.py:665
  194.6 2.7 %collective-permute-done.31.r_got = bf16[320,128]{1,0:T(8,128)(2,1)S(1)} collective-permute-done((bf16[320,128]{1,0:T(8,128)(2,1)S(1)}, bf16[320,128]{1,0:T(8,128)(2,1)S(1)}, u32[]{:S(2)}, u32[]{:S(2)}) %collective-permute-start.31) | collective-permute-done | bytes 81952 | tf_op jit(solution)/shard_map/ppermute | solution.py:665
  197.3 1.9 collective-permute-done.29.q_got
  199.8 1.8 unpack.1
  201.6 1.3 slice.94
  (111 shorter events, 9.9 us)
Async XLA Ops:
  3.5 6.9 %collective-permute-start = (bf16[208,128]{1,0:T(8,128)(2,1)}, bf16[208,128]{1,0:T(8,128)(2,1)S(1)}, u32[]{:S(2)}, u32[]{:S(2)}) collective-permute-start(bf16[208,128]{1,0:T(8,128)(2,1)} %get-tuple-element.58), channel_id=1, source_target_pairs={{0,4},{1,5},{2,6},{3,7},{4,0},{5,1},{6,2},{7,3},{8,12},{9,13},{10,... | collective-permute-start | bytes 159752 | tf_op jit(solution)/shard_map/ppermute | solution.py:665
  11.3 4.7 %collective-permute-start.1 = (bf16[416,128]{1,0:T(8,128)(2,1)S(1)}, bf16[416,128]{1,0:T(8,128)(2,1)S(1)}, u32[]{:S(2)}, u32[]{:S(2)}) collective-permute-start(bf16[416,128]{1,0:T(8,128)(2,1)S(1)} %pad_maximum_fusion.2), channel_id=1, source_target_pairs={{0,2},{1,3},{2,0},{3,1},{4,6},{5,7},{6,4},{7,5},{8,10},{9,11},{10,... | collective-permute-start | bytes 319496 | tf_op jit(solution)/shard_map/ppermute | solution.py:665
  16.0 22.2 %copy-start.10 = (bf16[832,128]{1,0:T(8,128)(2,1)}, bf16[832,128]{1,0:T(8,128)(2,1)S(1)}, u32[]{:S(2)}) copy-start(bf16[832,128]{1,0:T(8,128)(2,1)S(1)} %constant_dynamic-update-slice_fusion.refs_0_) | copy-start | bytes 638980
  16.0 7.3 %collective-permute-start.9 = (bf16[320,128]{1,0:T(8,128)(2,1)}, bf16[320,128]{1,0:T(8,128)(2,1)S(1)}, u32[]{:S(2)}, u32[]{:S(2)}) collective-permute-start(bf16[320,128]{1,0:T(8,128)(2,1)} %get-tuple-element.63), channel_id=1, source_target_pairs={{0,4},{1,5},{2,6},{3,7},{4,0},{5,1},{6,2},{7,3},{8,12},{9,13},{10,... | collective-permute-start | bytes 245768 | tf_op jit(solution)/shard_map/ppermute | solution.py:665
  19.8 13.9 %collective-permute-start.5 = (bf16[832,128]{1,0:T(8,128)(2,1)S(1)}, bf16[832,128]{1,0:T(8,128)(2,1)S(1)}, u32[]{:S(2)}, u32[]{:S(2)}) collective-permute-start(bf16[832,128]{1,0:T(8,128)(2,1)S(1)} %constant_dynamic-update-slice_fusion.refs_0_), channel_id=1, source_target_pairs={{0,8},{1,9},{2,10},{3,11},{4,12},{5,13},{6,14},{7,15},{8,0},{9,1},... | collective-permute-start | bytes 638984 | tf_op jit(solution)/shard_map/ppermute | solution.py:665
  19.8 9.0 %collective-permute-start.4 = (bf16[832,128]{1,0:T(8,128)(2,1)S(1)}, bf16[832,128]{1,0:T(8,128)(2,1)S(1)}, u32[]{:S(2)}, u32[]{:S(2)}) collective-permute-start(bf16[832,128]{1,0:T(8,128)(2,1)S(1)} %constant_dynamic-update-slice_fusion.refs_0_), channel_id=1, source_target_pairs={{0,17},{1,16},{2,19},{3,18},{4,21},{5,20},{6,23},{7,22},{8,25},{9,... | collective-permute-start | bytes 638984 | tf_op jit(solution)/shard_map/ppermute | solution.py:665
  22.2 10.7 %collective-permute-start.3 = (bf16[832,128]{1,0:T(8,128)(2,1)S(1)}, bf16[832,128]{1,0:T(8,128)(2,1)S(1)}, u32[]{:S(2)}, u32[]{:S(2)}) collective-permute-start(bf16[832,128]{1,0:T(8,128)(2,1)S(1)} %constant_dynamic-update-slice_fusion.refs_0_), channel_id=1, source_target_pairs={{0,16},{1,17},{2,18},{3,19},{4,20},{5,21},{6,22},{7,23},{8,24},{9,... | collective-permute-start | bytes 638984 | tf_op jit(solution)/shard_map/ppermute | solution.py:665
  22.7 10.3 %collective-permute-start.2 = (bf16[832,128]{1,0:T(8,128)(2,1)S(1)}, bf16[832,128]{1,0:T(8,128)(2,1)S(1)}, u32[]{:S(2)}, u32[]{:S(2)}) collective-permute-start(bf16[832,128]{1,0:T(8,128)(2,1)S(1)} %constant_dynamic-update-slice_fusion.refs_0_), channel_id=1, source_target_pairs={{0,1},{1,0},{2,3},{3,2},{4,5},{5,4},{6,7},{7,6},{8,9},{9,8},{10,11... | collective-permute-start | bytes 638984 | tf_op jit(solution)/shard_map/ppermute | solution.py:665
  24.2 9.3 %collective-permute-start.10 = (bf16[640,128]{1,0:T(8,128)(2,1)S(1)}, bf16[640,128]{1,0:T(8,128)(2,1)S(1)}, u32[]{:S(2)}, u32[]{:S(2)}) collective-permute-start(bf16[640,128]{1,0:T(8,128)(2,1)S(1)} %pad_maximum_fusion.1), channel_id=1, source_target_pairs={{0,2},{1,3},{2,0},{3,1},{4,6},{5,7},{6,4},{7,5},{8,10},{9,11},{10,... | collective-permute-start | bytes 491528 | tf_op jit(solution)/shard_map/ppermute | solution.py:665
  28.8 9.4 %copy-start.19 = (bf16[832,128]{1,0:T(8,128)(2,1)}, bf16[832,128]{1,0:T(8,128)(2,1)S(1)}, u32[]{:S(2)}) copy-start(bf16[832,128]{1,0:T(8,128)(2,1)S(1)} %collective-permute-done.4.refs_3_) | copy-start | bytes 638980
  28.8 4.9 %collective-permute-start.8 = (bf16[832,128]{1,0:T(8,128)(2,1)S(1)}, bf16[832,128]{1,0:T(8,128)(2,1)S(1)}, u32[]{:S(2)}, u32[]{:S(2)}) collective-permute-start(bf16[832,128]{1,0:T(8,128)(2,1)S(1)} %collective-permute-done.4.refs_3_), channel_id=1, source_target_pairs={{0,8},{1,9},{2,10},{3,11},{4,12},{5,13},{6,14},{7,15},{8,0},{9,1},... | collective-permute-start | bytes 638984 | tf_op jit(solution)/shard_map/ppermute | solution.py:665
  32.9 5.3 %copy-start.20 = (bf16[832,128]{1,0:T(8,128)(2,1)}, bf16[832,128]{1,0:T(8,128)(2,1)S(1)}, u32[]{:S(2)}) copy-start(bf16[832,128]{1,0:T(8,128)(2,1)S(1)} %collective-permute-done.3.refs_2_) | copy-start | bytes 638980
  32.9 1.5 collective-permute-start.7
  33.0 5.2 %copy-start.21 = (bf16[832,128]{1,0:T(8,128)(2,1)}, bf16[832,128]{1,0:T(8,128)(2,1)S(1)}, u32[]{:S(2)}) copy-start(bf16[832,128]{1,0:T(8,128)(2,1)S(1)} %collective-permute-done.2.refs_1_) | copy-start | bytes 638980
  33.0 1.7 collective-permute-start.6
  33.5 13.4 %copy-start.9 = (bf16[1280,128]{1,0:T(8,128)(2,1)}, bf16[1280,128]{1,0:T(8,128)(2,1)S(1)}, u32[]{:S(2)}) copy-start(bf16[1280,128]{1,0:T(8,128)(2,1)S(1)} %constant_dynamic-update-slice_fusion.3.refs_0_) | copy-start | bytes 983044
  33.5 36.7 %collective-permute-start.14 = (bf16[1280,128]{1,0:T(8,128)(2,1)S(1)}, bf16[1280,128]{1,0:T(8,128)(2,1)S(1)}, u32[]{:S(2)}, u32[]{:S(2)}) collective-permute-start(bf16[1280,128]{1,0:T(8,128)(2,1)S(1)} %constant_dynamic-update-slice_fusion.3.refs_0_), channel_id=1, source_target_pairs={{0,8},{1,9},{2,10},{3,11},{4,12},{5,13},{6,14},{7,15},{8,0},{9,1},... | collective-permute-start | bytes 983048 | tf_op jit(solution)/shard_map/ppermute | solution.py:665
  33.7 4.5 %copy-start.18 = (bf16[832,128]{1,0:T(8,128)(2,1)}, bf16[832,128]{1,0:T(8,128)(2,1)S(1)}, u32[]{:S(2)}) copy-start(bf16[832,128]{1,0:T(8,128)(2,1)S(1)} %collective-permute-done.5.refs_4_) | copy-start | bytes 638980
  33.7 4.5 %copy-start.22 = (bf16[832,128]{1,0:T(8,128)(2,1)}, bf16[832,128]{1,0:T(8,128)(2,1)S(1)}, u32[]{:S(2)}) copy-start(bf16[832,128]{1,0:T(8,128)(2,1)S(1)} %collective-permute-done.8.refs_7_) | copy-start | bytes 638980
  34.4 3.8 %copy-start.23 = (bf16[832,128]{1,0:T(8,128)(2,1)}, bf16[832,128]{1,0:T(8,128)(2,1)S(1)}, u32[]{:S(2)}) copy-start(bf16[832,128]{1,0:T(8,128)(2,1)S(1)} %collective-permute-done.7.refs_6_) | copy-start | bytes 638980
  34.7 3.5 %copy-start.24 = (bf16[832,128]{1,0:T(8,128)(2,1)}, bf16[832,128]{1,0:T(8,128)(2,1)S(1)}, u32[]{:S(2)}) copy-start(bf16[832,128]{1,0:T(8,128)(2,1)S(1)} %collective-permute-done.6.refs_5_) | copy-start | bytes 638980
  34.7 23.5 %collective-permute-start.13 = (bf16[1280,128]{1,0:T(8,128)(2,1)S(1)}, bf16[1280,128]{1,0:T(8,128)(2,1)S(1)}, u32[]{:S(2)}, u32[]{:S(2)}) collective-permute-start(bf16[1280,128]{1,0:T(8,128)(2,1)S(1)} %constant_dynamic-update-slice_fusion.3.refs_0_), channel_id=1, source_target_pairs={{0,17},{1,16},{2,19},{3,18},{4,21},{5,20},{6,23},{7,22},{8,25},{9,... | collective-permute-start | bytes 983048 | tf_op jit(solution)/shard_map/ppermute | solution.py:665
  36.4 21.8 %collective-permute-start.12 = (bf16[1280,128]{1,0:T(8,128)(2,1)S(1)}, bf16[1280,128]{1,0:T(8,128)(2,1)S(1)}, u32[]{:S(2)}, u32[]{:S(2)}) collective-permute-start(bf16[1280,128]{1,0:T(8,128)(2,1)S(1)} %constant_dynamic-update-slice_fusion.3.refs_0_), channel_id=1, source_target_pairs={{0,16},{1,17},{2,18},{3,19},{4,20},{5,21},{6,22},{7,23},{8,24},{9,... | collective-permute-start | bytes 983048 | tf_op jit(solution)/shard_map/ppermute | solution.py:665
  37.6 20.6 %collective-permute-start.11 = (bf16[1280,128]{1,0:T(8,128)(2,1)S(1)}, bf16[1280,128]{1,0:T(8,128)(2,1)S(1)}, u32[]{:S(2)}, u32[]{:S(2)}) collective-permute-start(bf16[1280,128]{1,0:T(8,128)(2,1)S(1)} %constant_dynamic-update-slice_fusion.3.refs_0_), channel_id=1, source_target_pairs={{0,1},{1,0},{2,3},{3,2},{4,5},{5,4},{6,7},{7,6},{8,9},{9,8},{10,11... | collective-permute-start | bytes 983048 | tf_op jit(solution)/shard_map/ppermute | solution.py:665
  58.2 12.0 %copy-start.12 = (bf16[1280,128]{1,0:T(8,128)(2,1)}, bf16[1280,128]{1,0:T(8,128)(2,1)S(1)}, u32[]{:S(2)}) copy-start(bf16[1280,128]{1,0:T(8,128)(2,1)S(1)} %collective-permute-done.13.refs_3_) | copy-start | bytes 983044
  58.2 11.9 %copy-start.13 = (bf16[1280,128]{1,0:T(8,128)(2,1)}, bf16[1280,128]{1,0:T(8,128)(2,1)S(1)}, u32[]{:S(2)}) copy-start(bf16[1280,128]{1,0:T(8,128)(2,1)S(1)} %collective-permute-done.12.refs_2_) | copy-start | bytes 983044
  58.2 11.9 %copy-start.14 = (bf16[1280,128]{1,0:T(8,128)(2,1)}, bf16[1280,128]{1,0:T(8,128)(2,1)S(1)}, u32[]{:S(2)}) copy-start(bf16[1280,128]{1,0:T(8,128)(2,1)S(1)} %collective-permute-done.11.refs_1_) | copy-start | bytes 983044
  58.3 11.9 %collective-permute-start.15 = (bf16[1280,128]{1,0:T(8,128)(2,1)S(1)}, bf16[1280,128]{1,0:T(8,128)(2,1)S(1)}, u32[]{:S(2)}, u32[]{:S(2)}) collective-permute-start(bf16[1280,128]{1,0:T(8,128)(2,1)S(1)} %collective-permute-done.11.refs_1_), channel_id=1, source_target_pairs={{0,8},{1,9},{2,10},{3,11},{4,12},{5,13},{6,14},{7,15},{8,0},{9,1},... | collective-permute-start | bytes 983048 | tf_op jit(solution)/shard_map/ppermute | solution.py:665
  58.3 11.9 %collective-permute-start.16 = (bf16[1280,128]{1,0:T(8,128)(2,1)S(1)}, bf16[1280,128]{1,0:T(8,128)(2,1)S(1)}, u32[]{:S(2)}, u32[]{:S(2)}) collective-permute-start(bf16[1280,128]{1,0:T(8,128)(2,1)S(1)} %collective-permute-done.12.refs_2_), channel_id=1, source_target_pairs={{0,8},{1,9},{2,10},{3,11},{4,12},{5,13},{6,14},{7,15},{8,0},{9,1},... | collective-permute-start | bytes 983048 | tf_op jit(solution)/shard_map/ppermute | solution.py:665
  58.8 11.4 %collective-permute-start.17 = (bf16[1280,128]{1,0:T(8,128)(2,1)S(1)}, bf16[1280,128]{1,0:T(8,128)(2,1)S(1)}, u32[]{:S(2)}, u32[]{:S(2)}) collective-permute-start(bf16[1280,128]{1,0:T(8,128)(2,1)S(1)} %collective-permute-done.13.refs_3_), channel_id=1, source_target_pairs={{0,8},{1,9},{2,10},{3,11},{4,12},{5,13},{6,14},{7,15},{8,0},{9,1},... | collective-permute-start | bytes 983048 | tf_op jit(solution)/shard_map/ppermute | solution.py:665
  101.3 17.7 %collective-permute-start.19 = (bf16[5120,128]{1,0:T(8,128)(2,1)}, bf16[5120,128]{1,0:T(8,128)(2,1)S(1)}, u32[]{:S(2)}, u32[]{:S(2)}) collective-permute-start(bf16[5120,128]{1,0:T(8,128)(2,1)} %get-tuple-element.83), channel_id=1, source_target_pairs={{0,8},{1,9},{2,10},{3,11},{4,12},{5,13},{6,14},{7,15},{8,0},{9,1},... | collective-permute-start | bytes 3932168 | tf_op jit(solution)/shard_map/ppermute | solution.py:665
  116.4 1.7 collective-permute-start.18
  123.3 30.7 %collective-permute-start.23 = (bf16[1280,128]{1,0:T(8,128)(2,1)}, bf16[1280,128]{1,0:T(8,128)(2,1)S(1)}, u32[]{:S(2)}, u32[]{:S(2)}) collective-permute-start(bf16[1280,128]{1,0:T(8,128)(2,1)} %get-tuple-element.114), channel_id=1, source_target_pairs={{0,17},{1,16},{2,19},{3,18},{4,21},{5,20},{6,23},{7,22},{8,25},{9,... | collective-permute-start | bytes 983048 | tf_op jit(solution)/shard_map/ppermute | solution.py:665
  125.0 28.9 %collective-permute-start.22 = (bf16[1280,128]{1,0:T(8,128)(2,1)}, bf16[1280,128]{1,0:T(8,128)(2,1)S(1)}, u32[]{:S(2)}, u32[]{:S(2)}) collective-permute-start(bf16[1280,128]{1,0:T(8,128)(2,1)} %get-tuple-element.115), channel_id=1, source_target_pairs={{0,16},{1,17},{2,18},{3,19},{4,20},{5,21},{6,22},{7,23},{8,24},{9,... | collective-permute-start | bytes 983048 | tf_op jit(solution)/shard_map/ppermute | solution.py:665
  126.2 27.7 %collective-permute-start.21 = (bf16[1280,128]{1,0:T(8,128)(2,1)}, bf16[1280,128]{1,0:T(8,128)(2,1)}, u32[]{:S(2)}, u32[]{:S(2)}) collective-permute-start(bf16[1280,128]{1,0:T(8,128)(2,1)} %get-tuple-element.116), channel_id=1, source_target_pairs={{0,1},{1,0},{2,3},{3,2},{4,5},{5,4},{6,7},{7,6},{8,9},{9,8},{10,11... | collective-permute-start | bytes 983048 | tf_op jit(solution)/shard_map/ppermute | solution.py:665
  153.9 19.5 %collective-permute-start.20 = (bf16[1536,128]{1,0:T(8,128)(2,1)}, bf16[1536,128]{1,0:T(8,128)(2,1)S(1)}, u32[]{:S(2)}, u32[]{:S(2)}) collective-permute-start(bf16[1536,128]{1,0:T(8,128)(2,1)} %get-tuple-element.88), channel_id=1, source_target_pairs={{0,8},{1,9},{2,10},{3,11},{4,12},{5,13},{6,14},{7,15},{8,0},{9,1},... | collective-permute-start | bytes 1179656 | tf_op jit(solution)/shard_map/ppermute | solution.py:665
  156.2 17.3 %collective-permute-start.30 = (bf16[640,128]{1,0:T(8,128)(2,1)S(1)}, bf16[640,128]{1,0:T(8,128)(2,1)S(1)}, u32[]{:S(2)}, u32[]{:S(2)}) collective-permute-start(bf16[640,128]{1,0:T(8,128)(2,1)S(1)} %slice.133), channel_id=1, source_target_pairs={{0,2},{1,3},{2,0},{3,1},{4,6},{5,7},{6,4},{7,5},{8,10},{9,11},{10,... | collective-permute-start | bytes 491528 | tf_op jit(solution)/shard_map/ppermute | solution.py:665
  158.2 15.1 %copy-start.1 = (bf16[1536,128]{1,0:T(8,128)(2,1)S(1)}, bf16[1536,128]{1,0:T(8,128)(2,1)}, u32[]{:S(2)}) copy-start(bf16[1536,128]{1,0:T(8,128)(2,1)} %get-tuple-element.87) | copy-start | bytes 1179652
  173.0 1.8 copy-start.4
  173.1 1.8 collective-permute-start.24
  173.4 1.6 copy-start.5
  175.1 13.0 %collective-permute-start.26 = (bf16[832,128]{1,0:T(8,128)(2,1)S(1)}, bf16[832,128]{1,0:T(8,128)(2,1)S(1)}, u32[]{:S(2)}, u32[]{:S(2)}) collective-permute-start(bf16[832,128]{1,0:T(8,128)(2,1)S(1)} %bitcast.44), channel_id=1, source_target_pairs={{0,16},{1,17},{2,18},{3,19},{4,20},{5,21},{6,22},{7,23},{8,24},{9,... | collective-permute-start | bytes 638984 | tf_op jit(solution)/shard_map/ppermute | solution.py:665
  176.7 11.5 %collective-permute-start.27 = (bf16[832,128]{1,0:T(8,128)(2,1)S(1)}, bf16[832,128]{1,0:T(8,128)(2,1)S(1)}, u32[]{:S(2)}, u32[]{:S(2)}) collective-permute-start(bf16[832,128]{1,0:T(8,128)(2,1)S(1)} %bitcast.43), channel_id=1, source_target_pairs={{0,17},{1,16},{2,19},{3,18},{4,21},{5,20},{6,23},{7,22},{8,25},{9,... | collective-permute-start | bytes 638984 | tf_op jit(solution)/shard_map/ppermute | solution.py:665
  178.1 10.2 %collective-permute-start.25 = (bf16[832,128]{1,0:T(8,128)(2,1)S(1)}, bf16[832,128]{1,0:T(8,128)(2,1)S(1)}, u32[]{:S(2)}, u32[]{:S(2)}) collective-permute-start(bf16[832,128]{1,0:T(8,128)(2,1)S(1)} %bitcast.42), channel_id=1, source_target_pairs={{0,1},{1,0},{2,3},{3,2},{4,5},{5,4},{6,7},{7,6},{8,9},{9,8},{10,11... | collective-permute-start | bytes 638984 | tf_op jit(solution)/shard_map/ppermute | solution.py:665
  188.5 5.4 %collective-permute-start.28 = (bf16[416,128]{1,0:T(8,128)(2,1)S(1)}, bf16[416,128]{1,0:T(8,128)(2,1)S(1)}, u32[]{:S(2)}, u32[]{:S(2)}) collective-permute-start(bf16[416,128]{1,0:T(8,128)(2,1)S(1)} %bitcast.50), channel_id=1, source_target_pairs={{0,2},{1,3},{2,0},{3,1},{4,6},{5,7},{6,4},{7,5},{8,10},{9,11},{10,... | collective-permute-start | bytes 319496 | tf_op jit(solution)/shard_map/ppermute | solution.py:665
  189.8 7.5 %collective-permute-start.31 = (bf16[320,128]{1,0:T(8,128)(2,1)S(1)}, bf16[320,128]{1,0:T(8,128)(2,1)S(1)}, u32[]{:S(2)}, u32[]{:S(2)}) collective-permute-start(bf16[320,128]{1,0:T(8,128)(2,1)S(1)} %slice.135), channel_id=1, source_target_pairs={{0,4},{1,5},{2,6},{3,7},{4,0},{5,1},{6,2},{7,3},{8,12},{9,13},{10,... | collective-permute-start | bytes 245768 | tf_op jit(solution)/shard_map/ppermute | solution.py:665
  193.9 5.3 %collective-permute-start.29 = (bf16[208,128]{1,0:T(8,128)(2,1)S(1)}, bf16[208,128]{1,0:T(8,128)(2,1)S(1)}, u32[]{:S(2)}, u32[]{:S(2)}) collective-permute-start(bf16[208,128]{1,0:T(8,128)(2,1)S(1)} %fusion.5), channel_id=1, source_target_pairs={{0,4},{1,5},{2,6},{3,7},{4,0},{5,1},{6,2},{7,3},{8,12},{9,13},{10,... | collective-permute-start | bytes 159752 | tf_op jit(solution)/shard_map/ppermute | solution.py:665
  197.3 1.9 copy-start.7
  (9 other events, 7.7 us)

commit v3 on v2

--- a/solution.py
+++ b/solution.py
@@ -24,15 +24,15 @@
 NN = (((1,), (0,)), ((), ()))
 TN = (((0,), (0,)), ((), ()))
 TT = (((0,), (1,)), ((), ()))
-VMEM_BYTES = 60 << 20
+VMEM_MIB = {"pack": 2, "project": 16, "attend": 28, "middle": 36, "attend_back": 28, "input_grad": 16, "unpack": 3}
 
 
 def dot(a, b, dims):
     return lax.dot_general(a, b, dims, preferred_element_type=f32)
 
 
-def params():
-    return pltpu.CompilerParams(vmem_limit_bytes=VMEM_BYTES)
+def params(name):
+    return pltpu.CompilerParams(vmem_limit_bytes=VMEM_MIB[name] << 20)
 
 
 def cost(flops, moved, special=0):
@@ -65,9 +65,11 @@
 PANELS = ((0, 48, 4), (192, 16, 4), (256, 16, 8), (384, 32, 4))
 
 
-def pack_kernel(vec_width, me_ref, flat, vec, q_out, r_out, wide):
+def pack_kernel(vec_width, me_ref, flat, vec, q_out, r_out, wide, line):
     wide[...] = flat[...].astype(f32)
-    shifted = pltpu.roll(vec[...].astype(f32), (me_ref[0] * vec_width) % 128, 1)
+    line[...] = jnp.zeros_like(line)
+    line[0:1, 0:vec_width] = vec[...].astype(f32)
+    shifted = pltpu.roll(line[...], (me_ref[0] * vec_width) % 128, 1)
     parts = []
     for start, rows, count in PANELS:
         for j in range(count):
@@ -87,7 +89,8 @@
             jax.ShapeDtypeStruct((Q_ROWS, 128), bf16),
             jax.ShapeDtypeStruct((R_ROWS, 128), bf16),
         ],
-        scratch_shapes=[pltpu.VMEM((512, 128), f32)],
+        scratch_shapes=[pltpu.VMEM((512, 128), f32), pltpu.VMEM((8, 256), f32)],
+        compiler_params=params("pack"),
         name="pack",
     )(me, flat, vec)
 
@@ -131,9 +134,11 @@
     keys_extra[...] = jnp.where(lane < 8, jnp.where(same, 1.0, 0.0), jnp.where(lane < 12, 1.0, 0.0)).astype(bf16)
     apart = jnp.where((lane < 8) & jnp.logical_not(same), FAR, 0.0)
     product = queries.astype(f32) * key_heads.astype(f32)
+    extra = apart
     for h in range(HEADS):
         own = jnp.sum(product[:, 128 * h : 128 * (h + 1)], axis=1, keepdims=True)
-        query_extra[h] = jnp.where(lane == 8, -own, apart).astype(bf16)
+        extra = jnp.where(lane == 8 + h, -own, extra)
+    query_extra[...] = extra.astype(bf16)
 
 
 def project(me, ends, tokens, pieces, masks, order, vec_width, rows=512):
@@ -151,81 +156,80 @@
         out_specs=[
             pl.BlockSpec((rows, 1536), lambda i: (i, 0)),
             pl.BlockSpec((rows, 128), lambda i: (i, 0)),
-            pl.BlockSpec((HEADS, rows, 128), lambda i: (0, i, 0)),
+            pl.BlockSpec((rows, 128), lambda i: (i, 0)),
             whole((48, 128)),
             whole((1536, 512)),
         ],
         out_shape=[
             jax.ShapeDtypeStruct((count, 1536), bf16),
             jax.ShapeDtypeStruct((count, 128), bf16),
-            jax.ShapeDtypeStruct((HEADS, count, 128), bf16),
+            jax.ShapeDtypeStruct((count, 128), bf16),
             jax.ShapeDtypeStruct((48, 128), f32),
             jax.ShapeDtypeStruct((1536, 512), bf16),
         ],
         scratch_shapes=[pltpu.VMEM((48, 128), f32)],
-        compiler_params=params(),
+        compiler_params=params("project"),
         cost_estimate=cost(2 * count * 512 * 1536, 12e6),
         name="project",
     )(me, ends, tokens, *pieces)
 
 
-def attend_kernel(q, k, v, query_extra, keys_extra, *refs):
-    attended, query_extra_out, total, mixed, peak = refs[-5:]
+def attend_kernel(base, q, k, v, query_extra, keys_extra, *refs):
+    attended, weights_out, inverse_out, total, mixed = refs[-5:]
     rows = q.shape[0]
+    head = base + pl.program_id(0)
+    lane = lax.broadcasted_iota(jnp.int32, (rows, 128), 1)
+    extra = jnp.where((lane < 8) | (lane == 8 + head), query_extra[...].astype(f32), 0.0).astype(bf16)
     left = jnp.concatenate([k[...], keys_extra[...]], axis=1)
-    right = jnp.concatenate([q[...], query_extra[0]], axis=1)
-    scores = dot(left, right, NT)
-    weights = jnp.exp(scores)
+    right = jnp.concatenate([q[...], extra], axis=1)
+    weights = jnp.exp(dot(left, right, NT))
+    low = weights.astype(bf16)
+    weights_out[0] = low
     total[...] = jnp.sum(weights, axis=0, keepdims=True)
-    mixed[...] = dot(v[...], weights.astype(bf16), TN)
-    peak[...] = jnp.zeros_like(peak)
-    good = jnp.where((total[...] > 1e-20) & (total[...] < 1e30), 0.0, 1.0)
-
-    @pl.when(jnp.sum(good) > 0.0)
+    mixed[...] = dot(v[...], low, TN)
+    good = (total[...] > 1e-8) & (total[...] < 1e8)
+
+    @pl.when(jnp.sum(jnp.where(good, 0.0, 1.0)) > 0.0)
     def _():
         again = dot(left, right, NT)
-        top = jnp.max(again, axis=0, keepdims=True)
-        safe = jnp.exp(again - top)
+        safe = jnp.exp(again - jnp.max(again, axis=0, keepdims=True))
+        safe_low = safe.astype(bf16)
+        weights_out[0] = safe_low
         total[...] = jnp.sum(safe, axis=0, keepdims=True)
-        mixed[...] = dot(v[...], safe.astype(bf16), TN)
-        peak[...] = top
-
-    attended[...] = (mixed[...] * (1.0 / total[...])).T.astype(bf16)
-    offset = jnp.broadcast_to(peak[...] + jnp.log(total[...]), (128, rows)).T
-    high, middle, low = split3(-offset)
-    lane = lax.broadcasted_iota(jnp.int32, (rows, 128), 1)
-    extra = query_extra[0].astype(f32)
-    extra = jnp.where(lane == 9, high.astype(f32), extra)
-    extra = jnp.where(lane == 10, middle.astype(f32), extra)
-    extra = jnp.where(lane == 11, low.astype(f32), extra)
-    query_extra_out[0] = extra.astype(bf16)
+        mixed[...] = dot(v[...], safe_low, TN)
+
+    inverse = 1.0 / total[...]
+    attended[...] = (mixed[...] * inverse).T.astype(bf16)
+    inverse_out[0] = inverse
 
 
 def attend(qkv, query_extra, keys_extra, base, heads, prior, rows=1024):
     count = qkv.shape[0]
     return pl.pallas_call(
-        attend_kernel,
+        functools.partial(attend_kernel, base),
         grid=(heads, count // rows),
         in_specs=[
             pl.BlockSpec((rows, 128), lambda h, i: (i, base + h)),
             pl.BlockSpec((count, 128), lambda h, i: (0, HEADS + base + h)),
             pl.BlockSpec((count, 128), lambda h, i: (0, 2 * HEADS + base + h)),
-            pl.BlockSpec((1, rows, 128), lambda h, i: (base + h, i, 0)),
+            pl.BlockSpec((rows, 128), lambda h, i: (i, 0)),
             pl.BlockSpec((count, 128), lambda h, i: (0, 0)),
         ]
         + [pl.BlockSpec(memory_space=pl.ANY) for _ in prior],
         out_specs=[
             pl.BlockSpec((rows, 128), lambda h, i: (i, base + h)),
-            pl.BlockSpec((1, rows, 128), lambda h, i: (base + h, i, 0)),
+            pl.BlockSpec((1, count, rows), lambda h, i: (base + h, 0, i)),
+            pl.BlockSpec((1, 1, rows), lambda h, i: (base + h, 0, i)),
         ],
         out_shape=[
             jax.ShapeDtypeStruct((count, 128 * HEADS), bf16),
-            jax.ShapeDtypeStruct((HEADS, count, 128), bf16),
-        ],
-        scratch_shapes=[pltpu.VMEM((1, rows), f32), pltpu.VMEM((128, rows), f32), pltpu.VMEM((1, rows), f32)],
-        input_output_aliases={5: 0, 6: 1} if prior else {},
-        compiler_params=params(),
-        cost_estimate=cost(heads * 8 * count * count * 128, 6e6, heads * count * count),
+            jax.ShapeDtypeStruct((HEADS, count, count), bf16),
+            jax.ShapeDtypeStruct((HEADS, 1, count), f32),
+        ],
+        scratch_shapes=[pltpu.VMEM((1, rows), f32), pltpu.VMEM((128, rows), f32)],
+        input_output_aliases={5: 0, 6: 1, 7: 2} if prior else {},
+        compiler_params=params("attend"),
+        cost_estimate=cost(heads * 8 * count * count * 128, 6e6 + heads * 8.4e6, heads * count * count),
         name="attend",
     )(qkv, qkv, qkv, query_extra, keys_extra, *prior)
 
@@ -248,9 +252,9 @@
     return jnp.sum(value.reshape(value.shape[0] // 8, 8, value.shape[1]), axis=0)
 
 
-def middle_kernel(masks, order_in, order_out, sub, me_ref, tokens, attended, cotangent, vec, *refs):
+def middle_kernel(masks, order_in, order_out, sub, me_ref, tokens, attended, inverse, cotangent, vec, *refs):
     pieces = refs[: len(masks)]
-    layer_output, grad_first_out, grad_attended_out, grad_extra, keep, send, vec_out = refs[len(masks) : -8]
+    layer_output, grad_branch_out, grad_attended_out, grad_extra, keep, send, vec_out = refs[len(masks) : -8]
     attn_weight, in_weight, out_weight, grad_attn, grad_in, grad_out, sums, hidden_sum = refs[-8:]
     step = pl.program_id(0)
     me = me_ref[0]
@@ -292,6 +296,9 @@
     attn_bias, ffn_bias, gain_one, shift_one, gain_two, shift_two = [row_of(i) for i in range(2, 8)]
     hidden_bias = jnp.concatenate([vec[32 + j : 33 + j, :] for j in range(8)], axis=1)
 
+    inverse_rows = jnp.concatenate([inverse[h] for h in range(HEADS)] + [jnp.zeros((4, tokens.shape[0]), f32)], axis=0)
+    inverse_columns = inverse_rows.T
+
     def chain(s):
         sl = slice(s * sub, (s + 1) * sub)
         att = attended[sl, :]
@@ -331,23 +338,23 @@
         sums[2] += fold8(grad_hidden * normed_one)
         sums[3] += fold8(grad_hidden)
         grad_first = norm_back(grad_hidden * gain_one, normed_one, inverse_one)
-        grad_first_out[sl, :] = grad_first
         grad_branch = grad_first.astype(bf16)
+        grad_branch_out[sl, :] = grad_branch
         sums[0] += fold8(grad_branch.astype(f32))
         yield
-        grad_attended = dot(grad_branch, attn_weight[...], NT).astype(bf16)
+        grad_attended = dot(grad_branch, attn_weight[...], NT)
         grad_attn[...] += dot(att, grad_branch, TN)
         yield
-        grad_attended_out[sl, :] = grad_attended
-        product = grad_attended.astype(f32) * att.astype(f32)
         lane = lax.broadcasted_iota(jnp.int32, (sub, 128), 1)
+        extra = jnp.zeros((sub, 128), f32)
         for h in range(HEADS):
-            centre = jnp.sum(product[:, 128 * h : 128 * (h + 1)], axis=1, keepdims=True)
-            high, middle, low = split3(-centre)
-            extra = jnp.where(lane == 0, high.astype(f32), 0.0)
-            extra = jnp.where(lane == 1, middle.astype(f32), extra)
-            extra = jnp.where(lane == 2, low.astype(f32), extra)
-            grad_extra[h, sl, :] = extra.astype(bf16)
+            cols = slice(128 * h, 128 * (h + 1))
+            scaled = (grad_attended[:, cols] * inverse_columns[sl, h : h + 1]).astype(bf16)
+            grad_attended_out[sl, cols] = scaled
+            centre = jnp.sum(scaled.astype(f32) * att[:, cols].astype(f32), axis=1, keepdims=True)
+            for i, part in enumerate(split3(-centre)):
+                extra = jnp.where(lane == 4 * h + i, part.astype(f32), extra)
+        grad_extra[sl, :] = extra.astype(bf16)
         yield
 
     chains = [chain(s) for s in range(tokens.shape[0] // sub)]
@@ -401,7 +408,7 @@
 
 
 def middle(
-    me, tokens, attended, cotangent, vec, pieces, masks, order_in, order_out, rows=512, sub=256
+    me, tokens, attended, inverse, cotangent, vec, pieces, masks, order_in, order_out, rows=512, sub=256
 ):
     count = tokens.shape[0]
     by_row = pl.BlockSpec((rows, 512), lambda i: (i, 0))
@@ -413,6 +420,7 @@
             scalar_spec(),
             by_row,
             by_row,
+            pl.BlockSpec((HEADS, 1, rows), lambda i: (0, 0, i)),
             by_row,
             whole((48, 128)),
         ]
@@ -421,16 +429,16 @@
             by_row,
             by_row,
             by_row,
-            pl.BlockSpec((HEADS, rows, 128), lambda i: (0, i, 0)),
+            pl.BlockSpec((rows, 128), lambda i: (i, 0)),
             whole((half_rows, 128)),
             whole((half_rows, 128)),
             whole((48, 128)),
         ],
         out_shape=[
             jax.ShapeDtypeStruct((count, 512), bf16),
-            jax.ShapeDtypeStruct((count, 512), f32),
             jax.ShapeDtypeStruct((count, 512), bf16),
-            jax.ShapeDtypeStruct((HEADS, count, 128), bf16),
+            jax.ShapeDtypeStruct((count, 512), bf16),
+            jax.ShapeDtypeStruct((count, 128), bf16),
             jax.ShapeDtypeStruct((half_rows, 128), bf16),
             jax.ShapeDtypeStruct((half_rows, 128), bf16),
             jax.ShapeDtypeStruct((48, 128), f32),
@@ -445,10 +453,10 @@
             pltpu.VMEM((6, 8, 512), f32),
             pltpu.VMEM((8, FF), f32),
         ],
-        compiler_params=params(),
+        compiler_params=params("middle"),
         cost_estimate=cost(6 * count * 1310720, 22e6, 3 * count * FF),
         name="middle",
-    )(me, tokens, attended, cotangent, vec, *pieces)
+    )(me, tokens, attended, inverse, cotangent, vec, *pieces)
 
 
 def attend_back_kernel(
@@ -458,12 +466,11 @@
     vec_width,
     me_ref,
     tokens,
+    weights,
     q,
     k,
     v,
     grad,
-    query_extra,
-    keys_extra,
     grad_extra,
     vec_in,
     grad_query,
@@ -473,8 +480,8 @@
     send,
     vec,
     acc,
-    keys_t,
-    values_t,
+    all_keys,
+    all_values,
     grad_weight,
     held,
     sem,
@@ -491,24 +498,20 @@
         copy.start()
         vec[...] = vec_in[...]
 
+    first_lane = 4 * (base + local)
     lane = lax.broadcasted_iota(jnp.int32, (width, 128), 1)
-    ones = jnp.where(lane < 3, 1.0, 0.0).astype(bf16)
-    scores = dot(
-        jnp.concatenate([q[...], query_extra[0]], axis=1),
-        jnp.concatenate([k[...], keys_extra[...]], axis=1),
-        NT,
+    ones = jnp.where((lane >= first_lane) & (lane < first_lane + 3), 1.0, 0.0).astype(bf16)
+    centred = dot(
+        jnp.concatenate([v[...], ones], axis=1), jnp.concatenate([grad[...], grad_extra[...]], axis=1), NT
     )
-    centred = dot(
-        jnp.concatenate([grad[...], grad_extra[0]], axis=1), jnp.concatenate([v[...], ones], axis=1), NT
-    )
-    probs = jnp.exp(scores)
-    probs_low = probs.astype(bf16)
-    grad_scores = (probs * centred).astype(bf16)
-    keys_t[step] = dot(q[...], grad_scores, TN).astype(bf16)
-    values_t[step] = dot(grad[...], probs_low, TN).astype(bf16)
-    grad_keys[...] = keys_t[step]
-    grad_values[...] = values_t[step]
-    part = dot(grad_scores, k[...], NN)
+    grad_scores = (weights[0].astype(f32) * centred).astype(bf16)
+    gv = dot(weights[0], grad[...], NN).astype(bf16)
+    gk = dot(grad_scores, q[...], NN).astype(bf16)
+    grad_values[...] = gv
+    grad_keys[...] = gk
+    all_values[step] = gv
+    all_keys[step] = gk
+    part = dot(k[...], grad_scores, TN)
 
     @pl.when(step == 0)
     def _():
@@ -527,16 +530,16 @@
         me = me_ref[0]
         scale = 1.0 / math.sqrt(HEAD_DIM)
         x = held[...]
-        gq = acc[...].astype(bf16)
-        grad_query[...] = gq
-        gk = jnp.concatenate([keys_t[i] for i in range(keys_t.shape[0])], axis=1)
-        gv = jnp.concatenate([values_t[i] for i in range(values_t.shape[0])], axis=1)
-        grad_weight[0:512, :] = dot(gq, x, TN).T * scale
-        grad_weight[512:1024, :] = dot(gk, x, NN).T
-        grad_weight[1024:1536, :] = dot(gv, x, NN).T
+        gq_all = acc[...].astype(bf16)
+        grad_query[...] = gq_all
+        gk_all = jnp.concatenate([all_keys[i] for i in range(all_keys.shape[0])], axis=0)
+        gv_all = jnp.concatenate([all_values[i] for i in range(all_values.shape[0])], axis=0)
+        grad_weight[0:512, :] = dot(gq_all, x, NN).T * scale
+        grad_weight[512:1024, :] = dot(gk_all, x, TN).T
+        grad_weight[1024:1536, :] = dot(gv_all, x, TN).T
         row_ones = jnp.ones((8, x.shape[0]), bf16)
-        vec[pl.ds(base + local, 1), :] = dot(row_ones, gq, NN)[0:1] * scale
-        vec[pl.ds(4 + base + local, 1), :] = dot(row_ones, gv, NT)[0:1]
+        vec[pl.ds(base + local, 1), :] = dot(row_ones, gq_all, NT)[0:1] * scale
+        vec[pl.ds(4 + base + local, 1), :] = dot(row_ones, gv_all, NN)[0:1]
         half = BLOCKS // 2
         block = heads * QKV_ROWS + (16 if last else 0)
         for start, ref in ((0, keep), (half, send)):
@@ -555,9 +558,7 @@
             lax.fori_loop(0, half, place, 0)
 
 
-def attend_back(
-    me, tokens, qkv, grad_attended, query_extra, keys_extra, grad_extra, vec, order, vec_width, base, heads, width=512
-):
+def attend_back(me, tokens, weights, qkv, grad_attended, grad_extra, vec, order, vec_width, base, heads, width=1024):
     count = qkv.shape[0]
     half_rows = BLOCKS // 2 * (heads * QKV_ROWS + (16 if base + heads == HEADS else 0))
     return pl.pallas_call(
@@ -566,79 +567,83 @@
         in_specs=[
             scalar_spec(),
             pl.BlockSpec(memory_space=pl.ANY),
+            pl.BlockSpec((1, width, count), lambda h, i: (base + h, i, 0)),
             pl.BlockSpec((count, 128), lambda h, i: (0, base + h)),
             pl.BlockSpec((width, 128), lambda h, i: (i, HEADS + base + h)),
             pl.BlockSpec((width, 128), lambda h, i: (i, 2 * HEADS + base + h)),
             pl.BlockSpec((count, 128), lambda h, i: (0, base + h)),
-            pl.BlockSpec((1, count, 128), lambda h, i: (base + h, 0, 0)),
-            pl.BlockSpec((width, 128), lambda h, i: (i, 0)),
-            pl.BlockSpec((1, count, 128), lambda h, i: (base + h, 0, 0)),
+            whole((count, 128)),
             whole((48, 128)),
         ],
         out_specs=[
-            pl.BlockSpec((count, 128), lambda h, i: (0, h)),
-            pl.BlockSpec((128, width), lambda h, i: (h, i)),
-            pl.BlockSpec((128, width), lambda h, i: (h, i)),
+            pl.BlockSpec((128, count), lambda h, i: (h, 0)),
+            pl.BlockSpec((width, 128), lambda h, i: (i, h)),
+            pl.BlockSpec((width, 128), lambda h, i: (i, h)),
             whole((half_rows, 128)),
             whole((half_rows, 128)),
             whole((48, 128)),
         ],
         out_shape=[
+            jax.ShapeDtypeStruct((128 * heads, count), bf16),
             jax.ShapeDtypeStruct((count, 128 * heads), bf16),
-            jax.ShapeDtypeStruct((128 * heads, count), bf16),
-            jax.ShapeDtypeStruct((128 * heads, count), bf16),
+            jax.ShapeDtypeStruct((count, 128 * heads), bf16),
             jax.ShapeDtypeStruct((half_rows, 128), bf16),
             jax.ShapeDtypeStruct((half_rows, 128), bf16),
             jax.ShapeDtypeStruct((48, 128), f32),
         ],
         scratch_shapes=[
-            pltpu.VMEM((count, 128), f32),
-            pltpu.VMEM((count // width, 128, width), bf16),
-            pltpu.VMEM((count // width, 128, width), bf16),
+            pltpu.VMEM((128, count), f32),
+            pltpu.VMEM((count // width, width, 128), bf16),
+            pltpu.VMEM((count // width, width, 128), bf16),
             pltpu.VMEM((1536, 128), f32),
             pltpu.VMEM((count, 512), bf16),
             pltpu.SemaphoreType.DMA,
         ],
-        compiler_params=params(),
-        cost_estimate=cost(heads * 20 * count * count * 128, heads * 6e6, heads * count * count),
+        compiler_params=params("attend_back"),
+        cost_estimate=cost(heads * 20 * count * count * 128, heads * 12e6, heads * count * count),
         name="attend_back",
-    )(me, tokens, qkv, qkv, qkv, grad_attended, query_extra, keys_extra, grad_extra, vec)
+    )(me, tokens, weights, qkv, qkv, qkv, grad_attended, grad_extra, vec)
 
 
 def input_grad_kernel(groups, *refs):
-    grad_first = refs[0]
+    grad_branch = refs[0]
     queries, keys, values = [refs[1 + i * groups : 1 + (i + 1) * groups] for i in range(3)]
     weight, out = refs[-2], refs[-1]
     scale = 1.0 / math.sqrt(HEAD_DIM)
-    gq = jnp.concatenate([r[...] for r in queries], axis=1)
-    gk = jnp.concatenate([r[...] for r in keys], axis=0)
-    gv = jnp.concatenate([r[...] for r in values], axis=0)
-    total = grad_first[...] + scale * dot(gq, weight[0:512, :], NT)
-    total = total + dot(gk, weight[512:1024, :], TT)
-    out[...] = total + dot(gv, weight[1024:1536, :], TT)
-
-
-def input_grad(grad_first, queries, keys, values, weight, rows=512):
-    count = grad_first.shape[0]
+    gq = jnp.concatenate([r[...] for r in queries], axis=0)
+    gk = jnp.concatenate([r[...] for r in keys], axis=1)
+    gv = jnp.concatenate([r[...] for r in values], axis=1)
+    total = grad_branch[...].astype(f32) + scale * dot(gq, weight[0:512, :], TT)
+    total = total + dot(gk, weight[512:1024, :], NT)
+    out[...] = total + dot(gv, weight[1024:1536, :], NT)
+
+
+def input_grad(grad_branch, queries, keys, values, weight, rows=512):
+    count = grad_branch.shape[0]
     by_row = pl.BlockSpec((rows, 512), lambda i: (i, 0))
     return pl.pallas_call(
         functools.partial(input_grad_kernel, len(queries)),
         grid=(count // rows,),
         in_specs=[by_row]
-        + [pl.BlockSpec((rows, a.shape[1]), lambda i: (i, 0)) for a in queries]
-        + [pl.BlockSpec((a.shape[0], rows), lambda i: (0, i)) for a in keys + values]
+        + [pl.BlockSpec((a.shape[0], rows), lambda i: (0, i)) for a in queries]
+        + [pl.BlockSpec((rows, a.shape[1]), lambda i: (i, 0)) for a in keys + values]
         + [whole((1536, 512))],
         out_specs=by_row,
         out_shape=jax.ShapeDtypeStruct((count, 512), f32),
-        compiler_params=params(),
+        compiler_params=params("input_grad"),
         cost_estimate=cost(2 * count * 512 * 1536, 16e6),
         name="input_grad",
-    )(grad_first, *queries, *keys, *values, weight)
-
-
-def unpack_kernel(vec_width, me_ref, q_keep, q_got, r_keep, r_got, out, vec_out):
-    q_sum = q_keep[...] + q_got[...].astype(f32)
-    r_sum = r_keep[...] + r_got[...].astype(f32)
+    )(grad_branch, *queries, *keys, *values, weight)
+
+
+def unpack_kernel(vec_width, me_ref, *refs):
+    q_parts, r_parts = refs[:4], refs[4:6]
+    out, vec_out, line = refs[6:]
+    q_sum, r_sum = q_parts[0][...], r_parts[0][...]
+    for part in q_parts[1:]:
+        q_sum = q_sum + part[...].astype(f32)
+    for part in r_parts[1:]:
+        r_sum = r_sum + part[...].astype(f32)
     at = 0
     source = q_sum
     for index, (start, rows, count) in enumerate(PANELS):
@@ -648,17 +653,20 @@
             out[pl.ds(start + j, rows, stride=count), :] = source[at : at + rows, :]
             at += rows
     pair = jnp.concatenate([q_sum[192:200, :], q_sum[193:201, :]], axis=1)
-    vec_out[...] = pltpu.roll(pair, 256 - (me_ref[0] * vec_width) % 128, 1)
-
-
-def unpack(me, q_keep, q_got, r_keep, r_got, vec_width):
+    line[...] = pltpu.roll(pair, 256 - (me_ref[0] * vec_width) % 128, 1)
+    vec_out[...] = line[0:1, 0:vec_width]
+
+
+def unpack(me, q_parts, r_parts, vec_width):
     vmem = pl.BlockSpec(memory_space=pltpu.VMEM)
     return pl.pallas_call(
         functools.partial(unpack_kernel, vec_width),
-        in_specs=[scalar_spec()] + [vmem] * 4,
-        out_shape=[jax.ShapeDtypeStruct((512, 128), f32), jax.ShapeDtypeStruct((8, 256), f32)],
+        in_specs=[scalar_spec()] + [vmem] * 6,
+        out_shape=[jax.ShapeDtypeStruct((512, 128), f32), jax.ShapeDtypeStruct((1, vec_width), f32)],
+        scratch_shapes=[pltpu.VMEM((8, 256), f32)],
+        compiler_params=params("unpack"),
         name="unpack",
-    )(me, q_keep, q_got, r_keep, r_got)
+    )(me, *q_parts, *r_parts)
 
 
 def swap(array, step, count):
@@ -670,29 +678,35 @@
 
 
 def quarters(groups):
-    totals = []
+    parts = []
     for keep, got in groups:
-        total = keep.astype(f32) + got.astype(f32)
-        totals.append(total.reshape(4, 4, -1, 128))
-    total = jnp.concatenate(totals, axis=2) if len(totals) > 1 else totals[0]
-    return total[0], [total[i].astype(bf16).reshape(-1, 128) for i in range(1, 4)]
-
-
-def halves(keep, gots, blocks):
+        keep, got = keep.reshape(4, 4, -1, 128), got.reshape(4, 4, -1, 128)
+        parts.append([keep[i].astype(f32) + got[i].astype(f32) for i in range(4)])
+    totals = [jnp.concatenate(same, axis=1) if len(same) > 1 else same[0] for same in zip(*parts)]
+    return totals[0], [total.astype(bf16).reshape(-1, 128) for total in totals[1:]]
+
+
+def halves(keep, gots):
     total = keep
     for got in gots:
         total = total + got.astype(f32).reshape(keep.shape)
-    rows = blocks // 2
-    return total[:rows], total[rows:].astype(bf16).reshape(-1, 128)
+    half = total.shape[0] // 2
+    return total[:half], total[half:].astype(bf16).reshape(-1, 128)
+
+
+def fourths(keep, gots):
+    total = keep
+    for got in gots:
+        total = total + got.astype(f32).reshape(keep.shape)
+    return [total[0]] + [total[i].astype(bf16) for i in range(1, 4)]
 
 
 def fast_layout(dp, fsdp):
     return dp == 4 and fsdp == 8
 
 
-def gather_far(block, z_far, z_near, count):
-    block = jnp.concatenate([block, swap(block, z_far, count)], axis=0)
-    return jnp.concatenate([block, swap(block, z_near, count)], axis=0)
+def gather_line(block, steps, count):
+    return jnp.concatenate([block] + [swap(block, step, count) for step in steps], axis=0)
 
 
 def body(dp, fsdp, tokens, lengths, assignment, weights, vectors, cotangent):
@@ -706,21 +720,24 @@
         vec_width = vectors.shape[0]
         core, x_step, y_step, z_near, z_far = fsdp, 1, 2 * fsdp, 2, 4
         planes = [x_step, y_step, x_step + y_step]
-        order_in = [z_far, z_near]
-        order_out = [z_far, z_near, x_step, y_step, core]
+        line = [z_near, z_far, z_near + z_far]
+        order_in, order_rest = [z_near, z_far], [z_far, z_near]
+        order_out = [z_near, z_far, x_step, y_step, core]
+        order_rest_out = order_rest + order_out[2:]
         masks = [0] + planes
         masks = masks + [m + core for m in masks]
         me = owner[None]
-        padded = jnp.pad(vectors, (0, 256 - vec_width)).reshape(1, 256)
-        q_block, r_block = pack(me, weights.reshape(512, 128), jnp.broadcast_to(padded, (16, 256)), vec_width)
-        q_far = gather_far(q_block, z_far, z_near, count)
+        q_block, r_block = pack(me, weights.reshape(512, 128), vectors.reshape(1, vec_width), vec_width)
+        q_far = gather_line(q_block, line, count)
         q_pieces = [q_far] + [swap(q_far, step, count) for step in planes]
         q_pieces = q_pieces + [swap(piece, core, count) for piece in q_pieces]
-        r_far = gather_far(after(r_block, q_far), z_far, z_near, count)
+        r_far = gather_line(after(r_block, q_far), [z_far], count)
+        r_far = gather_line(r_far, [z_near], count)
         r_pieces = [swap(after(r_far, *q_pieces), step, count) for step in planes]
     else:
         vec_width = 160
-        order_in, order_out = [1, 2], [1, 2, 4, 8, 16]
+        order_in, order_rest, order_out = [1, 2], [1, 2], [1, 2, 4, 8, 16]
+        order_rest_out = order_out
         masks = [4 * i for i in range(8)]
         me = jnp.zeros((1,), jnp.int32)
         blocks = lax.all_gather(weights, AXES, axis=0, tiled=True).reshape(count, -1)
@@ -751,27 +768,16 @@
         r_pieces = [r_far] + [after(piece, prior[0]) for piece in r_pieces]
         keys_extra = after(keys_extra, *r_pieces)
         r_pieces = r_pieces + [swap(piece, core, count) for piece in r_pieces]
-    attended, query_extra = attend(qkv, query_extra, keys_extra, 2, 2, prior)
-    layer_output, grad_first, grad_attended, grad_extra, r_keep, r_send, vec_grad = middle(
-        me, tokens, attended, cotangent, vec, r_pieces, masks, order_in, order_out
+    attended, probs, inverse = attend(qkv, query_extra, keys_extra, 2, 2, prior)
+    layer_output, grad_branch, grad_attended, grad_extra, r_keep, r_send, vec_grad = middle(
+        me, tokens, attended, inverse, cotangent, vec, r_pieces, masks, order_rest, order_rest_out
     )
     queries, keys, values, keeps, sends, gots = [], [], [], [], [], []
     if fast:
         r_got = swap(r_send, core, count)
     for base, heads in ((0, 1), (1, 2), (3, 1)):
         gq, gk, gv, keep, send, vec_grad = attend_back(
-            me,
-            tokens,
-            qkv,
-            grad_attended,
-            query_extra,
-            keys_extra,
-            grad_extra,
-            vec_grad,
-            order_out,
-            vec_width,
-            base,
-            heads,
+            me, tokens, probs, qkv, grad_attended, grad_extra, vec_grad, order_out, vec_width, base, heads
         )
         queries.append(gq)
         keys.append(gk)
@@ -787,27 +793,24 @@
             r_gots = [swap(part, step, count) for part, step in zip(r_sends, planes)]
         elif base == 1:
             r_gots = [after(part, gq) for part in r_gots]
-            r_keep, r_send = halves(r_keep, r_gots, 4)
+            r_keep, r_send = halves(r_keep, r_gots)
             vec_grad = after(vec_grad, r_send)
             r_got = swap(r_send, z_near, count)
     if fast:
-        r_keep, r_send = halves(r_keep, [after(r_got, gq)], 2)
-        r_got = swap(r_send, z_far, count)
+        r_keep, r_send = halves(r_keep, [after(r_got, gq)])
+        r_parts = [r_keep.reshape(-1, 128), swap(r_send, z_far, count)]
+        gots = [after(got, gq) for got in gots]
         q_keep, q_sends = quarters(list(zip(keeps, gots)))
-        grad_first = after(grad_first, *q_sends)
+        grad_branch = after(grad_branch, *q_sends)
         q_gots = [swap(part, step, count) for part, step in zip(q_sends, planes)]
-    grad_tokens = input_grad(grad_first, queries, keys, values, weight)
+    grad_tokens = input_grad(grad_branch, queries, keys, values, weight)
     if fast:
         q_gots = [after(part, grad_tokens) for part in q_gots]
-        q_keep, q_send = halves(q_keep, q_gots, 4)
-        q_got = swap(q_send, z_near, count)
-        q_keep, q_send = halves(q_keep, [q_got], 2)
-        q_got = swap(q_send, z_far, count)
-        own_weights, own_vec = unpack(
-            me, q_keep.reshape(-1, 128), q_got, r_keep.reshape(-1, 128), r_got, vec_width
-        )
+        q_parts = fourths(q_keep, q_gots)
+        q_parts = q_parts[:1] + [swap(part, step, count) for part, step in zip(q_parts[1:], line)]
+        own_weights, own_vectors = unpack(me, q_parts, r_parts, vec_width)
         own_weights = own_weights.reshape(-1)
-        own_vectors = own_vec[0, :vec_width]
+        own_vectors = own_vectors.reshape(-1)
     else:
         heads = [jnp.concatenate([k, g], axis=0).astype(f32).reshape(BLOCKS, -1, 128) for k, g in zip(keeps, sends)]
         q_all = jnp.concatenate(heads, axis=1)

time: 204 us -> 186 us (0.912)
  local copies, waits for them, and re-layouts: 10.8 us -> 3.5 us
  other arithmetic: 8.9 us -> 2.67 us
    pallas_call x2, Pallas kernels: 22.5 us -> 42.6 us  [attend(): pl.pallas_call(functools.partial(attend_kernel, base), grid=(heads, count...]
    pallas_call x3, Pallas kernels: 56.5 us -> 47.8 us  [attend_back(): pl.pallas_call(functools.partial(attend_back_kernel, base, heads, order,...]
    pallas_call x1, Pallas kernels: 8.67 us -> 4.62 us  [project(): pl.pallas_call(functools.partial(project_kernel, masks, order, vec_width)...]
    pallas_call x1, Pallas kernels: 9.36 us -> 5.35 us  [input_grad(): pl.pallas_call(functools.partial(input_grad_kernel, len(queries)), grid=(...]
    pallas_call x1, Pallas kernels: 30.1 us -> 26.8 us  [middle(): pl.pallas_call(functools.partial(middle_kernel, masks, order_in, order_ou...]
    unnamed x54 -> x13, local copies, waits for them, and re-layouts: 5.6 us -> 2.55 us
    slice x8 -> x4, local copies, waits for them, and re-layouts: 3.16 us -> 0.12 us  [the longest x1 1.26 us: body(): own_vectors = own_vec[0, :vec_width]]
    add x4 -> x3, other arithmetic: 3.16 us -> 0.22 us  [quarters(): parts.append([keep[i].astype(f32) + got[i].astype(f32) for i in range(4)])]
  transfers between devices with their start and end apart: 32 -> 34, of which waited for: 13 -> 11; matrix products, arithmetic and copies ran while one was open for 4% -> 2% of each run, Pallas kernels for 48% -> 54%
where the time goes in v3:
time: 186 us
  Pallas kernels  128 us (69%)
  starting transfers between devices  30.2 us (16%)
  waiting for transfers between devices  20.9 us (11%)
  local copies, waits for them, and re-layouts  3.5 us (2%)
  other arithmetic  2.67 us (1%)
    pallas_call x3, Pallas kernels, attend_back(): pl.pallas_call(functools.partial(attend_back_kernel, base, heads, order,...  47.8 us
    pallas_call x2, Pallas kernels, attend(): pl.pallas_call(functools.partial(attend_kernel, base), grid=(heads, count...  42.6 us
    ppermute x34, starting transfers between devices, swap(): return lax.ppermute(array, AXES, [(i, i ^ step) for i in range(count)])  30.2 us
    pallas_call x1, Pallas kernels, middle(): pl.pallas_call(functools.partial(middle_kernel, masks, order_in, order_ou...  26.8 us
    ppermute x34, waiting for transfers between devices, swap(): return lax.ppermute(array, AXES, [(i, i ^ step) for i in range(count)])  20.9 us
    pallas_call x1, Pallas kernels, input_grad(): pl.pallas_call(functools.partial(input_grad_kernel, len(queries)), grid=(...  5.35 us
    pallas_call x1, Pallas kernels, project(): pl.pallas_call(functools.partial(project_kernel, masks, order, vec_width)...  4.62 us
  transfers between devices with their start and end apart: 34, of which 11 were waited for; matrix products, arithmetic and copies ran while one was open for 2% of the time, Pallas kernels for 54%

profile of v3, /device:TPU:0, one launch (start us, length us, event | category | flops | bytes accessed | tf_op | source)
XLA Modules:
  0.0 186.2 jit_solution(6448360756757242878)
XLA Ops:
  0.6 0.7 reshape.215.vec
  1.3 0.9 copy-done.2
  2.3 3.1 %collective-permute-start = (bf16[208,128]{1,0:T(8,128)(2,1)S(1)}, bf16[208,128]{1,0:T(8,128)(2,1)S(1)}, u32[]{:S(2)}, u32[]{:S(2)}) collective-permute-start(bf16[208,128]{1,0:T(8,128)(2,1)S(1)} %get-tuple-element.63), channel_id=1, source_target_pairs={{0,2},{1,3},{2,0},{3,1},{4,6},{5,7},{6,4},{7,5},{8,10},{9,11},{10,... | collective-permute-start | bytes 159752 | tf_op jit(solution)/shard_map/ppermute | solution.py:673
  5.3 2.6 %collective-permute-start.1 = (bf16[208,128]{1,0:T(8,128)(2,1)S(1)}, bf16[208,128]{1,0:T(8,128)(2,1)S(1)}, u32[]{:S(2)}, u32[]{:S(2)}) collective-permute-start(bf16[208,128]{1,0:T(8,128)(2,1)S(1)} %get-tuple-element.63), channel_id=1, source_target_pairs={{0,4},{1,5},{2,6},{3,7},{4,0},{5,1},{6,2},{7,3},{8,12},{9,13},{10,... | collective-permute-start | bytes 159752 | tf_op jit(solution)/shard_map/ppermute | solution.py:673
  7.9 0.7 select_bitcast_fusion
  9.2 2.2 %collective-permute-done.1 = bf16[208,128]{1,0:T(8,128)(2,1)S(1)} collective-permute-done((bf16[208,128]{1,0:T(8,128)(2,1)S(1)}, bf16[208,128]{1,0:T(8,128)(2,1)S(1)}, u32[]{:S(2)}, u32[]{:S(2)}) %collective-permute-start.1) | collective-permute-done | bytes 53280 | tf_op jit(solution)/shard_map/ppermute | solution.py:673
  11.4 2.5 %collective-permute-done.2 = bf16[208,128]{1,0:T(8,128)(2,1)S(1)} collective-permute-done((bf16[208,128]{1,0:T(8,128)(2,1)S(1)}, bf16[208,128]{1,0:T(8,128)(2,1)S(1)}, u32[]{:S(2)}, u32[]{:S(2)}) %collective-permute-start.2) | collective-permute-done | bytes 53280 | tf_op jit(solution)/shard_map/ppermute | solution.py:673
  13.9 0.7 collective-permute-start.10
  14.6 0.7 bitcast_select_fusion
  15.4 1.5 collective-permute-start.3
  16.8 1.5 collective-permute-start.4
  18.4 0.5 collective-permute-start.5
  18.8 0.4 collective-permute-done.10
  19.3 0.6 collective-permute-start.11
  19.9 2.7 %collective-permute-done.3.refs_1_ = bf16[832,128]{1,0:T(8,128)(2,1)S(1)} collective-permute-done((bf16[832,128]{1,0:T(8,128)(2,1)S(1)}, bf16[832,128]{1,0:T(8,128)(2,1)S(1)}, u32[]{:S(2)}, u32[]{:S(2)}) %collective-permute-start.3) | collective-permute-done | bytes 213024 | tf_op jit(solution)/shard_map/ppermute | solution.py:673
  22.5 3.5 %collective-permute-done.4.refs_2_ = bf16[832,128]{1,0:T(8,128)(2,1)S(1)} collective-permute-done((bf16[832,128]{1,0:T(8,128)(2,1)S(1)}, bf16[832,128]{1,0:T(8,128)(2,1)S(1)}, u32[]{:S(2)}, u32[]{:S(2)}) %collective-permute-start.4) | collective-permute-done | bytes 213024 | tf_op jit(solution)/shard_map/ppermute | solution.py:673
  26.0 0.5 collective-permute-start.9
  26.7 0.8 collective-permute-done.8.refs_6_
  27.8 1.3 collective-permute-start.14
  29.1 0.9 collective-permute-start.13
  30.0 1.3 collective-permute-start.12
  31.3 1.6 copy-done
  32.9 4.6 %project.1 = (bf16[2048,1536]{1,0:T(8,128)(2,1)S(1)}, bf16[2048,128]{1,0:T(8,128)(2,1)S(1)}, bf16[2048,128]{1,0:T(8,128)(2,1)S(1)}, f32[48,128]{1,0:T(8,128)S(1)}, bf16[1536,512]{1,0:T(8,128)(2,1)S(1)}) custom-call(s32[1]{0:T(128)} %bitcast.me_ref, s32[1,256]{1,0:T(1,128)S(1)} %bitcast.39, bf16[2048,512]{1,0:T(8,128)(2,1)S(1)} %copy-done, ...), custom_call_target="tpu_custom_call" | custom-call | flops 3221225472 | bytes 12000000 | tf_op jit(solution)/shard_map/project/pallas_call | solution.py:147
  37.5 21.3 %attend.2 = (bf16[2048,512]{1,0:T(8,128)(2,1)S(1)}, bf16[4,2048,2048]{2,1,0:T(8,128)(2,1)}, f32[4,1,2048]{2,1,0:T(1,128)S(1)}) custom-call(bf16[2048,1536]{1,0:T(8,128)(2,1)S(1)} %get-tuple-element.64.q.k.v, bf16[2048,1536]{1,0:T(8,128)(2,1)S(1)} %get-tuple-element.64.q.k.v, bf16[2048,1536]{1,0:T(8,128)(2,1)S(1)} %get-tuple-element.64.q.k.v, ...), custom_call_target="tpu_custom_call" | custom-call | flops 8589934592 | bytes 22800000 | tf_op jit(solution)/shard_map/attend/pallas_call | solution.py:208
  58.9 0.5 collective-permute-start.17
  59.5 21.3 %attend.3 = (bf16[2048,512]{1,0:T(8,128)(2,1)S(1)}, bf16[4,2048,2048]{2,1,0:T(8,128)(2,1)}, f32[4,1,2048]{2,1,0:T(1,128)S(1)}) custom-call(bf16[2048,1536]{1,0:T(8,128)(2,1)S(1)} %get-tuple-element.64.q.k.v, bf16[2048,1536]{1,0:T(8,128)(2,1)S(1)} %get-tuple-element.64.q.k.v, ...), custom_call_target="tpu_custom_call", output_to_operand_aliasing={{0}: (5, {}), {1}: (6, {}), {2}: (7, {})} | custom-call | flops 8589934592 | bytes 22800000 | tf_op jit(solution)/shard_map/attend/pallas_call | solution.py:208
  80.8 26.8 %middle.1 = (bf16[2048,512]{1,0:T(8,128)(2,1)}, bf16[2048,512]{1,0:T(8,128)(2,1)S(1)}, bf16[2048,512]{1,0:T(8,128)(2,1)S(1)}, bf16[2048,128]{1,0:T(8,128)(2,1)S(...) custom-call(s32[1]{0:T(128)} %bitcast.me_ref, ...), custom_call_target="tpu_custom_call" | custom-call | flops 16106127360 | bytes 22000000 | tf_op jit(solution)/shard_map/middle/pallas_call | solution.py:416
  107.6 0.4 collective-permute-start.20
  108.0 12.1 %attend_back.3 = (bf16[128,2048]{1,0:T(8,128)(2,1)S(1)}, bf16[2048,128]{1,0:T(8,128)(2,1)S(1)}, bf16[2048,128]{1,0:T(8,128)(2,1)S(1)}, bf16[768,128]{1,0:T(8,128...) custom-call(s32[1]{0:T(128)} %bitcast.me_ref, bf16[2048,512]{1,0:T(8,128)(2,1)S(1)} %copy-done.1, ...), custom_call_target="tpu_custom_call" | custom-call | flops 10737418240 | bytes 12000000 | tf_op jit(solution)/shard_map/attend_back/pallas_call | solution.py:564
  120.5 0.8 collective-permute-start.21
  121.4 1.1 collective-permute-start.22
  122.5 1.6 collective-permute-start.23
  124.1 22.8 %attend_back.4 = (bf16[256,2048]{1,0:T(8,128)(2,1)S(1)}, bf16[2048,256]{1,0:T(8,128)(2,1)S(1)}, bf16[2048,256]{1,0:T(8,128)(2,1)S(1)}, bf16[1536,128]{1,0:T(8,12...) custom-call(s32[1]{0:T(128)} %bitcast.me_ref, bf16[2048,512]{1,0:T(8,128)(2,1)S(1)} %copy-done.1, ...), custom_call_target="tpu_custom_call" | custom-call | flops 21474836480 | bytes 24000000 | tf_op jit(solution)/shard_map/attend_back/pallas_call | solution.py:564
  147.2 1.2 collective-permute-start.32
  148.4 12.9 %attend_back.5 = (bf16[128,2048]{1,0:T(8,128)(2,1)S(1)}, bf16[2048,128]{1,0:T(8,128)(2,1)S(1)}, bf16[2048,128]{1,0:T(8,128)(2,1)S(1)}, bf16[1024,128]{1,0:T(8,12...) custom-call(s32[1]{0:T(128)} %bitcast.me_ref, bf16[2048,512]{1,0:T(8,128)(2,1)S(1)} %copy-done.1, ...), custom_call_target="tpu_custom_call" | custom-call | flops 10737418240 | bytes 12000000 | tf_op jit(solution)/shard_map/attend_back/pallas_call | solution.py:564
  161.8 1.3 collective-permute-start.33
  163.2 0.7 collective-permute-start.26
  163.9 1.5 collective-permute-start.27
  165.4 1.5 collective-permute-start.28
  166.9 5.3 %input_grad.1 = f32[2048,512]{1,0:T(8,128)} custom-call(bf16[2048,512]{1,0:T(8,128)(2,1)S(1)} %get-tuple-element.108.refs_0_, bf16[128,2048]{1,0:T(8,128)(2,1)S(1)} %get-tuple-element.91.refs_1_, bf16[256,2048]{1,0:T(8,128)(2,1)S(1)} %get-tuple-element.95.refs_2_, bf16[128,2048]{1,0:T(8,128)(2,1)S(1)} %get-tuple-element.100.refs_3_, ...), custom_call_target="tpu_custom_call" | custom-call | flops 3221225472 | bytes 16000000 | tf_op jit(solution)/shard_map/input_grad/pallas_call | solution.py:624
  172.3 2.1 %collective-permute-done.27 = bf16[832,128]{1,0:T(8,128)(2,1)S(1)} collective-permute-done((bf16[832,128]{1,0:T(8,128)(2,1)S(1)}, bf16[832,128]{1,0:T(8,128)(2,1)S(1)}, u32[]{:S(2)}, u32[]{:S(2)}) %collective-permute-start.27) | collective-permute-done | bytes 213024 | tf_op jit(solution)/shard_map/ppermute | solution.py:673
  174.4 1.8 collective-permute-done.28
  176.3 2.0 %collective-permute-start.29 = (bf16[208,128]{1,0:T(8,128)(2,1)S(1)}, bf16[208,128]{1,0:T(8,128)(2,1)S(1)}, u32[]{:S(2)}, u32[]{:S(2)}) collective-permute-start(bf16[208,128]{1,0:T(8,128)(2,1)S(1)} %get-tuple-element.141), channel_id=1, source_target_pairs={{0,2},{1,3},{2,0},{3,1},{4,6},{5,7},{6,4},{7,5},{8,10},{9,11},{10,... | collective-permute-start | bytes 159752 | tf_op jit(solution)/shard_map/ppermute | solution.py:673
  178.4 1.2 collective-permute-start.30
  179.5 1.3 collective-permute-start.31
  180.8 3.2 %collective-permute-done.30.refs_2_ = bf16[208,128]{1,0:T(8,128)(2,1)S(1)} collective-permute-done((bf16[208,128]{1,0:T(8,128)(2,1)S(1)}, bf16[208,128]{1,0:T(8,128)(2,1)S(1)}, u32[]{:S(2)}, u32[]{:S(2)}) %collective-permute-start.30) | collective-permute-done | bytes 53280 | tf_op jit(solution)/shard_map/ppermute | solution.py:673
  184.0 1.4 collective-permute-done.31.refs_3_
  185.5 0.8 unpack.1
  (68 shorter events, 2.7 us)
Async XLA Ops:
  1.3 0.9 copy-start.2
  2.3 6.9 %collective-permute-start = (bf16[208,128]{1,0:T(8,128)(2,1)S(1)}, bf16[208,128]{1,0:T(8,128)(2,1)S(1)}, u32[]{:S(2)}, u32[]{:S(2)}) collective-permute-start(bf16[208,128]{1,0:T(8,128)(2,1)S(1)} %get-tuple-element.63), channel_id=1, source_target_pairs={{0,2},{1,3},{2,0},{3,1},{4,6},{5,7},{6,4},{7,5},{8,10},{9,11},{10,... | collective-permute-start | bytes 159752 | tf_op jit(solution)/shard_map/ppermute | solution.py:673
  5.3 6.1 %collective-permute-start.1 = (bf16[208,128]{1,0:T(8,128)(2,1)S(1)}, bf16[208,128]{1,0:T(8,128)(2,1)S(1)}, u32[]{:S(2)}, u32[]{:S(2)}) collective-permute-start(bf16[208,128]{1,0:T(8,128)(2,1)S(1)} %get-tuple-element.63), channel_id=1, source_target_pairs={{0,4},{1,5},{2,6},{3,7},{4,0},{5,1},{6,2},{7,3},{8,12},{9,13},{10,... | collective-permute-start | bytes 159752 | tf_op jit(solution)/shard_map/ppermute | solution.py:673
  7.9 5.9 %collective-permute-start.2 = (bf16[208,128]{1,0:T(8,128)(2,1)S(1)}, bf16[208,128]{1,0:T(8,128)(2,1)S(1)}, u32[]{:S(2)}, u32[]{:S(2)}) collective-permute-start(bf16[208,128]{1,0:T(8,128)(2,1)S(1)} %get-tuple-element.63), channel_id=1, source_target_pairs={{0,6},{1,7},{2,4},{3,5},{4,2},{5,3},{6,0},{7,1},{8,14},{9,15},{10,... | collective-permute-start | bytes 159752 | tf_op jit(solution)/shard_map/ppermute | solution.py:673
  13.9 5.4 %collective-permute-start.10 = (bf16[320,128]{1,0:T(8,128)(2,1)S(1)}, bf16[320,128]{1,0:T(8,128)(2,1)S(1)}, u32[]{:S(2)}, u32[]{:S(2)}) collective-permute-start(bf16[320,128]{1,0:T(8,128)(2,1)S(1)} %get-tuple-element.68), channel_id=1, source_target_pairs={{0,4},{1,5},{2,6},{3,7},{4,0},{5,1},{6,2},{7,3},{8,12},{9,13},{10,... | collective-permute-start | bytes 245768 | tf_op jit(solution)/shard_map/ppermute | solution.py:673
  15.4 7.2 %collective-permute-start.3 = (bf16[832,128]{1,0:T(8,128)(2,1)S(1)}, bf16[832,128]{1,0:T(8,128)(2,1)S(1)}, u32[]{:S(2)}, u32[]{:S(2)}) collective-permute-start(bf16[832,128]{1,0:T(8,128)(2,1)S(1)} %constant_dynamic-update-slice_fusion.refs_0_), channel_id=1, source_target_pairs={{0,1},{1,0},{2,3},{3,2},{4,5},{5,4},{6,7},{7,6},{8,9},{9,8},{10,11... | collective-permute-start | bytes 638984 | tf_op jit(solution)/shard_map/ppermute | solution.py:673
  16.8 9.2 %collective-permute-start.4 = (bf16[832,128]{1,0:T(8,128)(2,1)S(1)}, bf16[832,128]{1,0:T(8,128)(2,1)S(1)}, u32[]{:S(2)}, u32[]{:S(2)}) collective-permute-start(bf16[832,128]{1,0:T(8,128)(2,1)S(1)} %constant_dynamic-update-slice_fusion.refs_0_), channel_id=1, source_target_pairs={{0,16},{1,17},{2,18},{3,19},{4,20},{5,21},{6,22},{7,23},{8,24},{9,... | collective-permute-start | bytes 638984 | tf_op jit(solution)/shard_map/ppermute | solution.py:673
  18.4 7.7 %collective-permute-start.5 = (bf16[832,128]{1,0:T(8,128)(2,1)S(1)}, bf16[832,128]{1,0:T(8,128)(2,1)S(1)}, u32[]{:S(2)}, u32[]{:S(2)}) collective-permute-start(bf16[832,128]{1,0:T(8,128)(2,1)S(1)} %constant_dynamic-update-slice_fusion.refs_0_), channel_id=1, source_target_pairs={{0,17},{1,16},{2,19},{3,18},{4,21},{5,20},{6,23},{7,22},{8,25},{9,... | collective-permute-start | bytes 638984 | tf_op jit(solution)/shard_map/ppermute | solution.py:673
  18.8 7.8 %collective-permute-start.6 = (bf16[832,128]{1,0:T(8,128)(2,1)S(1)}, bf16[832,128]{1,0:T(8,128)(2,1)S(1)}, u32[]{:S(2)}, u32[]{:S(2)}) collective-permute-start(bf16[832,128]{1,0:T(8,128)(2,1)S(1)} %constant_dynamic-update-slice_fusion.refs_0_), channel_id=1, source_target_pairs={{0,8},{1,9},{2,10},{3,11},{4,12},{5,13},{6,14},{7,15},{8,0},{9,1},... | collective-permute-start | bytes 638984 | tf_op jit(solution)/shard_map/ppermute | solution.py:673
  19.3 7.3 %collective-permute-start.11 = (bf16[640,128]{1,0:T(8,128)(2,1)S(1)}, bf16[640,128]{1,0:T(8,128)(2,1)S(1)}, u32[]{:S(2)}, u32[]{:S(2)}) collective-permute-start(bf16[640,128]{1,0:T(8,128)(2,1)S(1)} %pad_maximum_fusion.3), channel_id=1, source_target_pairs={{0,2},{1,3},{2,0},{3,1},{4,6},{5,7},{6,4},{7,5},{8,10},{9,11},{10,... | collective-permute-start | bytes 491528 | tf_op jit(solution)/shard_map/ppermute | solution.py:673
  22.5 4.2 %collective-permute-start.7 = (bf16[832,128]{1,0:T(8,128)(2,1)S(1)}, bf16[832,128]{1,0:T(8,128)(2,1)S(1)}, u32[]{:S(2)}, u32[]{:S(2)}) collective-permute-start(bf16[832,128]{1,0:T(8,128)(2,1)S(1)} %collective-permute-done.3.refs_1_), channel_id=1, source_target_pairs={{0,8},{1,9},{2,10},{3,11},{4,12},{5,13},{6,14},{7,15},{8,0},{9,1},... | collective-permute-start | bytes 638984 | tf_op jit(solution)/shard_map/ppermute | solution.py:673
  26.0 1.5 collective-permute-start.8
  26.0 1.8 collective-permute-start.9
  26.6 54.2 %collective-permute-start.15 = (bf16[1280,128]{1,0:T(8,128)(2,1)S(1)}, bf16[1280,128]{1,0:T(8,128)(2,1)S(1)}, u32[]{:S(2)}, u32[]{:S(2)}) collective-permute-start(bf16[1280,128]{1,0:T(8,128)(2,1)S(1)} %constant_dynamic-update-slice_fusion.4.refs_0_), channel_id=1, source_target_pairs={{0,8},{1,9},{2,10},{3,11},{4,12},{5,13},{6,14},{7,15},{8,0},{9,1},... | collective-permute-start | bytes 983048 | tf_op jit(solution)/shard_map/ppermute | solution.py:673
  27.8 31.0 %collective-permute-start.14 = (bf16[1280,128]{1,0:T(8,128)(2,1)S(1)}, bf16[1280,128]{1,0:T(8,128)(2,1)S(1)}, u32[]{:S(2)}, u32[]{:S(2)}) collective-permute-start(bf16[1280,128]{1,0:T(8,128)(2,1)S(1)} %constant_dynamic-update-slice_fusion.4.refs_0_), channel_id=1, source_target_pairs={{0,17},{1,16},{2,19},{3,18},{4,21},{5,20},{6,23},{7,22},{8,25},{9,... | collective-permute-start | bytes 983048 | tf_op jit(solution)/shard_map/ppermute | solution.py:673
  29.1 29.7 %collective-permute-start.13 = (bf16[1280,128]{1,0:T(8,128)(2,1)S(1)}, bf16[1280,128]{1,0:T(8,128)(2,1)S(1)}, u32[]{:S(2)}, u32[]{:S(2)}) collective-permute-start(bf16[1280,128]{1,0:T(8,128)(2,1)S(1)} %constant_dynamic-update-slice_fusion.4.refs_0_), channel_id=1, source_target_pairs={{0,16},{1,17},{2,18},{3,19},{4,20},{5,21},{6,22},{7,23},{8,24},{9,... | collective-permute-start | bytes 983048 | tf_op jit(solution)/shard_map/ppermute | solution.py:673
  30.0 28.8 %collective-permute-start.12 = (bf16[1280,128]{1,0:T(8,128)(2,1)S(1)}, bf16[1280,128]{1,0:T(8,128)(2,1)S(1)}, u32[]{:S(2)}, u32[]{:S(2)}) collective-permute-start(bf16[1280,128]{1,0:T(8,128)(2,1)S(1)} %constant_dynamic-update-slice_fusion.4.refs_0_), channel_id=1, source_target_pairs={{0,1},{1,0},{2,3},{3,2},{4,5},{5,4},{6,7},{7,6},{8,9},{9,8},{10,11... | collective-permute-start | bytes 983048 | tf_op jit(solution)/shard_map/ppermute | solution.py:673
  31.3 1.6 copy-start
  58.8 22.0 %collective-permute-start.18 = (bf16[1280,128]{1,0:T(8,128)(2,1)S(1)}, bf16[1280,128]{1,0:T(8,128)(2,1)S(1)}, u32[]{:S(2)}, u32[]{:S(2)}) collective-permute-start(bf16[1280,128]{1,0:T(8,128)(2,1)S(1)} %collective-permute-done.14.refs_3_), channel_id=1, source_target_pairs={{0,8},{1,9},{2,10},{3,11},{4,12},{5,13},{6,14},{7,15},{8,0},{9,1},... | collective-permute-start | bytes 983048 | tf_op jit(solution)/shard_map/ppermute | solution.py:673
  58.9 21.9 %collective-permute-start.17 = (bf16[1280,128]{1,0:T(8,128)(2,1)S(1)}, bf16[1280,128]{1,0:T(8,128)(2,1)S(1)}, u32[]{:S(2)}, u32[]{:S(2)}) collective-permute-start(bf16[1280,128]{1,0:T(8,128)(2,1)S(1)} %collective-permute-done.13.refs_2_), channel_id=1, source_target_pairs={{0,8},{1,9},{2,10},{3,11},{4,12},{5,13},{6,14},{7,15},{8,0},{9,1},... | collective-permute-start | bytes 983048 | tf_op jit(solution)/shard_map/ppermute | solution.py:673
  59.4 21.4 %collective-permute-start.16 = (bf16[1280,128]{1,0:T(8,128)(2,1)S(1)}, bf16[1280,128]{1,0:T(8,128)(2,1)S(1)}, u32[]{:S(2)}, u32[]{:S(2)}) collective-permute-start(bf16[1280,128]{1,0:T(8,128)(2,1)S(1)} %collective-permute-done.12.refs_1_), channel_id=1, source_target_pairs={{0,8},{1,9},{2,10},{3,11},{4,12},{5,13},{6,14},{7,15},{8,0},{9,1},... | collective-permute-start | bytes 983048 | tf_op jit(solution)/shard_map/ppermute | solution.py:673
  59.5 21.3 %copy-start.1 = (bf16[2048,512]{1,0:T(8,128)(2,1)S(1)}, bf16[2048,512]{1,0:T(8,128)(2,1)}, u32[]{:S(2)}) copy-start(bf16[2048,512]{1,0:T(8,128)(2,1)} %tokens.9) | copy-start | bytes 6291460
  59.5 21.3 %copy-start.3 = (bf16[2048,512]{1,0:T(8,128)(2,1)S(1)}, bf16[2048,512]{1,0:T(8,128)(2,1)}, u32[]{:S(2)}) copy-start(bf16[2048,512]{1,0:T(8,128)(2,1)} %cotangent.1) | copy-start | bytes 6291460
  107.6 12.7 %collective-permute-start.20 = (bf16[5120,128]{1,0:T(8,128)(2,1)S(1)}, bf16[5120,128]{1,0:T(8,128)(2,1)S(1)}, u32[]{:S(2)}, u32[]{:S(2)}) collective-permute-start(bf16[5120,128]{1,0:T(8,128)(2,1)S(1)} %get-tuple-element.90), channel_id=1, source_target_pairs={{0,8},{1,9},{2,10},{3,11},{4,12},{5,13},{6,14},{7,15},{8,0},{9,1},... | collective-permute-start | bytes 3932168 | tf_op jit(solution)/shard_map/ppermute | solution.py:673
  120.1 41.1 %collective-permute-start.19 = (bf16[768,128]{1,0:T(8,128)(2,1)S(1)}, bf16[768,128]{1,0:T(8,128)(2,1)S(1)}, u32[]{:S(2)}, u32[]{:S(2)}) collective-permute-start(bf16[768,128]{1,0:T(8,128)(2,1)S(1)} %get-tuple-element.87), channel_id=1, source_target_pairs={{0,8},{1,9},{2,10},{3,11},{4,12},{5,13},{6,14},{7,15},{8,0},{9,1},... | collective-permute-start | bytes 589832 | tf_op jit(solution)/shard_map/ppermute | solution.py:673
  120.5 26.4 %collective-permute-start.21 = (bf16[1280,128]{1,0:T(8,128)(2,1)S(1)}, bf16[1280,128]{1,0:T(8,128)(2,1)S(1)}, u32[]{:S(2)}, u32[]{:S(2)}) collective-permute-start(bf16[1280,128]{1,0:T(8,128)(2,1)S(1)} %get-tuple-element.126), channel_id=1, source_target_pairs={{0,1},{1,0},{2,3},{3,2},{4,5},{5,4},{6,7},{7,6},{8,9},{9,8},{10,11... | collective-permute-start | bytes 983048 | tf_op jit(solution)/shard_map/ppermute | solution.py:673
  121.4 25.6 %collective-permute-start.22 = (bf16[1280,128]{1,0:T(8,128)(2,1)S(1)}, bf16[1280,128]{1,0:T(8,128)(2,1)S(1)}, u32[]{:S(2)}, u32[]{:S(2)}) collective-permute-start(bf16[1280,128]{1,0:T(8,128)(2,1)S(1)} %get-tuple-element.125), channel_id=1, source_target_pairs={{0,16},{1,17},{2,18},{3,19},{4,20},{5,21},{6,22},{7,23},{8,24},{9,... | collective-permute-start | bytes 983048 | tf_op jit(solution)/shard_map/ppermute | solution.py:673
  122.5 24.5 %collective-permute-start.23 = (bf16[1280,128]{1,0:T(8,128)(2,1)S(1)}, bf16[1280,128]{1,0:T(8,128)(2,1)S(1)}, u32[]{:S(2)}, u32[]{:S(2)}) collective-permute-start(bf16[1280,128]{1,0:T(8,128)(2,1)S(1)} %get-tuple-element.124), channel_id=1, source_target_pairs={{0,17},{1,16},{2,19},{3,18},{4,21},{5,20},{6,23},{7,22},{8,25},{9,... | collective-permute-start | bytes 983048 | tf_op jit(solution)/shard_map/ppermute | solution.py:673
  146.9 14.7 %collective-permute-start.24 = (bf16[1536,128]{1,0:T(8,128)(2,1)S(1)}, bf16[1536,128]{1,0:T(8,128)(2,1)S(1)}, u32[]{:S(2)}, u32[]{:S(2)}) collective-permute-start(bf16[1536,128]{1,0:T(8,128)(2,1)S(1)} %get-tuple-element.103), channel_id=1, source_target_pairs={{0,8},{1,9},{2,10},{3,11},{4,12},{5,13},{6,14},{7,15},{8,0},{9,1},... | collective-permute-start | bytes 1179656 | tf_op jit(solution)/shard_map/ppermute | solution.py:673
  147.2 14.5 %collective-permute-start.32 = (bf16[640,128]{1,0:T(8,128)(2,1)S(1)}, bf16[640,128]{1,0:T(8,128)(2,1)S(1)}, u32[]{:S(2)}, u32[]{:S(2)}) collective-permute-start(bf16[640,128]{1,0:T(8,128)(2,1)S(1)} %slice.258), channel_id=1, source_target_pairs={{0,2},{1,3},{2,0},{3,1},{4,6},{5,7},{6,4},{7,5},{8,10},{9,11},{10,... | collective-permute-start | bytes 491528 | tf_op jit(solution)/shard_map/ppermute | solution.py:673
  161.3 1.8 collective-permute-start.25
  161.8 19.0 %collective-permute-start.33 = (bf16[320,128]{1,0:T(8,128)(2,1)S(1)}, bf16[320,128]{1,0:T(8,128)(2,1)S(1)}, u32[]{:S(2)}, u32[]{:S(2)}) collective-permute-start(bf16[320,128]{1,0:T(8,128)(2,1)S(1)} %slice.259), channel_id=1, source_target_pairs={{0,4},{1,5},{2,6},{3,7},{4,0},{5,1},{6,2},{7,3},{8,12},{9,13},{10,... | collective-permute-start | bytes 245768 | tf_op jit(solution)/shard_map/ppermute | solution.py:673
  163.2 9.1 %collective-permute-start.26 = (bf16[832,128]{1,0:T(8,128)(2,1)S(1)}, bf16[832,128]{1,0:T(8,128)(2,1)S(1)}, u32[]{:S(2)}, u32[]{:S(2)}) collective-permute-start(bf16[832,128]{1,0:T(8,128)(2,1)S(1)} %bitcast.51), channel_id=1, source_target_pairs={{0,1},{1,0},{2,3},{3,2},{4,5},{5,4},{6,7},{7,6},{8,9},{9,8},{10,11... | collective-permute-start | bytes 638984 | tf_op jit(solution)/shard_map/ppermute | solution.py:673
  163.9 10.5 %collective-permute-start.27 = (bf16[832,128]{1,0:T(8,128)(2,1)S(1)}, bf16[832,128]{1,0:T(8,128)(2,1)S(1)}, u32[]{:S(2)}, u32[]{:S(2)}) collective-permute-start(bf16[832,128]{1,0:T(8,128)(2,1)S(1)} %bitcast.53), channel_id=1, source_target_pairs={{0,16},{1,17},{2,18},{3,19},{4,20},{5,21},{6,22},{7,23},{8,24},{9,... | collective-permute-start | bytes 638984 | tf_op jit(solution)/shard_map/ppermute | solution.py:673
  165.4 10.7 %collective-permute-start.28 = (bf16[832,128]{1,0:T(8,128)(2,1)S(1)}, bf16[832,128]{1,0:T(8,128)(2,1)S(1)}, u32[]{:S(2)}, u32[]{:S(2)}) collective-permute-start(bf16[832,128]{1,0:T(8,128)(2,1)S(1)} %bitcast.54), channel_id=1, source_target_pairs={{0,17},{1,16},{2,19},{3,18},{4,21},{5,20},{6,23},{7,22},{8,25},{9,... | collective-permute-start | bytes 638984 | tf_op jit(solution)/shard_map/ppermute | solution.py:673
  176.3 4.5 %collective-permute-start.29 = (bf16[208,128]{1,0:T(8,128)(2,1)S(1)}, bf16[208,128]{1,0:T(8,128)(2,1)S(1)}, u32[]{:S(2)}, u32[]{:S(2)}) collective-permute-start(bf16[208,128]{1,0:T(8,128)(2,1)S(1)} %get-tuple-element.141), channel_id=1, source_target_pairs={{0,2},{1,3},{2,0},{3,1},{4,6},{5,7},{6,4},{7,5},{8,10},{9,11},{10,... | collective-permute-start | bytes 159752 | tf_op jit(solution)/shard_map/ppermute | solution.py:673
  178.4 5.7 %collective-permute-start.30 = (bf16[208,128]{1,0:T(8,128)(2,1)S(1)}, bf16[208,128]{1,0:T(8,128)(2,1)S(1)}, u32[]{:S(2)}, u32[]{:S(2)}) collective-permute-start(bf16[208,128]{1,0:T(8,128)(2,1)S(1)} %get-tuple-element.140), channel_id=1, source_target_pairs={{0,4},{1,5},{2,6},{3,7},{4,0},{5,1},{6,2},{7,3},{8,12},{9,13},{10,... | collective-permute-start | bytes 159752 | tf_op jit(solution)/shard_map/ppermute | solution.py:673
  179.5 5.9 %collective-permute-start.31 = (bf16[208,128]{1,0:T(8,128)(2,1)S(1)}, bf16[208,128]{1,0:T(8,128)(2,1)S(1)}, u32[]{:S(2)}, u32[]{:S(2)}) collective-permute-start(bf16[208,128]{1,0:T(8,128)(2,1)S(1)} %get-tuple-element.139), channel_id=1, source_target_pairs={{0,6},{1,7},{2,4},{3,5},{4,2},{5,3},{6,0},{7,1},{8,14},{9,15},{10,... | collective-permute-start | bytes 159752 | tf_op jit(solution)/shard_map/ppermute | solution.py:673
